TPU v7x, 32 devices: a whole 2x2x4 slice. The times are simulated.
32 devices in a mesh: xy: 8 (over y, x, core), gz: 4 (over z).
Axes of the slice: x: 2, y: 2, z: 4, core: 2. Of those that a mesh axis runs over, the one named last changes fastest.
Arguments:
- velocity: float32 [3, 16, 256, 1024], P(None, 'gz', 'xy'), may hold values from -6 to 6
- magnetic: float32 [3, 8, 128, 512], P(None, 'gz', 'xy'), may hold values from -6 to 6
- slot_block_table: int32 [256], P('xy'), may hold values from 0 to 255, as said below
Outputs:
- updated_fine_velocity: float32 [3, 16, 256, 1024], P(None, 'gz', 'xy')
- magnetic_next: float32 [3, 8, 128, 512], P(None, 'gz', 'xy')
Inputs may be any that keep to these rules, and one draw needn't show every extreme that they name: `slot_block_table`: each block number appears in one slot; the 32 slots of one device along xy hold exactly 4 blocks of every block row.
All inputs are finite; a program needn't handle non-finite values.
Results may differ from a plain program's by a relative error of at most 0.00005.
Values sent between devices are 32-bit elements; how exact they have to be, the bound alone decides.
No kernel may reach another device: no remote copies, remote signals or barrier semaphores. Data moves between devices by JAX's collectives and lax.ppermute only.
A program may use at most 64 MiB of HBM per device.

v0:
```python
import jax
import jax.numpy as jnp
from jax import lax
from jax.sharding import PartitionSpec as P

BLOCK_EDGE = 32


def with_halo(value, sides, width):
    for axis, dim in sides:
        size, length = (lax.axis_size(axis), value.shape[dim])
        up = [(i, (i + 1) % size) for i in range(size)]
        down = [(j, i) for i, j in up]
        last = lax.slice_in_dim(value, length - width, length, axis=dim)
        first = lax.slice_in_dim(value, 0, width, axis=dim)
        before = lax.ppermute(last, axis, up)
        after = lax.ppermute(first, axis, down)
        value = jnp.concatenate([before, value, after], axis=dim)
    return value


def restrict(fine, blk):
    half_width = blk // 2
    s = fine.shape
    v = fine.reshape(s[0], s[1] // 2, 2, s[2], half_width, 2, half_width, 2)
    return (jnp.sum(v, axis=(2, 5, 7)) * 0.125).reshape(
        s[0], s[1] // 2, s[2], half_width * half_width
    )


def inner(padded):
    return padded[:, 1:-1, 1:-1]


def along_z(padded):
    return (padded[:, 2:, 1:-1] - padded[:, :-2, 1:-1]) * 0.5


def along_y(padded):
    return (padded[:, 1:-1, 2:] - padded[:, 1:-1, :-2]) * 0.5


def along_x(padded):
    middle = inner(padded)
    return (jnp.roll(middle, -1, 3) - jnp.roll(middle, 1, 3)) * 0.5


def curl_padded(padded):
    dzv = along_z(padded)
    dyv = along_y(padded)
    dxv = along_x(padded)
    return jnp.stack([dyv[2] - dzv[1], dzv[0] - dxv[2], dxv[1] - dyv[0]])


def cross(a, b):
    return jnp.stack(
        [a[1] * b[2] - a[2] * b[1], a[2] * b[0] - a[0] * b[2], a[0] * b[1] - a[1] * b[0]]
    )


def laplace_padded(padded):
    middle = inner(padded)
    total = padded[:, 2:, 1:-1] + padded[:, :-2, 1:-1] + padded[:, 1:-1, 2:] + padded[:, 1:-1, :-2]
    return total + jnp.roll(middle, 1, 3) + jnp.roll(middle, -1, 3) - 6.0 * middle


def split_into_tiles(magnetic_state, coarse_depth_index, half_width, slot_count):
    return (
        magnetic_state.reshape(
            magnetic_state.shape[0], coarse_depth_index, half_width, slot_count, half_width
        )
        .transpose(0, 1, 3, 2, 4)
        .reshape(magnetic_state.shape[0], coarse_depth_index, slot_count, half_width * half_width)
    )


def assemble_from_tiles(tile_stack, coarse_depth_index, half_width, slot_count):
    return (
        tile_stack.reshape(
            tile_stack.shape[0], coarse_depth_index, slot_count, half_width, half_width
        )
        .transpose(0, 1, 3, 2, 4)
        .reshape(tile_stack.shape[0], coarse_depth_index, half_width, slot_count * half_width)
    )


def body(velocity, magnetic, slot_block_table):
    half_width = BLOCK_EDGE // 2
    slot_count = velocity.shape[2]
    coarse_depth_index = velocity.shape[1] // 2
    column_indices = slot_block_table % slot_count
    sorted_positions = jnp.argsort(slot_block_table)
    dispatched_columns = column_indices[sorted_positions].reshape(1, 1, slot_count, 1)
    ordered = velocity[:, :, sorted_positions]
    got, received_columns = (
        lax.all_to_all(
            restrict(ordered, BLOCK_EDGE), "xy", split_axis=2, concat_axis=2, tiled=True
        ),
        lax.all_to_all(dispatched_columns, "xy", split_axis=2, concat_axis=2, tiled=True),
    )
    column_listing = received_columns.reshape(slot_count)
    grouped_by_column = got[:, :, jnp.argsort(column_listing)]
    coarse_flow_field = assemble_from_tiles(
        grouped_by_column, coarse_depth_index, half_width, slot_count
    )
    emf = cross(coarse_flow_field, magnetic)
    stacked = jnp.concatenate([magnetic, emf], axis=0)
    padded = with_halo(stacked, (("xy", 2), ("gz", 1)), 1)
    field_pad = padded[0:3]
    current = curl_padded(field_pad)
    magnetic_next = magnetic + 0.1 * (curl_padded(padded[3:6]) + 0.5 * laplace_padded(field_pad))
    lorentz_force = cross(current, magnetic)
    returned_back_tiles = split_into_tiles(
        lorentz_force, coarse_depth_index, half_width, slot_count
    )[:, :, column_listing]
    returned = lax.all_to_all(returned_back_tiles, "xy", split_axis=2, concat_axis=2, tiled=True)
    blocks_per_slot = returned[:, :, jnp.argsort(sorted_positions)]
    widened_tiles = jnp.broadcast_to(
        blocks_per_slot.reshape(3, coarse_depth_index, 1, slot_count, half_width, 1, half_width, 1),
        (3, coarse_depth_index, 2, slot_count, half_width, 2, half_width, 2),
    )
    updated_fine_velocity = velocity + 0.1 * widened_tiles.reshape(
        3, coarse_depth_index * 2, slot_count, BLOCK_EDGE * BLOCK_EDGE
    )
    return (updated_fine_velocity, magnetic_next)


def solution(mesh):
    return jax.shard_map(
        body,
        mesh=mesh,
        in_specs=(P(None, "gz", "xy", None), P(None, "gz", "xy", None), P("xy")),
        out_specs=(P(None, "gz", "xy", None), P(None, "gz", "xy", None)),
        check_vma=False,
    )
```

profile of v0, /device:TPU:0, one launch (start us, length us, event | category | flops | bytes accessed | tf_op | source)
XLA Modules:
  0.0 104.9 jit_solution(8437130082161293835)
XLA Ops:
  1.4 2.3 %sort.45 = (s32[32]{0:T(128)}, s32[32]{0:T(128)S(1)}) sort(s32[32]{0:T(128)} %param.5, s32[32]{0:T(128)S(1)} %iota.10), dimensions={0}, to_apply=%region_0.1 | sort | flops 160 | bytes 512 | tf_op jit(solution)/shard_map/jit(argsort)/sort | solution.py:92
  5.7 5.2 %all-to-all-start.1 = ((s32[1,1,32,1]{3,1,0,2:T(1,128)}), s32[1,1,32,1]{3,1,0,2:T(1,128)S(1)}, u32[]{:S(2)}, u32[]{:S(2)}) async-start(s32[1,1,32,1]{3,1,0,2:T(1,128)} %copy.33), calls=%async_computation.1 | async-start | bytes 32768 | tf_op jit(solution)/shard_map/all_to_all | solution.py:99
  10.9 1.5 %fusion.14 = (f32[3,2,16,1]{3,2,1,0:T(8,128)}, f32[3,2,16,1]{3,2,1,0:T(8,128)}) fusion(f32[3,2,16,512]{3,2,1,0:T(8,128)} %param.4), kind=kLoop, calls=%fused_computation.82 | loop fusion | bytes 1536 | tf_op jit(solution)/shard_map/jit(_roll_static)/slice | solution.py:45
  13.6 3.0 %gather_fusion = f32[32,3,4,1024]{3,0,2,1:T(8,128)S(1)} fusion(f32[3,4,32,1024]{3,2,1,0:T(8,128)S(1)} %copy-done, s32[1024]{0:T(1024)} %copy-done.18), kind=kCustom, calls=%fused_computation | custom fusion | bytes 3145856 | tf_op jit(solution)/shard_map/gather | solution.py:94
  16.5 4.0 %copy.43 = f32[3,4,32,1024]{2,3,1,0:T(8,128)} copy(f32[3,4,32,1024]{3,2,1,0:T(8,128)S(1)} %copy-done) | data formatting | bytes 3145728 | tf_op args[0]
  20.5 2.3 %sort.47 = (s32[32]{0:T(128)}, s32[32]{0:T(128)S(1)}) sort(s32[32]{0:T(128)} %copy-done.19, s32[32]{0:T(128)S(1)} %iota.12), dimensions={0}, to_apply=%region_3.4 | sort | flops 160 | bytes 512 | tf_op jit(solution)/shard_map/jit(argsort)/sort | solution.py:117
  23.4 4.0 %copy.31 = f32[3,4,32,1024]{2,3,1,0:T(8,128)} copy(f32[3,4,32,1024]{3,2,1,0:T(8,128)S(1)} %bitcast.34) | data formatting | bytes 3145728 | tf_op jit(solution)/shard_map/gather | solution.py:94
  27.3 7.3 %reduce_sum.9 = f32[3,2,32,16,16]{2,4,3,1,0:T(8,128)S(1)} reduce(f32[3,2,2,32,16,2,16,2]{3,7,6,5,4,2,1,0:T(2,128)} %bitcast.32, f32[]{:T(128)} %constant.10.clone.1), dimensions={2,5,7}, to_apply=%region_1.2 | reduce | flops 344064 | bytes 1769476 | tf_op jit(solution)/shard_map/reduce_sum | solution.py:26
  36.5 4.2 %all-to-all-start = ((f32[3,2,32,256]{3,1,0,2:T(2,128)}), f32[3,2,32,256]{3,1,0,2:T(2,128)S(1)}, u32[]{:S(2)}, u32[]{:S(2)}) async-start(f32[3,2,32,256]{3,1,0,2:T(2,128)} %copy.32), calls=%async_computation | async-start | bytes 393216 | tf_op jit(solution)/shard_map/all_to_all | solution.py:96
  41.4 1.6 %sort.46 = (s32[32]{0:T(128)}, s32[32]{0:T(128)S(1)}) sort(s32[32]{0:T(128)S(1)} %reduce, s32[32]{0:T(128)S(1)} %iota.11), dimensions={0}, to_apply=%region_2.3 | sort | flops 160 | bytes 512 | tf_op jit(solution)/shard_map/jit(argsort)/sort | solution.py:102
  43.0 3.9 %all-to-all-done = f32[3,2,32,256]{3,1,0,2:T(2,128)S(1)} async-done(((f32[3,2,32,256]{3,1,0,2:T(2,128)}), f32[3,2,32,256]{3,1,0,2:T(2,128)S(1)}, u32[]{:S(2)}, u32[]{:S(2)}) %all-to-all-start) | async-done | bytes 196640 | tf_op jit(solution)/shard_map/all_to_all | solution.py:96
  49.8 2.6 %collective-permute-start.1 = (f32[6,2,1,512]{3,2,1,0:T(1,128)S(1)}, f32[6,2,1,512]{3,2,1,0:T(1,128)S(1)}, u32[]{:S(2)}, u32[]{:S(2)}) collective-permute-start(f32[6,2,1,512]{3,2,1,0:T(1,128)S(1)} %get-tuple-element.23), channel_id=1, source_target_pairs={{4,0},{8,4},{12,8},{16,12},{20,16},{24,20},{28,24},{0,28},{5,1},{9... | collective-permute-start | bytes 73736 | tf_op jit(solution)/shard_map/ppermute | solution.py:17
  52.4 1.7 %collective-permute-done = f32[6,2,1,512]{3,2,1,0:T(1,128)S(1)} collective-permute-done((f32[6,2,1,512]{3,2,1,0:T(1,128)S(1)}, f32[6,2,1,512]{3,2,1,0:T(1,128)S(1)}, u32[]{:S(2)}, u32[]{:S(2)}) %collective-permute-start) | collective-permute-done | bytes 24608 | tf_op jit(solution)/shard_map/ppermute | solution.py:16
  54.3 1.6 %collective-permute-start.3 = (f32[6,1,18,512]{3,2,1,0:T(8,128)S(1)}, f32[6,1,18,512]{3,2,1,0:T(8,128)S(1)}, u32[]{:S(2)}, u32[]{:S(2)}) collective-permute-start(f32[6,1,18,512]{3,2,1,0:T(8,128)S(1)} %get-tuple-element.20), channel_id=1, source_target_pairs={{0,1},{1,2},{2,3},{3,0},{4,5},{5,6},{6,7},{7,4},{8,9},{9,10},{10,1... | collective-permute-start | bytes 663560 | tf_op jit(solution)/shard_map/ppermute | solution.py:16
  55.9 2.3 %collective-permute-start.2 = (f32[6,1,18,512]{3,2,1,0:T(8,128)S(1)}, f32[6,1,18,512]{3,2,1,0:T(8,128)S(1)}, u32[]{:S(2)}, u32[]{:S(2)}) collective-permute-start(f32[6,1,18,512]{3,2,1,0:T(8,128)S(1)} %get-tuple-element.21), channel_id=1, source_target_pairs={{1,0},{2,1},{3,2},{0,3},{5,4},{6,5},{7,6},{4,7},{9,8},{10,9},{11,1... | collective-permute-start | bytes 663560 | tf_op jit(solution)/shard_map/ppermute | solution.py:17
  59.0 7.1 %collective-permute-done.3 = f32[6,1,18,512]{3,2,1,0:T(8,128)S(1)} collective-permute-done((f32[6,1,18,512]{3,2,1,0:T(8,128)S(1)}, f32[6,1,18,512]{3,2,1,0:T(8,128)S(1)}, u32[]{:S(2)}, u32[]{:S(2)}) %collective-permute-start.3) | collective-permute-done | bytes 221216 | tf_op jit(solution)/shard_map/ppermute | solution.py:16
  66.0 4.7 %collective-permute-done.2 = f32[6,1,18,512]{3,2,1,0:T(8,128)S(1)} collective-permute-done((f32[6,1,18,512]{3,2,1,0:T(8,128)S(1)}, f32[6,1,18,512]{3,2,1,0:T(8,128)S(1)}, u32[]{:S(2)}, u32[]{:S(2)}) %collective-permute-start.2) | collective-permute-done | bytes 221216 | tf_op jit(solution)/shard_map/ppermute | solution.py:17
  75.3 1.4 %maximum_bitcast_fusion = f32[3,2,32,16,16]{4,2,3,1,0:T(8,128)S(1)} fusion(f32[1,2,16,32,16]{4,3,2,1,0:T(8,128)} %stack.23, f32[1,2,16,32,16]{4,3,2,1,0:T(8,128)} %stack.22, f32[1,2,16,32,16]{4,3,2,1,0:T(8,128)S(1)} %stack.10), kind=kLoop, calls=%fused_computation.5 | loop fusion | flops 98304 | bytes 393216 | tf_op jit(solution)/shard_map/transpose | solution.py:72
  77.5 1.5 %gather_fusion.3 = f32[32,3,2,256]{3,2,1,0:T(2,128)} fusion(f32[3,2,32,256]{3,1,2,0:T(2,128)S(1)} %copy.40, s32[1024]{0:T(1024)S(1)} %pad_clamp_fusion.1), kind=kCustom, calls=%fused_computation.3 | custom fusion | bytes 393344 | tf_op jit(solution)/shard_map/gather | solution.py:113
  78.9 3.4 %all-to-all-start.2 = ((f32[3,2,32,256]{3,1,0,2:T(2,128)}), f32[3,2,32,256]{3,1,0,2:T(2,128)S(1)}, u32[]{:S(2)}, u32[]{:S(2)}) async-start(f32[3,2,32,256]{3,1,0,2:T(2,128)} %bitcast.11), calls=%async_computation.2 | async-start | bytes 393216 | tf_op jit(solution)/shard_map/all_to_all | solution.py:116
  83.5 5.0 %all-to-all-done.2 = f32[3,2,32,256]{3,1,0,2:T(2,128)S(1)} async-done(((f32[3,2,32,256]{3,1,0,2:T(2,128)}), f32[3,2,32,256]{3,1,0,2:T(2,128)S(1)}, u32[]{:S(2)}, u32[]{:S(2)}) %all-to-all-start.2) | async-done | bytes 196640 | tf_op jit(solution)/shard_map/all_to_all | solution.py:116
  89.8 3.2 %broadcast_in_dim.19 = f32[3,2,2,32,16,2,16,2]{3,7,6,5,4,2,1,0:T(2,128)S(1)} broadcast(f32[3,2,32,16,16]{2,4,3,1,0:T(8,128)S(1)} %bitcast.35), dimensions={0,1,3,4,6} | broadcast | bytes 1769472 | tf_op jit(solution)/shard_map/broadcast_in_dim | solution.py:118
  93.0 6.3 %add.55 = f32[3,4,32,1024]{2,3,1,0:T(8,128)} add(f32[3,4,32,1024]{2,3,1,0:T(8,128)} %copy.43, f32[3,4,32,1024]{2,3,1,0:T(8,128)S(1)} %bitcast.33) | non-fusion elementwise | flops 393216 | bytes 4718592 | tf_op jit(solution)/shard_map/add | solution.py:122
  99.3 5.5 %copy.44 = f32[3,4,32,1024]{3,2,1,0:T(8,128)} copy(f32[3,4,32,1024]{2,3,1,0:T(8,128)} %add.55) | data formatting | bytes 3145728
  (95 shorter events, 18.4 us)
Async XLA Ops:
  0.6 12.9 %copy-start = (f32[3,4,32,1024]{3,2,1,0:T(8,128)S(1)}, f32[3,4,32,1024]{3,2,1,0:T(8,128)}, u32[]{:S(2)}) copy-start(f32[3,4,32,1024]{3,2,1,0:T(8,128)} %param.3) | copy-start | bytes 4718596
  4.3 8.1 %copy-start.18 = (s32[1024]{0:T(1024)}, s32[1024]{0:T(1024)S(1)}, u32[]{:S(2)}) copy-start(s32[1024]{0:T(1024)S(1)} %pad_clamp_fusion.3) | copy-start | bytes 12292
  5.7 30.8 %all-to-all-start.1 = ((s32[1,1,32,1]{3,1,0,2:T(1,128)}), s32[1,1,32,1]{3,1,0,2:T(1,128)S(1)}, u32[]{:S(2)}, u32[]{:S(2)}) async-start(s32[1,1,32,1]{3,1,0,2:T(1,128)} %copy.33), calls=%async_computation.1 | async-start | bytes 32768 | tf_op jit(solution)/shard_map/all_to_all | solution.py:99
  13.6 21.2 %copy-start.2 = (f32[3,2,16,511]{3,2,1,0:T(8,128)}, f32[3,2,16,511]{3,2,1,0:T(8,128)S(1)}, u32[]{:S(2)}) copy-start(f32[3,2,16,511]{3,2,1,0:T(8,128)S(1)} %get-tuple-element.37) | copy-start | bytes 588676
  36.5 10.4 %all-to-all-start = ((f32[3,2,32,256]{3,1,0,2:T(2,128)}), f32[3,2,32,256]{3,1,0,2:T(2,128)S(1)}, u32[]{:S(2)}, u32[]{:S(2)}) async-start(f32[3,2,32,256]{3,1,0,2:T(2,128)} %copy.32), calls=%async_computation | async-start | bytes 393216 | tf_op jit(solution)/shard_map/all_to_all | solution.py:96
  48.3 1.3 %copy-start.1 = (f32[3,2,16,512]{3,2,1,0:T(8,128)S(1)}, f32[3,2,16,512]{3,2,1,0:T(8,128)}, u32[]{:S(2)}) copy-start(f32[3,2,16,512]{3,2,1,0:T(8,128)} %param.4) | copy-start | bytes 589828
  49.7 4.4 %collective-permute-start = (f32[6,2,1,512]{3,2,1,0:T(1,128)S(1)}, f32[6,2,1,512]{3,2,1,0:T(1,128)S(1)}, u32[]{:S(2)}, u32[]{:S(2)}) collective-permute-start(f32[6,2,1,512]{3,2,1,0:T(1,128)S(1)} %get-tuple-element.22), channel_id=1, source_target_pairs={{0,4},{4,8},{8,12},{12,16},{16,20},{20,24},{24,28},{28,0},{1,5},{5... | collective-permute-start | bytes 73736 | tf_op jit(solution)/shard_map/ppermute | solution.py:16
  49.8 4.4 %collective-permute-start.1 = (f32[6,2,1,512]{3,2,1,0:T(1,128)S(1)}, f32[6,2,1,512]{3,2,1,0:T(1,128)S(1)}, u32[]{:S(2)}, u32[]{:S(2)}) collective-permute-start(f32[6,2,1,512]{3,2,1,0:T(1,128)S(1)} %get-tuple-element.23), channel_id=1, source_target_pairs={{4,0},{8,4},{12,8},{16,12},{20,16},{24,20},{28,24},{0,28},{5,1},{9... | collective-permute-start | bytes 73736 | tf_op jit(solution)/shard_map/ppermute | solution.py:17
  54.1 18.8 %copy-start.4 = (f32[6,2,1,512]{3,2,1,0:T(1,128)}, f32[6,2,1,512]{3,2,1,0:T(1,128)S(1)}, u32[]{:S(2)}) copy-start(f32[6,2,1,512]{3,2,1,0:T(1,128)S(1)} %collective-permute-done) | copy-start | bytes 73732
  54.1 18.8 %copy-start.6 = (f32[6,2,1,512]{3,2,1,0:T(1,128)}, f32[6,2,1,512]{3,2,1,0:T(1,128)S(1)}, u32[]{:S(2)}) copy-start(f32[6,2,1,512]{3,2,1,0:T(1,128)S(1)} %collective-permute-done.1) | copy-start | bytes 73732
  54.3 11.8 %collective-permute-start.3 = (f32[6,1,18,512]{3,2,1,0:T(8,128)S(1)}, f32[6,1,18,512]{3,2,1,0:T(8,128)S(1)}, u32[]{:S(2)}, u32[]{:S(2)}) collective-permute-start(f32[6,1,18,512]{3,2,1,0:T(8,128)S(1)} %get-tuple-element.20), channel_id=1, source_target_pairs={{0,1},{1,2},{2,3},{3,0},{4,5},{5,6},{6,7},{7,4},{8,9},{9,10},{10,1... | collective-permute-start | bytes 663560 | tf_op jit(solution)/shard_map/ppermute | solution.py:16
  55.9 14.8 %collective-permute-start.2 = (f32[6,1,18,512]{3,2,1,0:T(8,128)S(1)}, f32[6,1,18,512]{3,2,1,0:T(8,128)S(1)}, u32[]{:S(2)}, u32[]{:S(2)}) collective-permute-start(f32[6,1,18,512]{3,2,1,0:T(8,128)S(1)} %get-tuple-element.21), channel_id=1, source_target_pairs={{1,0},{2,1},{3,2},{0,3},{5,4},{6,5},{7,6},{4,7},{9,8},{10,9},{11,1... | collective-permute-start | bytes 663560 | tf_op jit(solution)/shard_map/ppermute | solution.py:17
  77.1 5.2 %copy-start.8 = (f32[3,2,16,511]{3,2,1,0:T(8,128)S(1)}, f32[3,2,16,511]{3,2,1,0:T(8,128)}, u32[]{:S(2)}) copy-start(f32[3,2,16,511]{3,2,1,0:T(8,128)} %get-tuple-element.34) | copy-start | bytes 588676
  77.1 5.2 %copy-start.9 = (f32[3,2,16,511]{3,2,1,0:T(8,128)S(1)}, f32[3,2,16,511]{3,2,1,0:T(8,128)}, u32[]{:S(2)}) copy-start(f32[3,2,16,511]{3,2,1,0:T(8,128)} %get-tuple-element.35) | copy-start | bytes 588676
  77.1 5.2 %copy-start.16 = (f32[3,2,16,1]{3,2,1,0:T(8,128)S(1)}, f32[3,2,16,1]{3,2,1,0:T(8,128)}, u32[]{:S(2)}) copy-start(f32[3,2,16,1]{3,2,1,0:T(8,128)} %get-tuple-element.32) | copy-start | bytes 1156
  77.1 5.2 %copy-start.17 = (f32[3,2,16,1]{3,2,1,0:T(8,128)S(1)}, f32[3,2,16,1]{3,2,1,0:T(8,128)}, u32[]{:S(2)}) copy-start(f32[3,2,16,1]{3,2,1,0:T(8,128)} %get-tuple-element.33) | copy-start | bytes 1156
  77.2 5.4 %copy-start.10 = (f32[3,2,16,512]{3,2,1,0:T(8,128)S(1)}, f32[3,2,16,512]{3,2,1,0:T(8,128)}, u32[]{:S(2)}) copy-start(f32[3,2,16,512]{3,2,1,0:T(8,128)} %fusion.3) | copy-start | bytes 589828
  77.2 5.4 %copy-start.11 = (f32[3,2,16,512]{3,2,1,0:T(8,128)S(1)}, f32[3,2,16,512]{3,2,1,0:T(8,128)}, u32[]{:S(2)}) copy-start(f32[3,2,16,512]{3,2,1,0:T(8,128)} %get-tuple-element.30) | copy-start | bytes 589828
  77.2 5.4 %copy-start.3 = (f32[3,2,16,511]{3,2,1,0:T(8,128)S(1)}, f32[3,2,16,511]{3,2,1,0:T(8,128)}, u32[]{:S(2)}) copy-start(f32[3,2,16,511]{3,2,1,0:T(8,128)} %copy-done.2) | copy-start | bytes 588676
  77.2 5.4 %copy-start.5 = (f32[6,2,1,512]{3,2,1,0:T(1,128)S(1)}, f32[6,2,1,512]{3,2,1,0:T(1,128)}, u32[]{:S(2)}) copy-start(f32[6,2,1,512]{3,2,1,0:T(1,128)} %copy-done.4) | copy-start | bytes 73732
  77.2 5.4 %copy-start.7 = (f32[6,2,1,512]{3,2,1,0:T(1,128)S(1)}, f32[6,2,1,512]{3,2,1,0:T(1,128)}, u32[]{:S(2)}) copy-start(f32[6,2,1,512]{3,2,1,0:T(1,128)} %copy-done.6) | copy-start | bytes 73732
  77.2 5.4 %copy-start.13 = (f32[3,2,16,1]{3,2,1,0:T(8,128)S(1)}, f32[3,2,16,1]{3,2,1,0:T(8,128)}, u32[]{:S(2)}) copy-start(f32[3,2,16,1]{3,2,1,0:T(8,128)} %get-tuple-element.38) | copy-start | bytes 1156
  77.2 5.4 %copy-start.15 = (f32[3,2,16,1]{3,2,1,0:T(8,128)S(1)}, f32[3,2,16,1]{3,2,1,0:T(8,128)}, u32[]{:S(2)}) copy-start(f32[3,2,16,1]{3,2,1,0:T(8,128)} %get-tuple-element.39) | copy-start | bytes 1156
  78.9 9.5 %all-to-all-start.2 = ((f32[3,2,32,256]{3,1,0,2:T(2,128)}), f32[3,2,32,256]{3,1,0,2:T(2,128)S(1)}, u32[]{:S(2)}, u32[]{:S(2)}) async-start(f32[3,2,32,256]{3,1,0,2:T(2,128)} %bitcast.11), calls=%async_computation.2 | async-start | bytes 393216 | tf_op jit(solution)/shard_map/all_to_all | solution.py:116
  (3 other events, 2.2 us)
where the time goes:
time: 106 us; the launch traced here: 105 us
  local copies, waits for them, and re-layouts  35.8 us (34%)
  other arithmetic  26.2 us (25%)
  waiting for transfers between devices  22.3 us (21%)
  starting transfers between devices  19.4 us (18%)
  between operations  1.12 us (1%)
    unnamed x42, local copies, waits for them, and re-layouts  10.9 us
    ppermute x2, waiting for transfers between devices, with_halo(): before = lax.ppermute(last, axis, up)  8.8 us
    reduce_sum x1, other arithmetic, restrict(): jnp.sum(v, axis=(2, 5, 7)) * 0.125  7.27 us
    gather x2, local copies, waits for them, and re-layouts, body(): ordered = velocity[:, :, sorted_positions]  6.93 us
    add x1, other arithmetic, body(): velocity + 0.1 * widened_tiles.reshape(3, coarse_depth_index * 2, slot_co...  6.28 us
    all_to_all x1, starting transfers between devices, body(): lax.all_to_all(dispatched_columns, 'xy', split_axis=2, concat_axis=2, til...  5.2 us
    all_to_all x1, waiting for transfers between devices, body(): lax.all_to_all(returned_back_tiles, 'xy', split_axis=2, concat_axis=2, ti...  4.99 us
    ppermute x2, starting transfers between devices, with_halo(): after = lax.ppermute(first, axis, down)  4.9 us
  transfers between devices with their start and end apart: 7, of which 5 were waited for; matrix products, arithmetic and copies ran while one was open for 28% of the time, Pallas kernels for 0%

commit v1 on v0

v1 whole, which is shorter than its diff:
```python
import functools
import math

import jax
import jax.numpy as jnp
from jax import lax
from jax.experimental import pallas as pl
from jax.experimental.pallas import tpu as pltpu
from jax.sharding import PartitionSpec as P

F32, BF16 = jnp.float32, jnp.bfloat16
VMEM = pl.BlockSpec(memory_space=pltpu.VMEM)


def split(x):
    hi = x.astype(BF16)
    return hi, (x - hi.astype(F32)).astype(BF16)


def dot(a, b):
    return jnp.dot(a, b, preferred_element_type=F32)


def iota(shape, dim):
    return lax.broadcasted_iota(jnp.int32, shape, dim)


def one_hot(mask):
    return jnp.where(mask, 1.0, 0.0).astype(BF16)


def log2(x):
    assert x == 1 << (x.bit_length() - 1)
    return x.bit_length() - 1


class Plan:
    def __init__(self, vshape, bshape, n):
        self.n = n
        self.slots = vshape[2]
        self.k = self.slots // n
        self.zc = bshape[1]
        self.ny, self.nx = bshape[2:]
        self.edge = math.isqrt(vshape[3])
        self.half = self.edge // 2
        self.area = self.half * self.half
        self.bcols = self.nx // self.half
        self.cz = 3 * self.zc
        self.ru = -(-self.cz * self.k // 8) * 8
        self.rows = n * self.ru
        self.rb = self.cz * self.nx // self.area
        self.r1 = -(-(self.ru + self.rb + 1) // 8) * 8
        self.re = 2 * self.zc * self.nx // self.area
        self.r2 = -(-(self.ru + self.re) // 8) * 8
        self.wrap = self.nx // self.area


def send_positions(p, table):
    s = p.slots
    row = jnp.broadcast_to((table >> log2(p.bcols)).astype(F32), (s, s))
    i, j = iota((s, s), 0), iota((s, s), 1)
    row_s = jnp.sum(jnp.where(i == j, row, 0.0), axis=1, keepdims=True)
    rank = jnp.sum(jnp.where((row_s == row) & (i < j), 1.0, 0.0), axis=0, keepdims=True)
    q = row[0:1] * p.k + rank
    q_s = jnp.sum(jnp.where(i == j, jnp.broadcast_to(q, (s, s)), 0.0), axis=1, keepdims=True)
    return q, q_s


def lane_route(p):
    lane = iota((1, p.rows), 1)
    r = jnp.floor((lane.astype(F32) + 0.5) * (1.0 / p.ru)).astype(jnp.int32)
    i = lane - r * p.ru
    return r, i >> log2(p.k), i & (p.k - 1)


def restrict_kernel(p, v_ref, t_ref, b_ref, out_ref, g3_ref, up_ref, down_ref, last, first):
    n, k, s = p.n, p.k, p.slots
    me = lax.axis_index("xy")
    table = t_ref[...]
    q, q_s = send_positions(p, table)
    lanes = p.cz * s
    rep = one_hot((iota((s, lanes), 1) & (s - 1)) == iota((s, lanes), 0))
    qt = dot(jnp.broadcast_to(q, (8, s)).astype(BF16), rep)[0:1]
    shape = (n, p.ru, lanes)
    i = iota(shape, 1)
    target = (iota(shape, 0) * k + (i & (k - 1))).astype(F32)
    g = one_hot(((i >> log2(k)) == (iota(shape, 2) >> log2(s))) & (target == qt.reshape(1, 1, lanes)))
    g = g.reshape(p.rows, lanes)
    r_l, c_l, j_l = lane_route(p)
    shape = (p.cz, s, p.rows)
    g3 = (iota(shape, 0) == c_l.reshape(1, 1, p.rows)) & (
        q_s.reshape(1, s, 1) == (r_l * k + j_l).astype(F32).reshape(1, 1, p.rows)
    )
    g3_ref[...] = one_hot(g3).reshape(p.cz * s, p.rows)
    half_fine = p.edge * p.edge // 2
    half_area = p.area // 2
    f, c = iota((half_fine, half_area), 0), iota((half_fine, half_area), 1)
    e = log2(p.edge)
    coarse = ((f >> (e + 1)) << (e - 1)) + ((f & (p.edge - 1)) >> 1)
    sel = one_hot(coarse == c)
    z_sum = jnp.concatenate(
        [v_ref[c, 2 * z] + v_ref[c, 2 * z + 1] for c in range(3) for z in range(p.zc)], axis=0
    )
    hi, lo = split(z_sum)
    parts = []
    for h in range(2):
        w = slice(h * half_fine, (h + 1) * half_fine)
        parts.append(dot(hi[:, w], sel) + dot(lo[:, w], sel))
    u = jnp.concatenate(parts, axis=1) * 0.125
    hi, lo = split(u)
    out_ref[:, : p.ru, :] = (dot(g, hi) + dot(g, lo)).reshape(n, p.ru, p.area)
    for c in range(3):
        for z in range(p.zc):
            for h in range(p.wrap):
                at = (c * p.zc + z) * p.wrap + h
                w = slice(h * p.area, (h + 1) * p.area)
                last[at : at + 1, :] = b_ref[c, z, p.ny - 1 : p.ny, w]
                first[at : at + 1, :] = b_ref[c, z, 0:1, w]
    nxt = lax.rem(me + 1, n)
    for r in range(n):
        out_ref[r, p.ru : p.ru + p.rb, :] = jnp.where(r == nxt, last[: p.rb], first[: p.rb])
    col = jnp.broadcast_to((table & (p.bcols - 1)).astype(F32), (s, s))
    qi = iota((s, s), 0).astype(F32)
    col_q = jnp.sum(jnp.where(qi == jnp.broadcast_to(q, (s, s)), col, 0.0), axis=1, keepdims=True)
    qa, la = iota((s, p.area), 0), iota((s, p.area), 1)
    spread = jnp.where((qa & (k - 1)) == (la & (k - 1)), col_q, 0.0).astype(BF16)
    gather = one_hot((iota((n, s), 1) >> log2(k)) == iota((n, s), 0))
    cols = dot(gather, spread)
    at = p.ru + p.rb
    for r in range(n):
        out_ref[r, at : at + 1, :] = cols[r : r + 1]
    up_ref[...] = b_ref[:, p.zc - 1]
    down_ref[...] = b_ref[:, 0]


def tile_transpose(p, t):
    ax = t.ndim - 2
    s, g = iota(t.shape, ax), iota(t.shape, ax + 1) >> log2(p.half)
    for b in (1, 2, 4):
        w = b * p.half
        up = pltpu.roll(pltpu.roll(t, 8 - b, ax), w, ax + 1)
        dn = up if b == 4 else pltpu.roll(pltpu.roll(t, b, ax), 128 - w, ax + 1)
        sb, gb = (s & b) != 0, (g & b) != 0
        t = jnp.where(sb == gb, t, jnp.where(gb, up, dn))
    return t


def blocks_to_grid(p, blk):
    rows = []
    for yh in range(p.half // 8):
        rows.append(
            jnp.concatenate(
                [
                    tile_transpose(p, blk[8 * c : 8 * c + 8, 128 * yh : 128 * yh + 128])
                    for c in range(p.bcols // 8)
                ],
                axis=1,
            )
        )
    return jnp.concatenate(rows, axis=0)


def grid_to_blocks(p, grid):
    rows = []
    for c in range(p.bcols // 8):
        rows.append(
            jnp.concatenate(
                [
                    tile_transpose(p, grid[8 * yh : 8 * yh + 8, 128 * c : 128 * c + 128])
                    for yh in range(p.half // 8)
                ],
                axis=1,
            )
        )
    return jnp.concatenate(rows, axis=0)


def x_next(f):
    return pltpu.roll(f, f.shape[1] - 1, 1)


def x_prev(f):
    return pltpu.roll(f, 1, 1)


def y_next(f, halo):
    return jnp.where(iota(f.shape, 0) == f.shape[0] - 1, halo, pltpu.roll(f, f.shape[0] - 1, 0))


def y_prev(f, halo):
    return jnp.where(iota(f.shape, 0) == 0, halo, pltpu.roll(f, 1, 0))


def row_of(p, ref, src, at):
    return jnp.concatenate([ref[src, pl.ds(at + h, 1), :] for h in range(p.wrap)], axis=1)


def field_kernel(p, r_ref, b_ref, lo_ref, hi_ref, out_ref, next_ref, up_ref, down_ref, e_rows):
    n, k, zc = p.n, p.k, p.zc
    me = lax.axis_index("xy")
    nxt, prv = lax.rem(me + 1, n), lax.rem(me + n - 1, n)
    cols = r_ref[:, p.ru + p.rb, :]
    r_l, c_l, _ = lane_route(p)
    shape = (n, p.rows)
    col_l = jnp.sum(jnp.where(iota(shape, 0) == r_l, cols[:, : p.rows], 0.0), axis=0, keepdims=True)
    shape = (p.cz, p.bcols, p.rows)
    g2 = one_hot(
        (iota(shape, 0) == c_l.reshape(1, 1, p.rows))
        & (iota(shape, 1).astype(F32) == col_l.reshape(1, 1, p.rows))
    ).reshape(p.cz * p.bcols, p.rows)
    shape = (n, p.ru, 128)
    col_s = jnp.sum(
        jnp.where((iota(shape, 1) & (k - 1)) == iota(shape, 2), cols[:, None, :128], 0.0), axis=2, keepdims=True
    )
    lanes = p.cz * p.bcols
    shape = (n, p.ru, lanes)
    lane = iota(shape, 2)
    g2t = one_hot(
        ((iota(shape, 1) >> log2(k)) == (lane >> log2(p.bcols)))
        & (col_s == (lane & (p.bcols - 1)).astype(F32))
    ).reshape(p.rows, lanes)
    hi, lo = split(r_ref[:, : p.ru, :].reshape(p.rows, p.area))
    u_blk = dot(g2, hi) + dot(g2, lo)
    u = [
        [blocks_to_grid(p, u_blk[(c * zc + z) * p.bcols : (c * zc + z + 1) * p.bcols]) for z in range(zc)]
        for c in range(3)
    ]
    b = [[b_ref[c, z] for z in range(zc)] for c in range(3)]
    force = []
    for z in range(zc):
        bz = [b[c][z] for c in range(3)]
        below = [lo_ref[c] if z == 0 else b[c][z - 1] for c in range(3)]
        above = [hi_ref[c] if z == zc - 1 else b[c][z + 1] for c in range(3)]
        north, south, east, west = [], [], [], []
        for c in range(3):
            at = p.ru + (c * zc + z) * p.wrap
            south.append(y_prev(bz[c], row_of(p, r_ref, prv, at)))
            north.append(y_next(bz[c], row_of(p, r_ref, nxt, at)))
            east.append(x_next(bz[c]))
            west.append(x_prev(bz[c]))
        dz = [(above[c] - below[c]) * 0.5 for c in range(2)]
        j0 = (north[2] - south[2]) * 0.5 - dz[1]
        j1 = dz[0] - (east[2] - west[2]) * 0.5
        j2 = (east[1] - west[1]) * 0.5 - (north[0] - south[0]) * 0.5
        force.append([j1 * bz[2] - j2 * bz[1], j2 * bz[0] - j0 * bz[2], j0 * bz[1] - j1 * bz[0]])
        for c in range(3):
            lap = above[c] + below[c] + north[c] + south[c] + east[c] + west[c] - 6.0 * bz[c]
            next_ref[c, z] = bz[c] + 0.05 * lap
    f_blk = jnp.concatenate([grid_to_blocks(p, force[z][c]) for c in range(3) for z in range(zc)], axis=0)
    hi, lo = split(f_blk)
    out_ref[:, : p.ru, :] = (dot(g2t, hi) + dot(g2t, lo)).reshape(n, p.ru, p.area)
    e = []
    for z in range(zc):
        uz, bz = [u[c][z] for c in range(3)], [b[c][z] for c in range(3)]
        e.append([uz[1] * bz[2] - uz[2] * bz[1], uz[2] * bz[0] - uz[0] * bz[2], uz[0] * bz[1] - uz[1] * bz[0]])
    for z in range(zc):
        ez = e[z]
        zero = jnp.zeros_like(ez[0])
        above = e[z + 1] if z < zc - 1 else (zero, zero)
        below = e[z - 1] if z > 0 else (zero, zero)
        dy2 = y_next(ez[2], 0.0) - y_prev(ez[2], 0.0)
        dy0 = y_next(ez[0], 0.0) - y_prev(ez[0], 0.0)
        next_ref[0, z] += 0.05 * (dy2 - (above[1] - below[1]))
        next_ref[1, z] += 0.05 * ((above[0] - below[0]) - (x_next(ez[2]) - x_prev(ez[2])))
        next_ref[2, z] += 0.05 * ((x_next(ez[1]) - x_prev(ez[1])) - dy0)
        for i, c in enumerate((0, 2)):
            for h in range(p.wrap):
                at = (i * zc + z) * p.wrap + h
                w = slice(h * p.area, (h + 1) * p.area)
                e_rows[0, at : at + 1, :] = ez[c][0:1, w]
                e_rows[1, at : at + 1, :] = ez[c][p.ny - 1 : p.ny, w]
    for r in range(n):
        out_ref[r, p.ru : p.ru + p.re, :] = jnp.where(r == nxt, e_rows[1], e_rows[0])
    up_ref[0], up_ref[1] = e[zc - 1][0], e[zc - 1][1]
    down_ref[0], down_ref[1] = e[0][0], e[0][1]


def widen_kernel(p, r_ref, g_ref, v_ref, out_ref):
    half_fine = p.edge * p.edge // 2
    half_area = p.area // 2
    e = log2(p.edge)
    c, f = iota((half_area, half_fine), 0), iota((half_area, half_fine), 1)
    coarse = ((f >> (e + 1)) << (e - 1)) + ((f & (p.edge - 1)) >> 1)
    sel = one_hot(coarse == c)
    hi, lo = split(r_ref[:, : p.ru, :].reshape(p.rows, p.area) * 0.1)
    g = g_ref[...]
    hi, lo = dot(g, hi).astype(BF16), dot(g, lo).astype(BF16)
    s = p.slots
    for h in range(2):
        w = slice(h * half_area, (h + 1) * half_area)
        wide = dot(hi[:, w], sel) + dot(lo[:, w], sel)
        fw = slice(h * half_fine, (h + 1) * half_fine)
        for c in range(3):
            for z in range(p.zc):
                add = wide[(c * p.zc + z) * s : (c * p.zc + z + 1) * s]
                for d in range(2):
                    out_ref[c, 2 * z + d, :, fw] = v_ref[c, 2 * z + d, :, fw] + add


def finish_kernel(p, n_ref, r_ref, lo_ref, hi_ref, out_ref):
    n, zc = p.n, p.zc
    me = lax.axis_index("xy")
    nxt, prv = lax.rem(me + 1, n), lax.rem(me + n - 1, n)
    y = iota((p.ny, p.nx), 0)

    def dy(i, z):
        at = p.ru + (i * zc + z) * p.wrap
        north, south = row_of(p, r_ref, nxt, at), row_of(p, r_ref, prv, at)
        return jnp.where(y == p.ny - 1, north, 0.0) - jnp.where(y == 0, south, 0.0)

    for z in range(zc):
        zero = jnp.zeros((p.ny, p.nx), F32)
        dz = [zero, zero]
        for c in range(2):
            if z == zc - 1:
                dz[c] = dz[c] + hi_ref[c]
            if z == 0:
                dz[c] = dz[c] - lo_ref[c]
        out_ref[0, z] = n_ref[0, z] + 0.05 * (dy(1, z) - dz[1])
        out_ref[1, z] = n_ref[1, z] + 0.05 * dz[0]
        out_ref[2, z] = n_ref[2, z] - 0.05 * dy(0, z)


def struct(*shape, dtype=F32):
    return jax.ShapeDtypeStruct(shape, dtype)


def call(kernel, outs, n_in, name, scratch=()):
    return pl.pallas_call(
        kernel,
        out_shape=outs,
        in_specs=[VMEM] * n_in,
        out_specs=jax.tree.map(lambda _: VMEM, outs),
        scratch_shapes=list(scratch),
        name=name,
    )


def ring(axis, step):
    n = lax.axis_size(axis)
    return [(i, (i + step) % n) for i in range(n)]


def body(velocity, magnetic, slot_block_table):
    p = Plan(velocity.shape, magnetic.shape, lax.axis_size("xy"))
    plane = (p.ny, p.nx)
    sent, g3, up, down = call(
        functools.partial(restrict_kernel, p),
        (
            struct(p.n, p.r1, p.area),
            struct(p.cz * p.slots, p.rows, dtype=BF16),
            struct(3, *plane),
            struct(3, *plane),
        ),
        3,
        "restrict",
        [pltpu.VMEM((-(-p.rb // 8) * 8, p.area), F32)] * 2,
    )(velocity, slot_block_table.reshape(1, p.slots), magnetic)
    got = lax.all_to_all(sent, "xy", 0, 0, tiled=True)
    below = lax.ppermute(up, "gz", ring("gz", 1))
    above = lax.ppermute(down, "gz", ring("gz", -1))
    sent, partial, up, down = call(
        functools.partial(field_kernel, p),
        (struct(p.n, p.r2, p.area), struct(*magnetic.shape), struct(2, *plane), struct(2, *plane)),
        4,
        "field",
        [pltpu.VMEM((2, p.re, p.area), F32)],
    )(got, magnetic, below, above)
    got = lax.all_to_all(sent, "xy", 0, 0, tiled=True)
    below = lax.ppermute(up, "gz", ring("gz", 1))
    above = lax.ppermute(down, "gz", ring("gz", -1))
    updated = call(functools.partial(widen_kernel, p), struct(*velocity.shape), 3, "widen")(got, g3, velocity)
    finished = call(functools.partial(finish_kernel, p), struct(*magnetic.shape), 4, "finish")(
        partial, got, below, above
    )
    return updated, finished


def solution(mesh):
    return jax.shard_map(
        body,
        mesh=mesh,
        in_specs=(P(None, "gz", "xy", None), P(None, "gz", "xy", None), P("xy")),
        out_specs=(P(None, "gz", "xy", None), P(None, "gz", "xy", None)),
        check_vma=False,
    )
```

time: 106 us -> 39.1 us (0.37)
  local copies, waits for them, and re-layouts: 35.8 us -> 2.68 us
  other arithmetic: 26.2 us -> 0 us
  waiting for transfers between devices: 22.3 us -> 8.08 us
  Pallas kernels: 0 us -> 10.6 us
  starting transfers between devices: 19.4 us -> 16.7 us
    gather x7 -> x0, local copies, waits for them, and re-layouts: 11 us -> none  [the longest x2 6.93 us: body(): ordered = velocity[:, :, sorted_positions]]
    pallas_call x0 -> x4, Pallas kernels: none -> 10.6 us  [the longest x1 3.19 us: body(): call(functools.partial(widen_kernel, p), struct(*velocity.shape), 3, 'wid...]
    ppermute x4, waiting for transfers between devices: 13.5 us -> 5 us  [the longest x2 3.86 us: body(): below = lax.ppermute(up, 'gz', ring('gz', 1))]
    unnamed x42 -> x12, local copies, waits for them, and re-layouts: 10.9 us -> 2.68 us
    reduce_sum x1 -> x0, other arithmetic: 7.27 us -> none  [restrict(): jnp.sum(v, axis=(2, 5, 7)) * 0.125]
    add x2 -> x0, other arithmetic: 7.14 us -> none  [the longest x1 6.28 us: body(): velocity + 0.1 * widened_tiles.reshape(3, coarse_depth_index * 2, slot_co...]
    sort x3 -> x0, other arithmetic: 6.14 us -> none  [the longest x1 2.27 us: body(): blocks_per_slot = returned[:, :, jnp.argsort(sorted_positions)]]
    all_to_all x3 -> x2, waiting for transfers between devices: 8.9 us -> 3.08 us  [body(): got = lax.all_to_all(sent, 'xy', 0, 0, tiled=True)]
  transfers between devices with their start and end apart: 7 -> 6, of which waited for: 5 -> 3; matrix products, arithmetic and copies ran while one was open for 28% -> 0% of each run, Pallas kernels for 0% -> 8%
where the time goes in v1:
time: 39.1 us; the launch traced here: 38.7 us
  starting transfers between devices  16.7 us (43%)
  Pallas kernels  10.6 us (27%)
  waiting for transfers between devices  8.08 us (21%)
  local copies, waits for them, and re-layouts  2.68 us (7%)
  between operations  0.66 us (2%)
    all_to_all x2, starting transfers between devices, body(): got = lax.all_to_all(sent, 'xy', 0, 0, tiled=True)  9.01 us
    ppermute x2, starting transfers between devices, body(): above = lax.ppermute(down, 'gz', ring('gz', -1))  4.95 us
    ppermute x2, waiting for transfers between devices, body(): below = lax.ppermute(up, 'gz', ring('gz', 1))  3.86 us
    pallas_call x1, Pallas kernels, body(): call(functools.partial(widen_kernel, p), struct(*velocity.shape), 3, 'wid...  3.19 us
    all_to_all x2, waiting for transfers between devices, body(): got = lax.all_to_all(sent, 'xy', 0, 0, tiled=True)  3.08 us
    pallas_call x1, Pallas kernels, body(): call(functools.partial(field_kernel, p), (struct(p.n, p.r2, p.area), stru...  2.88 us
    pallas_call x1, Pallas kernels, body(): call(functools.partial(restrict_kernel, p), (struct(p.n, p.r1, p.area), s...  2.81 us
    ppermute x2, starting transfers between devices, body(): below = lax.ppermute(up, 'gz', ring('gz', 1))  2.7 us
  transfers between devices with their start and end apart: 6, of which 3 were waited for; matrix products, arithmetic and copies ran while one was open for 0% of the time, Pallas kernels for 8%

profile of v1, /device:TPU:0, one launch (start us, length us, event | category | flops | bytes accessed | tf_op | source)
XLA Modules:
  0.0 38.7 jit_solution(5456568529047498528)
XLA Ops:
  0.6 2.8 %restrict.1 = (f32[8,40,256]{2,1,0:T(8,128)}, bf16[192,192]{1,0:T(8,128)(2,1)}, f32[3,16,512]{2,1,0:T(8,128)}, f32[3,16,512]{2,1,0:T(8,128)}) custom-call(f32[3,4,32,1024]{3,2,1,0:T(8,128)} %v_ref.3, s32[1,32]{1,0:T(1,128)} %bitcast.1, f32[3,2,16,512]{3,2,1,0:T(8,128)} %b_ref.3), custom_call_target="tpu_custom_call" | custom-call | tf_op jit(solution)/shard_map/restrict/pallas_call | solution.py:347
  3.4 5.2 %all-to-all-start = ((f32[8,40,256]{2,1,0:T(8,128)}), f32[8,40,256]{2,1,0:T(8,128)S(1)}, u32[]{:S(2)}, u32[]{:S(2)}) async-start(f32[8,40,256]{2,1,0:T(8,128)} %get-tuple-element.10), calls=%async_computation | async-start | bytes 655360 | tf_op jit(solution)/shard_map/all_to_all | solution.py:359
  8.6 1.6 %collective-permute-start = (f32[3,16,512]{2,1,0:T(8,128)}, f32[3,16,512]{2,1,0:T(8,128)S(1)}, u32[]{:S(2)}, u32[]{:S(2)}) collective-permute-start(f32[3,16,512]{2,1,0:T(8,128)} %get-tuple-element.11), channel_id=1, source_target_pairs={{0,1},{1,2},{2,3},{3,0},{4,5},{5,6},{6,7},{7,4},{8,9},{9,10},{10,1... | collective-permute-start | bytes 294920 | tf_op jit(solution)/shard_map/ppermute | solution.py:360
  10.2 2.2 %collective-permute-start.1 = (f32[3,16,512]{2,1,0:T(8,128)}, f32[3,16,512]{2,1,0:T(8,128)S(1)}, u32[]{:S(2)}, u32[]{:S(2)}) collective-permute-start(f32[3,16,512]{2,1,0:T(8,128)} %get-tuple-element.12), channel_id=1, source_target_pairs={{0,3},{1,0},{2,1},{3,2},{4,7},{5,4},{6,5},{7,6},{8,11},{9,8},{10,9... | collective-permute-start | bytes 294920 | tf_op jit(solution)/shard_map/ppermute | solution.py:361
  12.5 3.9 %collective-permute-done.lo_ref = f32[3,16,512]{2,1,0:T(8,128)S(1)} collective-permute-done((f32[3,16,512]{2,1,0:T(8,128)}, f32[3,16,512]{2,1,0:T(8,128)S(1)}, u32[]{:S(2)}, u32[]{:S(2)}) %collective-permute-start) | collective-permute-done | bytes 98336 | tf_op jit(solution)/shard_map/ppermute | solution.py:360
  16.3 0.0 copy-start.2
  16.3 1.1 %collective-permute-done.1.hi_ref = f32[3,16,512]{2,1,0:T(8,128)S(1)} collective-permute-done((f32[3,16,512]{2,1,0:T(8,128)}, f32[3,16,512]{2,1,0:T(8,128)S(1)}, u32[]{:S(2)}, u32[]{:S(2)}) %collective-permute-start.1) | collective-permute-done | bytes 98336 | tf_op jit(solution)/shard_map/ppermute | solution.py:361
  17.5 0.0 all-to-all-done.r_ref
  17.5 0.0 copy-done.2
  17.5 0.6 %copy-done.3 = f32[3,16,512]{2,1,0:T(8,128)} copy-done((f32[3,16,512]{2,1,0:T(8,128)}, f32[3,16,512]{2,1,0:T(8,128)S(1)}, u32[]{:S(2)}) %copy-start.3) | copy-done | bytes 98328
  18.1 0.7 %copy-done.1 = f32[8,40,256]{2,1,0:T(8,128)} copy-done((f32[8,40,256]{2,1,0:T(8,128)}, f32[8,40,256]{2,1,0:T(8,128)S(1)}, u32[]{:S(2)}) %copy-start.1) | copy-done | bytes 327704
  18.8 2.9 %field.1 = (f32[8,32,256]{2,1,0:T(8,128)}, f32[3,2,16,512]{3,2,1,0:T(8,128)}, f32[2,16,512]{2,1,0:T(8,128)}, f32[2,16,512]{2,1,0:T(8,128)}) custom-call(f32[8,40,256]{2,1,0:T(8,128)} %copy-done.1, f32[3,2,16,512]{3,2,1,0:T(8,128)} %b_ref.3, f32[3,16,512]{2,1,0:T(8,128)} %copy-done.2, f32[3,16,512]{2,1,0:T(8,128)} %copy-done.3), custom_call_target="tpu_custom_call" | custom-call | tf_op jit(solution)/shard_map/field/pallas_call | solution.py:362
  21.7 3.8 %all-to-all-start.1 = ((f32[8,32,256]{2,1,0:T(8,128)}), f32[8,32,256]{2,1,0:T(8,128)S(1)}, u32[]{:S(2)}, u32[]{:S(2)}) async-start(f32[8,32,256]{2,1,0:T(8,128)} %get-tuple-element.13), calls=%async_computation.1 | async-start | bytes 524288 | tf_op jit(solution)/shard_map/all_to_all | solution.py:369
  25.5 1.1 %collective-permute-start.2 = (f32[2,16,512]{2,1,0:T(8,128)}, f32[2,16,512]{2,1,0:T(8,128)S(1)}, u32[]{:S(2)}, u32[]{:S(2)}) collective-permute-start(f32[2,16,512]{2,1,0:T(8,128)} %get-tuple-element.16), channel_id=1, source_target_pairs={{0,1},{1,2},{2,3},{3,0},{4,5},{5,6},{6,7},{7,4},{8,9},{9,10},{10,1... | collective-permute-start | bytes 196616 | tf_op jit(solution)/shard_map/ppermute | solution.py:370
  26.6 2.7 %collective-permute-start.3 = (f32[2,16,512]{2,1,0:T(8,128)}, f32[2,16,512]{2,1,0:T(8,128)S(1)}, u32[]{:S(2)}, u32[]{:S(2)}) collective-permute-start(f32[2,16,512]{2,1,0:T(8,128)} %get-tuple-element.17), channel_id=1, source_target_pairs={{0,3},{1,0},{2,1},{3,2},{4,7},{5,4},{6,5},{7,6},{8,11},{9,8},{10,9... | collective-permute-start | bytes 196616 | tf_op jit(solution)/shard_map/ppermute | solution.py:371
  29.3 3.1 %all-to-all-done.1.r_ref = f32[8,32,256]{2,1,0:T(8,128)S(1)} async-done(((f32[8,32,256]{2,1,0:T(8,128)}), f32[8,32,256]{2,1,0:T(8,128)S(1)}, u32[]{:S(2)}, u32[]{:S(2)}) %all-to-all-start.1) | async-done | bytes 262176 | tf_op jit(solution)/shard_map/all_to_all | solution.py:369
  32.4 0.7 %copy-done = f32[8,32,256]{2,1,0:T(8,128)} copy-done((f32[8,32,256]{2,1,0:T(8,128)}, f32[8,32,256]{2,1,0:T(8,128)S(1)}, u32[]{:S(2)}) %copy-start) | copy-done | bytes 262168
  33.1 3.2 %widen.1 = f32[3,4,32,1024]{3,2,1,0:T(8,128)} custom-call(f32[8,32,256]{2,1,0:T(8,128)} %copy-done, bf16[192,192]{1,0:T(8,128)(2,1)} %get-tuple-element.14.g_ref, f32[3,4,32,1024]{3,2,1,0:T(8,128)} %v_ref.3), custom_call_target="tpu_custom_call" | custom-call | tf_op jit(solution)/shard_map/widen/pallas_call | solution.py:372
  36.3 0.0 collective-permute-done.2.lo_ref
  36.3 0.0 collective-permute-done.3.hi_ref
  36.3 0.0 copy-start.5
  36.3 0.6 %copy-done.4 = f32[2,16,512]{2,1,0:T(8,128)} copy-done((f32[2,16,512]{2,1,0:T(8,128)}, f32[2,16,512]{2,1,0:T(8,128)S(1)}, u32[]{:S(2)}) %copy-start.4) | copy-done | bytes 65560
  36.9 0.0 copy-done.5
  36.9 1.8 %finish.1 = f32[3,2,16,512]{3,2,1,0:T(8,128)} custom-call(f32[3,2,16,512]{3,2,1,0:T(8,128)} %get-tuple-element.15.n_ref, f32[8,32,256]{2,1,0:T(8,128)} %copy-done, f32[2,16,512]{2,1,0:T(8,128)} %copy-done.4, f32[2,16,512]{2,1,0:T(8,128)} %copy-done.5), custom_call_target="tpu_custom_call" | custom-call | tf_op jit(solution)/shard_map/finish/pallas_call | solution.py:373
  (4 shorter events, 0.0 us)
Async XLA Ops:
  3.4 14.0 %all-to-all-start = ((f32[8,40,256]{2,1,0:T(8,128)}), f32[8,40,256]{2,1,0:T(8,128)S(1)}, u32[]{:S(2)}, u32[]{:S(2)}) async-start(f32[8,40,256]{2,1,0:T(8,128)} %get-tuple-element.10), calls=%async_computation | async-start | bytes 655360 | tf_op jit(solution)/shard_map/all_to_all | solution.py:359
  8.6 7.7 %collective-permute-start = (f32[3,16,512]{2,1,0:T(8,128)}, f32[3,16,512]{2,1,0:T(8,128)S(1)}, u32[]{:S(2)}, u32[]{:S(2)}) collective-permute-start(f32[3,16,512]{2,1,0:T(8,128)} %get-tuple-element.11), channel_id=1, source_target_pairs={{0,1},{1,2},{2,3},{3,0},{4,5},{5,6},{6,7},{7,4},{8,9},{9,10},{10,1... | collective-permute-start | bytes 294920 | tf_op jit(solution)/shard_map/ppermute | solution.py:360
  10.2 7.2 %collective-permute-start.1 = (f32[3,16,512]{2,1,0:T(8,128)}, f32[3,16,512]{2,1,0:T(8,128)S(1)}, u32[]{:S(2)}, u32[]{:S(2)}) collective-permute-start(f32[3,16,512]{2,1,0:T(8,128)} %get-tuple-element.12), channel_id=1, source_target_pairs={{0,3},{1,0},{2,1},{3,2},{4,7},{5,4},{6,5},{7,6},{8,11},{9,8},{10,9... | collective-permute-start | bytes 294920 | tf_op jit(solution)/shard_map/ppermute | solution.py:361
  16.3 1.1 %copy-start.2 = (f32[3,16,512]{2,1,0:T(8,128)}, f32[3,16,512]{2,1,0:T(8,128)S(1)}, u32[]{:S(2)}) copy-start(f32[3,16,512]{2,1,0:T(8,128)S(1)} %collective-permute-done.lo_ref) | copy-start | bytes 294916
  17.5 0.6 %copy-start.3 = (f32[3,16,512]{2,1,0:T(8,128)}, f32[3,16,512]{2,1,0:T(8,128)S(1)}, u32[]{:S(2)}) copy-start(f32[3,16,512]{2,1,0:T(8,128)S(1)} %collective-permute-done.1.hi_ref) | copy-start | bytes 294916
  18.1 0.7 %copy-start.1 = (f32[8,40,256]{2,1,0:T(8,128)}, f32[8,40,256]{2,1,0:T(8,128)S(1)}, u32[]{:S(2)}) copy-start(f32[8,40,256]{2,1,0:T(8,128)S(1)} %all-to-all-done.r_ref) | copy-start | bytes 983044
  21.7 10.7 %all-to-all-start.1 = ((f32[8,32,256]{2,1,0:T(8,128)}), f32[8,32,256]{2,1,0:T(8,128)S(1)}, u32[]{:S(2)}, u32[]{:S(2)}) async-start(f32[8,32,256]{2,1,0:T(8,128)} %get-tuple-element.13), calls=%async_computation.1 | async-start | bytes 524288 | tf_op jit(solution)/shard_map/all_to_all | solution.py:369
  25.5 10.8 %collective-permute-start.2 = (f32[2,16,512]{2,1,0:T(8,128)}, f32[2,16,512]{2,1,0:T(8,128)S(1)}, u32[]{:S(2)}, u32[]{:S(2)}) collective-permute-start(f32[2,16,512]{2,1,0:T(8,128)} %get-tuple-element.16), channel_id=1, source_target_pairs={{0,1},{1,2},{2,3},{3,0},{4,5},{5,6},{6,7},{7,4},{8,9},{9,10},{10,1... | collective-permute-start | bytes 196616 | tf_op jit(solution)/shard_map/ppermute | solution.py:370
  26.6 9.7 %collective-permute-start.3 = (f32[2,16,512]{2,1,0:T(8,128)}, f32[2,16,512]{2,1,0:T(8,128)S(1)}, u32[]{:S(2)}, u32[]{:S(2)}) collective-permute-start(f32[2,16,512]{2,1,0:T(8,128)} %get-tuple-element.17), channel_id=1, source_target_pairs={{0,3},{1,0},{2,1},{3,2},{4,7},{5,4},{6,5},{7,6},{8,11},{9,8},{10,9... | collective-permute-start | bytes 196616 | tf_op jit(solution)/shard_map/ppermute | solution.py:371
  32.4 0.7 %copy-start = (f32[8,32,256]{2,1,0:T(8,128)}, f32[8,32,256]{2,1,0:T(8,128)S(1)}, u32[]{:S(2)}) copy-start(f32[8,32,256]{2,1,0:T(8,128)S(1)} %all-to-all-done.1.r_ref) | copy-start | bytes 786436
  36.3 0.6 %copy-start.4 = (f32[2,16,512]{2,1,0:T(8,128)}, f32[2,16,512]{2,1,0:T(8,128)S(1)}, u32[]{:S(2)}) copy-start(f32[2,16,512]{2,1,0:T(8,128)S(1)} %collective-permute-done.2.lo_ref) | copy-start | bytes 196612
  36.3 0.6 %copy-start.5 = (f32[2,16,512]{2,1,0:T(8,128)}, f32[2,16,512]{2,1,0:T(8,128)S(1)}, u32[]{:S(2)}) copy-start(f32[2,16,512]{2,1,0:T(8,128)S(1)} %collective-permute-done.3.hi_ref) | copy-start | bytes 196612

commit v2 on v1

--- a/solution.py
+++ b/solution.py
@@ -333,6 +333,7 @@
         out_specs=jax.tree.map(lambda _: VMEM, outs),
         scratch_shapes=list(scratch),
         name=name,
+        compiler_params=pltpu.CompilerParams(vmem_limit_bytes=20 << 20),
     )
 
 

time: 39.1 us -> 34 us (0.87)
  Pallas kernels: 10.6 us -> 5.48 us
    pallas_call x1, Pallas kernels: 3.19 us -> 1.64 us  [body(): call(functools.partial(widen_kernel, p), struct(*velocity.shape), 3, 'wid...]
    pallas_call x1, Pallas kernels: 2.81 us -> 1.37 us  [body(): call(functools.partial(restrict_kernel, p), (struct(p.n, p.r1, p.area), s...]
    pallas_call x1, Pallas kernels: 2.88 us -> 1.75 us  [body(): call(functools.partial(field_kernel, p), (struct(p.n, p.r2, p.area), stru...]
    pallas_call x1, Pallas kernels: 1.76 us -> 0.72 us  [body(): call(functools.partial(finish_kernel, p), struct(*magnetic.shape), 4, 'fi...]
    unnamed x12 -> x10, local copies, waits for them, and re-layouts: 2.68 us -> 2.99 us
  transfers between devices with their start and end apart: 6 -> 6, of which waited for: 3 -> 3; matrix products, arithmetic and copies ran while one was open for 0% -> 0% of each run, Pallas kernels for 8% -> 5%
where the time goes in v2:
time: 34 us; the launch traced here: 33.6 us
  starting transfers between devices  16.7 us (49%)
  waiting for transfers between devices  7.87 us (23%)
  Pallas kernels  5.48 us (16%)
  local copies, waits for them, and re-layouts  2.99 us (9%)
  between operations  0.65 us (2%)
    all_to_all x2, starting transfers between devices, body(): got = lax.all_to_all(sent, 'xy', 0, 0, tiled=True)  9.01 us
    ppermute x2, starting transfers between devices, body(): above = lax.ppermute(down, 'gz', ring('gz', -1))  4.95 us
    ppermute x2, waiting for transfers between devices, body(): below = lax.ppermute(up, 'gz', ring('gz', 1))  3.65 us
    all_to_all x2, waiting for transfers between devices, body(): got = lax.all_to_all(sent, 'xy', 0, 0, tiled=True)  3.08 us
    unnamed x10, local copies, waits for them, and re-layouts  2.99 us
    ppermute x2, starting transfers between devices, body(): below = lax.ppermute(up, 'gz', ring('gz', 1))  2.7 us
    pallas_call x1, Pallas kernels, body(): call(functools.partial(field_kernel, p), (struct(p.n, p.r2, p.area), stru...  1.75 us
    pallas_call x1, Pallas kernels, body(): call(functools.partial(widen_kernel, p), struct(*velocity.shape), 3, 'wid...  1.64 us
  transfers between devices with their start and end apart: 6, of which 3 were waited for; matrix products, arithmetic and copies ran while one was open for 0% of the time, Pallas kernels for 5%

profile of v2, /device:TPU:0, one launch (start us, length us, event | category | flops | bytes accessed | tf_op | source)
XLA Modules:
  0.0 33.6 jit_solution(13877205567287450615)
XLA Ops:
  0.6 0.0 copy-start
  0.6 1.4 %copy-done = f32[3,4,32,1024]{3,2,1,0:T(8,128)S(1)} copy-done((f32[3,4,32,1024]{3,2,1,0:T(8,128)S(1)}, f32[3,4,32,1024]{3,2,1,0:T(8,128)}, u32[]{:S(2)}) %copy-start) | copy-done | bytes 1572888
  2.0 0.0 copy-start.2
  2.0 0.9 %copy-done.2 = f32[3,2,16,512]{3,2,1,0:T(8,128)S(1)} copy-done((f32[3,2,16,512]{3,2,1,0:T(8,128)S(1)}, f32[3,2,16,512]{3,2,1,0:T(8,128)}, u32[]{:S(2)}) %copy-start.2) | copy-done | bytes 196632
  3.0 0.0 copy-start.4
  3.0 0.7 %copy-done.4 = s32[32]{0:T(128)S(1)} copy-done((s32[32]{0:T(128)S(1)}, s32[32]{0:T(128)}, u32[]{:S(2)}) %copy-start.4) | copy-done | bytes 152
  3.6 1.4 %restrict.1 = (f32[8,40,256]{2,1,0:T(8,128)}, bf16[192,192]{1,0:T(8,128)(2,1)S(1)}, f32[3,16,512]{2,1,0:T(8,128)S(1)}, f32[3,16,512]{2,1,0:T(8,128)S(1)}) custom-call(f32[3,4,32,1024]{3,2,1,0:T(8,128)S(1)} %copy-done, s32[1,32]{1,0:T(1,128)S(1)} %bitcast.1, f32[3,2,16,512]{3,2,1,0:T(8,128)S(1)} %copy-done.2), custom_call_target="tpu_custom_call" | custom-call | tf_op jit(solution)/shard_map/restrict/pallas_call | solution.py:348
  5.0 5.2 %all-to-all-start = ((f32[8,40,256]{2,1,0:T(8,128)}), f32[8,40,256]{2,1,0:T(8,128)S(1)}, u32[]{:S(2)}, u32[]{:S(2)}) async-start(f32[8,40,256]{2,1,0:T(8,128)} %get-tuple-element.10), calls=%async_computation | async-start | bytes 655360 | tf_op jit(solution)/shard_map/all_to_all | solution.py:360
  10.2 1.6 %collective-permute-start = (f32[3,16,512]{2,1,0:T(8,128)S(1)}, f32[3,16,512]{2,1,0:T(8,128)S(1)}, u32[]{:S(2)}, u32[]{:S(2)}) collective-permute-start(f32[3,16,512]{2,1,0:T(8,128)S(1)} %get-tuple-element.11), channel_id=1, source_target_pairs={{0,1},{1,2},{2,3},{3,0},{4,5},{5,6},{6,7},{7,4},{8,9},{9,10},{10,1... | collective-permute-start | bytes 294920 | tf_op jit(solution)/shard_map/ppermute | solution.py:361
  11.8 2.2 %collective-permute-start.1 = (f32[3,16,512]{2,1,0:T(8,128)S(1)}, f32[3,16,512]{2,1,0:T(8,128)S(1)}, u32[]{:S(2)}, u32[]{:S(2)}) collective-permute-start(f32[3,16,512]{2,1,0:T(8,128)S(1)} %get-tuple-element.12), channel_id=1, source_target_pairs={{0,3},{1,0},{2,1},{3,2},{4,7},{5,4},{6,5},{7,6},{8,11},{9,8},{10,9... | collective-permute-start | bytes 294920 | tf_op jit(solution)/shard_map/ppermute | solution.py:362
  14.0 3.6 %collective-permute-done.lo_ref = f32[3,16,512]{2,1,0:T(8,128)S(1)} collective-permute-done((f32[3,16,512]{2,1,0:T(8,128)S(1)}, f32[3,16,512]{2,1,0:T(8,128)S(1)}, u32[]{:S(2)}, u32[]{:S(2)}) %collective-permute-start) | collective-permute-done | bytes 98336 | tf_op jit(solution)/shard_map/ppermute | solution.py:361
  17.7 1.1 %collective-permute-done.1.hi_ref = f32[3,16,512]{2,1,0:T(8,128)S(1)} collective-permute-done((f32[3,16,512]{2,1,0:T(8,128)S(1)}, f32[3,16,512]{2,1,0:T(8,128)S(1)}, u32[]{:S(2)}, u32[]{:S(2)}) %collective-permute-start.1) | collective-permute-done | bytes 98336 | tf_op jit(solution)/shard_map/ppermute | solution.py:362
  18.8 0.0 all-to-all-done.r_ref
  18.8 0.0 copy-done.3
  18.8 1.8 %field.1 = (f32[8,32,256]{2,1,0:T(8,128)}, f32[3,2,16,512]{3,2,1,0:T(8,128)S(1)}, f32[2,16,512]{2,1,0:T(8,128)S(1)}, f32[2,16,512]{2,1,0:T(8,128)S(1)}) custom-call(f32[8,40,256]{2,1,0:T(8,128)S(1)} %all-to-all-done.r_ref, f32[3,2,16,512]{3,2,1,0:T(8,128)S(1)} %copy-done.3, f32[3,16,512]{2,1,0:T(8,128)S(1)} %collective-permute-done.lo_ref, ...), custom_call_target="tpu_custom_call" | custom-call | tf_op jit(solution)/shard_map/field/pallas_call | solution.py:363
  20.6 3.8 %all-to-all-start.1 = ((f32[8,32,256]{2,1,0:T(8,128)}), f32[8,32,256]{2,1,0:T(8,128)S(1)}, u32[]{:S(2)}, u32[]{:S(2)}) async-start(f32[8,32,256]{2,1,0:T(8,128)} %get-tuple-element.13), calls=%async_computation.1 | async-start | bytes 524288 | tf_op jit(solution)/shard_map/all_to_all | solution.py:370
  24.4 1.1 %collective-permute-start.2 = (f32[2,16,512]{2,1,0:T(8,128)S(1)}, f32[2,16,512]{2,1,0:T(8,128)S(1)}, u32[]{:S(2)}, u32[]{:S(2)}) collective-permute-start(f32[2,16,512]{2,1,0:T(8,128)S(1)} %get-tuple-element.16), channel_id=1, source_target_pairs={{0,1},{1,2},{2,3},{3,0},{4,5},{5,6},{6,7},{7,4},{8,9},{9,10},{10,1... | collective-permute-start | bytes 196616 | tf_op jit(solution)/shard_map/ppermute | solution.py:371
  25.5 2.7 %collective-permute-start.3 = (f32[2,16,512]{2,1,0:T(8,128)S(1)}, f32[2,16,512]{2,1,0:T(8,128)S(1)}, u32[]{:S(2)}, u32[]{:S(2)}) collective-permute-start(f32[2,16,512]{2,1,0:T(8,128)S(1)} %get-tuple-element.17), channel_id=1, source_target_pairs={{0,3},{1,0},{2,1},{3,2},{4,7},{5,4},{6,5},{7,6},{8,11},{9,8},{10,9... | collective-permute-start | bytes 196616 | tf_op jit(solution)/shard_map/ppermute | solution.py:372
  28.2 3.1 %all-to-all-done.1.r_ref = f32[8,32,256]{2,1,0:T(8,128)S(1)} async-done(((f32[8,32,256]{2,1,0:T(8,128)}), f32[8,32,256]{2,1,0:T(8,128)S(1)}, u32[]{:S(2)}, u32[]{:S(2)}) %all-to-all-start.1) | async-done | bytes 262176 | tf_op jit(solution)/shard_map/all_to_all | solution.py:370
  31.3 0.0 copy-done.1
  31.3 1.6 %widen.1 = f32[3,4,32,1024]{3,2,1,0:T(8,128)} custom-call(f32[8,32,256]{2,1,0:T(8,128)S(1)} %all-to-all-done.1.r_ref, bf16[192,192]{1,0:T(8,128)(2,1)S(1)} %get-tuple-element.14.g_ref, f32[3,4,32,1024]{3,2,1,0:T(8,128)S(1)} %copy-done.1), custom_call_target="tpu_custom_call" | custom-call | tf_op jit(solution)/shard_map/widen/pallas_call | solution.py:373
  32.9 0.0 collective-permute-done.2.lo_ref
  32.9 0.0 collective-permute-done.3.hi_ref
  32.9 0.7 %finish.1 = f32[3,2,16,512]{3,2,1,0:T(8,128)} custom-call(f32[3,2,16,512]{3,2,1,0:T(8,128)S(1)} %get-tuple-element.15.n_ref, f32[8,32,256]{2,1,0:T(8,128)S(1)} %all-to-all-done.1.r_ref, f32[2,16,512]{2,1,0:T(8,128)S(1)} %collective-permute-done.2.lo_ref, f32[2,16,512]{2,1,0:T(8,128)S(1)} %collective-permute-done.3.hi_ref), custom_call_target="tpu_custom_call" | custom-call | tf_op jit(solution)/shard_map/finish/pallas_call | solution.py:374
  (2 shorter events, 0.0 us)
Async XLA Ops:
  0.6 1.4 %copy-start = (f32[3,4,32,1024]{3,2,1,0:T(8,128)S(1)}, f32[3,4,32,1024]{3,2,1,0:T(8,128)}, u32[]{:S(2)}) copy-start(f32[3,4,32,1024]{3,2,1,0:T(8,128)} %v_ref.3) | copy-start | bytes 4718596
  2.0 0.9 %copy-start.2 = (f32[3,2,16,512]{3,2,1,0:T(8,128)S(1)}, f32[3,2,16,512]{3,2,1,0:T(8,128)}, u32[]{:S(2)}) copy-start(f32[3,2,16,512]{3,2,1,0:T(8,128)} %b_ref.3) | copy-start | bytes 589828
  3.0 0.7 %copy-start.4 = (s32[32]{0:T(128)S(1)}, s32[32]{0:T(128)}, u32[]{:S(2)}) copy-start(s32[32]{0:T(128)} %param.5) | copy-start | bytes 388
  3.6 15.2 %copy-start.3 = (f32[3,2,16,512]{3,2,1,0:T(8,128)S(1)}, f32[3,2,16,512]{3,2,1,0:T(8,128)}, u32[]{:S(2)}) copy-start(f32[3,2,16,512]{3,2,1,0:T(8,128)} %b_ref.3) | copy-start | bytes 589828
  3.6 27.7 %copy-start.1 = (f32[3,4,32,1024]{3,2,1,0:T(8,128)S(1)}, f32[3,4,32,1024]{3,2,1,0:T(8,128)}, u32[]{:S(2)}) copy-start(f32[3,4,32,1024]{3,2,1,0:T(8,128)} %v_ref.3) | copy-start | bytes 4718596
  5.0 13.8 %all-to-all-start = ((f32[8,40,256]{2,1,0:T(8,128)}), f32[8,40,256]{2,1,0:T(8,128)S(1)}, u32[]{:S(2)}, u32[]{:S(2)}) async-start(f32[8,40,256]{2,1,0:T(8,128)} %get-tuple-element.10), calls=%async_computation | async-start | bytes 655360 | tf_op jit(solution)/shard_map/all_to_all | solution.py:360
  10.2 7.5 %collective-permute-start = (f32[3,16,512]{2,1,0:T(8,128)S(1)}, f32[3,16,512]{2,1,0:T(8,128)S(1)}, u32[]{:S(2)}, u32[]{:S(2)}) collective-permute-start(f32[3,16,512]{2,1,0:T(8,128)S(1)} %get-tuple-element.11), channel_id=1, source_target_pairs={{0,1},{1,2},{2,3},{3,0},{4,5},{5,6},{6,7},{7,4},{8,9},{9,10},{10,1... | collective-permute-start | bytes 294920 | tf_op jit(solution)/shard_map/ppermute | solution.py:361
  11.8 7.0 %collective-permute-start.1 = (f32[3,16,512]{2,1,0:T(8,128)S(1)}, f32[3,16,512]{2,1,0:T(8,128)S(1)}, u32[]{:S(2)}, u32[]{:S(2)}) collective-permute-start(f32[3,16,512]{2,1,0:T(8,128)S(1)} %get-tuple-element.12), channel_id=1, source_target_pairs={{0,3},{1,0},{2,1},{3,2},{4,7},{5,4},{6,5},{7,6},{8,11},{9,8},{10,9... | collective-permute-start | bytes 294920 | tf_op jit(solution)/shard_map/ppermute | solution.py:362
  20.6 10.7 %all-to-all-start.1 = ((f32[8,32,256]{2,1,0:T(8,128)}), f32[8,32,256]{2,1,0:T(8,128)S(1)}, u32[]{:S(2)}, u32[]{:S(2)}) async-start(f32[8,32,256]{2,1,0:T(8,128)} %get-tuple-element.13), calls=%async_computation.1 | async-start | bytes 524288 | tf_op jit(solution)/shard_map/all_to_all | solution.py:370
  24.4 8.5 %collective-permute-start.2 = (f32[2,16,512]{2,1,0:T(8,128)S(1)}, f32[2,16,512]{2,1,0:T(8,128)S(1)}, u32[]{:S(2)}, u32[]{:S(2)}) collective-permute-start(f32[2,16,512]{2,1,0:T(8,128)S(1)} %get-tuple-element.16), channel_id=1, source_target_pairs={{0,1},{1,2},{2,3},{3,0},{4,5},{5,6},{6,7},{7,4},{8,9},{9,10},{10,1... | collective-permute-start | bytes 196616 | tf_op jit(solution)/shard_map/ppermute | solution.py:371
  25.5 7.4 %collective-permute-start.3 = (f32[2,16,512]{2,1,0:T(8,128)S(1)}, f32[2,16,512]{2,1,0:T(8,128)S(1)}, u32[]{:S(2)}, u32[]{:S(2)}) collective-permute-start(f32[2,16,512]{2,1,0:T(8,128)S(1)} %get-tuple-element.17), channel_id=1, source_target_pairs={{0,3},{1,0},{2,1},{3,2},{4,7},{5,4},{6,5},{7,6},{8,11},{9,8},{10,9... | collective-permute-start | bytes 196616 | tf_op jit(solution)/shard_map/ppermute | solution.py:372

commit v3 on v1

--- a/solution.py
+++ b/solution.py
@@ -10,6 +10,8 @@
 
 F32, BF16 = jnp.float32, jnp.bfloat16
 VMEM = pl.BlockSpec(memory_space=pltpu.VMEM)
+ALL_VMEM = 67043328
+HBM = pl.BlockSpec(memory_space=pltpu.HBM)
 
 
 def split(x):
@@ -73,9 +75,17 @@
     return r, i >> log2(p.k), i & (p.k - 1)
 
 
-def restrict_kernel(p, v_ref, t_ref, b_ref, out_ref, g3_ref, up_ref, down_ref, last, first):
+def restrict_kernel(p, v_hbm, t_hbm, b_hbm, out_ref, g3_ref, up_ref, down_ref, v_ref, t_ref, b_ref, last, first, sems):
     n, k, s = p.n, p.k, p.slots
     me = lax.axis_index("xy")
+    t_copy = pltpu.make_async_copy(t_hbm, t_ref, sems.at[0])
+    b_copy = pltpu.make_async_copy(b_hbm, b_ref, sems.at[1])
+    v_copies = [pltpu.make_async_copy(v_hbm.at[c], v_ref.at[c], sems.at[2 + c]) for c in range(3)]
+    t_copy.start()
+    for copy in v_copies:
+        copy.start()
+    b_copy.start()
+    t_copy.wait()
     table = t_ref[...]
     q, q_s = send_positions(p, table)
     lanes = p.cz * s
@@ -92,23 +102,32 @@
         q_s.reshape(1, s, 1) == (r_l * k + j_l).astype(F32).reshape(1, 1, p.rows)
     )
     g3_ref[...] = one_hot(g3).reshape(p.cz * s, p.rows)
+    col = jnp.broadcast_to((table & (p.bcols - 1)).astype(F32), (s, s))
+    qi = iota((s, s), 0).astype(F32)
+    col_q = jnp.sum(jnp.where(qi == jnp.broadcast_to(q, (s, s)), col, 0.0), axis=1, keepdims=True)
+    qa, la = iota((s, p.area), 0), iota((s, p.area), 1)
+    spread = jnp.where((qa & (k - 1)) == (la & (k - 1)), col_q, 0.0).astype(BF16)
+    gather = one_hot((iota((n, s), 1) >> log2(k)) == iota((n, s), 0))
+    cols = dot(gather, spread)
+    at = p.ru + p.rb
+    for r in range(n):
+        out_ref[r, at : at + 1, :] = cols[r : r + 1]
     half_fine = p.edge * p.edge // 2
     half_area = p.area // 2
     f, c = iota((half_fine, half_area), 0), iota((half_fine, half_area), 1)
     e = log2(p.edge)
     coarse = ((f >> (e + 1)) << (e - 1)) + ((f & (p.edge - 1)) >> 1)
     sel = one_hot(coarse == c)
-    z_sum = jnp.concatenate(
-        [v_ref[c, 2 * z] + v_ref[c, 2 * z + 1] for c in range(3) for z in range(p.zc)], axis=0
-    )
-    hi, lo = split(z_sum)
     parts = []
-    for h in range(2):
-        w = slice(h * half_fine, (h + 1) * half_fine)
-        parts.append(dot(hi[:, w], sel) + dot(lo[:, w], sel))
-    u = jnp.concatenate(parts, axis=1) * 0.125
-    hi, lo = split(u)
+    for c in range(3):
+        v_copies[c].wait()
+        z_sum = jnp.concatenate([v_ref[c, 2 * z] + v_ref[c, 2 * z + 1] for z in range(p.zc)], axis=0)
+        hi, lo = split(z_sum)
+        ws = [slice(h * half_fine, (h + 1) * half_fine) for h in range(2)]
+        parts.append(jnp.concatenate([dot(hi[:, w], sel) + dot(lo[:, w], sel) for w in ws], axis=1))
+    hi, lo = split(jnp.concatenate(parts, axis=0) * 0.125)
     out_ref[:, : p.ru, :] = (dot(g, hi) + dot(g, lo)).reshape(n, p.ru, p.area)
+    b_copy.wait()
     for c in range(3):
         for z in range(p.zc):
             for h in range(p.wrap):
@@ -119,18 +138,8 @@
     nxt = lax.rem(me + 1, n)
     for r in range(n):
         out_ref[r, p.ru : p.ru + p.rb, :] = jnp.where(r == nxt, last[: p.rb], first[: p.rb])
-    col = jnp.broadcast_to((table & (p.bcols - 1)).astype(F32), (s, s))
-    qi = iota((s, s), 0).astype(F32)
-    col_q = jnp.sum(jnp.where(qi == jnp.broadcast_to(q, (s, s)), col, 0.0), axis=1, keepdims=True)
-    qa, la = iota((s, p.area), 0), iota((s, p.area), 1)
-    spread = jnp.where((qa & (k - 1)) == (la & (k - 1)), col_q, 0.0).astype(BF16)
-    gather = one_hot((iota((n, s), 1) >> log2(k)) == iota((n, s), 0))
-    cols = dot(gather, spread)
-    at = p.ru + p.rb
-    for r in range(n):
-        out_ref[r, at : at + 1, :] = cols[r : r + 1]
-    up_ref[...] = b_ref[:, p.zc - 1]
-    down_ref[...] = b_ref[:, 0]
+    up_ref[...] = b_ref[0:2, p.zc - 1]
+    down_ref[...] = b_ref[0:2, 0]
 
 
 def tile_transpose(p, t):
@@ -195,7 +204,30 @@
     return jnp.concatenate([ref[src, pl.ds(at + h, 1), :] for h in range(p.wrap)], axis=1)
 
 
-def field_kernel(p, r_ref, b_ref, lo_ref, hi_ref, out_ref, next_ref, up_ref, down_ref, e_rows):
+def interior_kernel(p, b_ref, copy_ref, j_ref, next_ref):
+    zero = jnp.zeros((p.ny, p.nx), F32)
+    for z in range(p.zc):
+        b = [b_ref[c, z] for c in range(3)]
+        below = [b_ref[c, z - 1] if z > 0 else zero for c in range(3)]
+        above = [b_ref[c, z + 1] if z < p.zc - 1 else zero for c in range(3)]
+        south, north = [y_prev(f, 0.0) for f in b], [y_next(f, 0.0) for f in b]
+        west, east = [x_prev(f) for f in b], [x_next(f) for f in b]
+        j_ref[0, z] = ((north[2] - south[2]) - (above[1] - below[1])) * 0.5
+        j_ref[1, z] = ((above[0] - below[0]) - (east[2] - west[2])) * 0.5
+        j_ref[2, z] = ((east[1] - west[1]) - (north[0] - south[0])) * 0.5
+        for c in range(3):
+            lap = below[c] + above[c] + south[c] + north[c] + west[c] + east[c] - 6.0 * b[c]
+            next_ref[c, z] = b[c] + 0.05 * lap
+            copy_ref[c, z] = b[c]
+
+
+def edge_rows(p, ref, nxt, prv, at):
+    y = iota((p.ny, p.nx), 0)
+    north = jnp.where(y == p.ny - 1, row_of(p, ref, nxt, at), 0.0)
+    return north, jnp.where(y == 0, row_of(p, ref, prv, at), 0.0)
+
+
+def field_kernel(p, r_ref, b_ref, j_ref, lo_ref, hi_ref, out_ref, e_ref, up_ref, down_ref, e_rows):
     n, k, zc = p.n, p.k, p.zc
     me = lax.axis_index("xy")
     nxt, prv = lax.rem(me + 1, n), lax.rem(me + n - 1, n)
@@ -227,42 +259,35 @@
     ]
     b = [[b_ref[c, z] for z in range(zc)] for c in range(3)]
     force = []
+    zero = jnp.zeros((p.ny, p.nx), F32)
     for z in range(zc):
         bz = [b[c][z] for c in range(3)]
-        below = [lo_ref[c] if z == 0 else b[c][z - 1] for c in range(3)]
-        above = [hi_ref[c] if z == zc - 1 else b[c][z + 1] for c in range(3)]
-        north, south, east, west = [], [], [], []
-        for c in range(3):
-            at = p.ru + (c * zc + z) * p.wrap
-            south.append(y_prev(bz[c], row_of(p, r_ref, prv, at)))
-            north.append(y_next(bz[c], row_of(p, r_ref, nxt, at)))
-            east.append(x_next(bz[c]))
-            west.append(x_prev(bz[c]))
-        dz = [(above[c] - below[c]) * 0.5 for c in range(2)]
-        j0 = (north[2] - south[2]) * 0.5 - dz[1]
-        j1 = dz[0] - (east[2] - west[2]) * 0.5
-        j2 = (east[1] - west[1]) * 0.5 - (north[0] - south[0]) * 0.5
+        dy = {}
+        for c in (0, 2):
+            north, south = edge_rows(p, r_ref, nxt, prv, p.ru + (c * zc + z) * p.wrap)
+            dy[c] = north - south
+        dz = [zero, zero]
+        for c in range(2):
+            if z == zc - 1:
+                dz[c] = dz[c] + hi_ref[c]
+            if z == 0:
+                dz[c] = dz[c] - lo_ref[c]
+        j0 = j_ref[0, z] + (dy[2] - dz[1]) * 0.5
+        j1 = j_ref[1, z] + dz[0] * 0.5
+        j2 = j_ref[2, z] - dy[0] * 0.5
         force.append([j1 * bz[2] - j2 * bz[1], j2 * bz[0] - j0 * bz[2], j0 * bz[1] - j1 * bz[0]])
-        for c in range(3):
-            lap = above[c] + below[c] + north[c] + south[c] + east[c] + west[c] - 6.0 * bz[c]
-            next_ref[c, z] = bz[c] + 0.05 * lap
     f_blk = jnp.concatenate([grid_to_blocks(p, force[z][c]) for c in range(3) for z in range(zc)], axis=0)
     hi, lo = split(f_blk)
     out_ref[:, : p.ru, :] = (dot(g2t, hi) + dot(g2t, lo)).reshape(n, p.ru, p.area)
-    e = []
     for z in range(zc):
         uz, bz = [u[c][z] for c in range(3)], [b[c][z] for c in range(3)]
-        e.append([uz[1] * bz[2] - uz[2] * bz[1], uz[2] * bz[0] - uz[0] * bz[2], uz[0] * bz[1] - uz[1] * bz[0]])
-    for z in range(zc):
-        ez = e[z]
-        zero = jnp.zeros_like(ez[0])
-        above = e[z + 1] if z < zc - 1 else (zero, zero)
-        below = e[z - 1] if z > 0 else (zero, zero)
-        dy2 = y_next(ez[2], 0.0) - y_prev(ez[2], 0.0)
-        dy0 = y_next(ez[0], 0.0) - y_prev(ez[0], 0.0)
-        next_ref[0, z] += 0.05 * (dy2 - (above[1] - below[1]))
-        next_ref[1, z] += 0.05 * ((above[0] - below[0]) - (x_next(ez[2]) - x_prev(ez[2])))
-        next_ref[2, z] += 0.05 * ((x_next(ez[1]) - x_prev(ez[1])) - dy0)
+        ez = [uz[1] * bz[2] - uz[2] * bz[1], uz[2] * bz[0] - uz[0] * bz[2], uz[0] * bz[1] - uz[1] * bz[0]]
+        for c in range(3):
+            e_ref[c, z] = ez[c]
+        if z == zc - 1:
+            up_ref[0], up_ref[1], up_ref[2] = ez[0], ez[1], bz[2]
+        if z == 0:
+            down_ref[0], down_ref[1], down_ref[2] = ez[0], ez[1], bz[2]
         for i, c in enumerate((0, 2)):
             for h in range(p.wrap):
                 at = (i * zc + z) * p.wrap + h
@@ -271,68 +296,95 @@
                 e_rows[1, at : at + 1, :] = ez[c][p.ny - 1 : p.ny, w]
     for r in range(n):
         out_ref[r, p.ru : p.ru + p.re, :] = jnp.where(r == nxt, e_rows[1], e_rows[0])
-    up_ref[0], up_ref[1] = e[zc - 1][0], e[zc - 1][1]
-    down_ref[0], down_ref[1] = e[0][0], e[0][1]
-
-
-def widen_kernel(p, r_ref, g_ref, v_ref, out_ref):
+
+
+def local_kernel(p, r_ref, b_ref, lo_ref, hi_ref, e_ref, next_ref):
+    n, zc = p.n, p.zc
+    me = lax.axis_index("xy")
+    nxt, prv = lax.rem(me + 1, n), lax.rem(me + n - 1, n)
+    zero = jnp.zeros((p.ny, p.nx), F32)
+    for z in range(zc):
+        e = [e_ref[c, z] for c in range(3)]
+        above = [e_ref[c, z + 1] if z < zc - 1 else zero for c in range(2)]
+        below = [e_ref[c, z - 1] if z > 0 else zero for c in range(2)]
+        curl = [
+            (y_next(e[2], 0.0) - y_prev(e[2], 0.0)) - (above[1] - below[1]),
+            (above[0] - below[0]) - (x_next(e[2]) - x_prev(e[2])),
+            (x_next(e[1]) - x_prev(e[1])) - (y_next(e[0], 0.0) - y_prev(e[0], 0.0)),
+        ]
+        for c in range(3):
+            north, south = edge_rows(p, r_ref, nxt, prv, p.ru + (c * zc + z) * p.wrap)
+            total = curl[c] + north + south
+            if c < 2 and z == 0:
+                total = total + lo_ref[c]
+            if c < 2 and z == zc - 1:
+                total = total + hi_ref[c]
+            next_ref[c, z] = b_ref[c, z] + 0.05 * total
+
+
+def finish_kernel(p, r_ref, g_ref, v_ref, n_ref, lo_ref, hi_ref, vel_hbm, mag_hbm, vel, mag, sems):
+    n, zc = p.n, p.zc
     half_fine = p.edge * p.edge // 2
     half_area = p.area // 2
-    e = log2(p.edge)
+    ex = log2(p.edge)
     c, f = iota((half_area, half_fine), 0), iota((half_area, half_fine), 1)
-    coarse = ((f >> (e + 1)) << (e - 1)) + ((f & (p.edge - 1)) >> 1)
+    coarse = ((f >> (ex + 1)) << (ex - 1)) + ((f & (p.edge - 1)) >> 1)
     sel = one_hot(coarse == c)
     hi, lo = split(r_ref[:, : p.ru, :].reshape(p.rows, p.area) * 0.1)
     g = g_ref[...]
     hi, lo = dot(g, hi).astype(BF16), dot(g, lo).astype(BF16)
     s = p.slots
-    for h in range(2):
-        w = slice(h * half_area, (h + 1) * half_area)
-        wide = dot(hi[:, w], sel) + dot(lo[:, w], sel)
-        fw = slice(h * half_fine, (h + 1) * half_fine)
-        for c in range(3):
-            for z in range(p.zc):
-                add = wide[(c * p.zc + z) * s : (c * p.zc + z + 1) * s]
+    copies = []
+    for c in range(3):
+        for z in range(zc):
+            at = slice((c * zc + z) * s, (c * zc + z + 1) * s)
+            for h in range(2):
+                w = slice(h * half_area, (h + 1) * half_area)
+                fw = slice(h * half_fine, (h + 1) * half_fine)
+                add = dot(hi[at, w], sel) + dot(lo[at, w], sel)
                 for d in range(2):
-                    out_ref[c, 2 * z + d, :, fw] = v_ref[c, 2 * z + d, :, fw] + add
-
-
-def finish_kernel(p, n_ref, r_ref, lo_ref, hi_ref, out_ref):
-    n, zc = p.n, p.zc
+                    vel[c, 2 * z + d, :, fw] = v_ref[c, 2 * z + d, :, fw] + add
+        copies.append(pltpu.make_async_copy(vel.at[c], vel_hbm.at[c], sems.at[c]))
+        copies[-1].start()
     me = lax.axis_index("xy")
     nxt, prv = lax.rem(me + 1, n), lax.rem(me + n - 1, n)
-    y = iota((p.ny, p.nx), 0)
 
     def dy(i, z):
-        at = p.ru + (i * zc + z) * p.wrap
-        north, south = row_of(p, r_ref, nxt, at), row_of(p, r_ref, prv, at)
-        return jnp.where(y == p.ny - 1, north, 0.0) - jnp.where(y == 0, south, 0.0)
+        north, south = edge_rows(p, r_ref, nxt, prv, p.ru + (i * zc + z) * p.wrap)
+        return north - south
 
     for z in range(zc):
-        zero = jnp.zeros((p.ny, p.nx), F32)
-        dz = [zero, zero]
-        for c in range(2):
-            if z == zc - 1:
-                dz[c] = dz[c] + hi_ref[c]
-            if z == 0:
-                dz[c] = dz[c] - lo_ref[c]
-        out_ref[0, z] = n_ref[0, z] + 0.05 * (dy(1, z) - dz[1])
-        out_ref[1, z] = n_ref[1, z] + 0.05 * dz[0]
-        out_ref[2, z] = n_ref[2, z] - 0.05 * dy(0, z)
+        dz = [jnp.zeros((p.ny, p.nx), F32)] * 2
+        outer = dz[0]
+        if z == zc - 1:
+            dz = [dz[c] + hi_ref[c] for c in range(2)]
+            outer = outer + hi_ref[2]
+        if z == 0:
+            dz = [dz[c] - lo_ref[c] for c in range(2)]
+            outer = outer + lo_ref[2]
+        mag[0, z] = n_ref[0, z] + 0.05 * (dy(1, z) - dz[1])
+        mag[1, z] = n_ref[1, z] + 0.05 * dz[0]
+        mag[2, z] = n_ref[2, z] + 0.05 * (outer - dy(0, z))
+    copies.append(pltpu.make_async_copy(mag, mag_hbm, sems.at[3]))
+    copies[-1].start()
+    for copy in copies:
+        copy.wait()
 
 
 def struct(*shape, dtype=F32):
     return jax.ShapeDtypeStruct(shape, dtype)
 
 
-def call(kernel, outs, n_in, name, scratch=()):
+def call(kernel, ins, outs, name, scratch=(), grant=20 << 20):
     return pl.pallas_call(
         kernel,
-        out_shape=outs,
-        in_specs=[VMEM] * n_in,
-        out_specs=jax.tree.map(lambda _: VMEM, outs),
+        out_shape=[o for o, _ in outs],
+        in_specs=ins,
+        out_specs=[spec for _, spec in outs],
         scratch_shapes=list(scratch),
         name=name,
+        cost_estimate=pl.CostEstimate(flops=1 << 24, bytes_accessed=1 << 20, transcendentals=0),
+        compiler_params=pltpu.CompilerParams(vmem_limit_bytes=grant),
     )
 
 
@@ -344,36 +396,61 @@
 def body(velocity, magnetic, slot_block_table):
     p = Plan(velocity.shape, magnetic.shape, lax.axis_size("xy"))
     plane = (p.ny, p.nx)
+    dma = pltpu.SemaphoreType.DMA
     sent, g3, up, down = call(
         functools.partial(restrict_kernel, p),
-        (
-            struct(p.n, p.r1, p.area),
-            struct(p.cz * p.slots, p.rows, dtype=BF16),
-            struct(3, *plane),
-            struct(3, *plane),
-        ),
-        3,
+        [HBM] * 3,
+        [
+            (struct(p.n, p.r1, p.area), VMEM),
+            (struct(p.cz * p.slots, p.rows, dtype=BF16), VMEM),
+            (struct(2, *plane), VMEM),
+            (struct(2, *plane), VMEM),
+        ],
         "restrict",
-        [pltpu.VMEM((-(-p.rb // 8) * 8, p.area), F32)] * 2,
+        [
+            pltpu.VMEM(velocity.shape, F32),
+            pltpu.VMEM((1, p.slots), jnp.int32),
+            pltpu.VMEM(magnetic.shape, F32),
+            pltpu.VMEM((-(-p.rb // 8) * 8, p.area), F32),
+            pltpu.VMEM((-(-p.rb // 8) * 8, p.area), F32),
+            dma((5,)),
+        ],
+        ALL_VMEM,
     )(velocity, slot_block_table.reshape(1, p.slots), magnetic)
     got = lax.all_to_all(sent, "xy", 0, 0, tiled=True)
     below = lax.ppermute(up, "gz", ring("gz", 1))
     above = lax.ppermute(down, "gz", ring("gz", -1))
-    sent, partial, up, down = call(
+    held, _ = lax.optimization_barrier((magnetic, up))
+    field, current, diffused = call(
+        functools.partial(interior_kernel, p), [VMEM], [(struct(*magnetic.shape), VMEM)] * 3, "interior"
+    )(held)
+    sent, emf, up, down = call(
         functools.partial(field_kernel, p),
-        (struct(p.n, p.r2, p.area), struct(*magnetic.shape), struct(2, *plane), struct(2, *plane)),
-        4,
+        [VMEM] * 5,
+        [
+            (struct(p.n, p.r2, p.area), VMEM),
+            (struct(*magnetic.shape), VMEM),
+            (struct(3, *plane), VMEM),
+            (struct(3, *plane), VMEM),
+        ],
         "field",
         [pltpu.VMEM((2, p.re, p.area), F32)],
-    )(got, magnetic, below, above)
-    got = lax.all_to_all(sent, "xy", 0, 0, tiled=True)
-    below = lax.ppermute(up, "gz", ring("gz", 1))
-    above = lax.ppermute(down, "gz", ring("gz", -1))
-    updated = call(functools.partial(widen_kernel, p), struct(*velocity.shape), 3, "widen")(got, g3, velocity)
-    finished = call(functools.partial(finish_kernel, p), struct(*magnetic.shape), 4, "finish")(
-        partial, got, below, above
+    )(got, field, current, below, above)
+    got_force = lax.all_to_all(sent, "xy", 0, 0, tiled=True)
+    emf_below = lax.ppermute(up, "gz", ring("gz", 1))
+    emf_above = lax.ppermute(down, "gz", ring("gz", -1))
+    (partial,) = call(
+        functools.partial(local_kernel, p), [VMEM] * 5, [(struct(*magnetic.shape), VMEM)], "local"
+    )(got, diffused, below, above, emf)
+    return tuple(
+        call(
+            functools.partial(finish_kernel, p),
+            [VMEM] * 6,
+            [(struct(*velocity.shape), HBM), (struct(*magnetic.shape), HBM)],
+            "finish",
+            [pltpu.VMEM(velocity.shape, F32), pltpu.VMEM(magnetic.shape, F32), dma((4,))],
+        )(got_force, g3, velocity, partial, emf_below, emf_above)
     )
-    return updated, finished
 
 
 def solution(mesh):

time: 39.1 us -> 33.9 us (0.87)
  Pallas kernels: 10.6 us -> 6.25 us
  local copies, waits for them, and re-layouts: 2.68 us -> 0.94 us
  waiting for transfers between devices: 8.08 us -> 8.64 us
    pallas_call x4 -> x5, Pallas kernels: 10.6 us -> 6.25 us  [the longest x1 2.77 us: body(): call(functools.partial(restrict_kernel, p), [HBM] * 3, [(struct(p.n, p.r1...]
    all_to_all x0 -> x1, starting transfers between devices: none -> 4.2 us  [body(): got_force = lax.all_to_all(sent, 'xy', 0, 0, tiled=True)]
    ppermute x0 -> x2, starting transfers between devices: none -> 3.82 us  [the longest x1 3.82 us: body(): emf_above = lax.ppermute(down, 'gz', ring('gz', -1))]
    all_to_all x2 -> x1, starting transfers between devices: 9.01 us -> 5.34 us  [body(): got = lax.all_to_all(sent, 'xy', 0, 0, tiled=True)]
    ppermute x0 -> x2, waiting for transfers between devices: none -> 3.49 us  [the longest x1 3.49 us: body(): emf_below = lax.ppermute(up, 'gz', ring('gz', 1))]
    all_to_all x2 -> x1, waiting for transfers between devices: 3.08 us -> 0.01 us  [body(): got = lax.all_to_all(sent, 'xy', 0, 0, tiled=True)]
    ppermute x2 -> x1, starting transfers between devices: 2.7 us -> 0.01 us  [body(): below = lax.ppermute(up, 'gz', ring('gz', 1))]
    unnamed x12 -> x6, local copies, waits for them, and re-layouts: 2.68 us -> 0.94 us
  transfers between devices with their start and end apart: 6 -> 6, of which waited for: 3 -> 3; matrix products, arithmetic and copies ran while one was open for 0% -> 0% of each run, Pallas kernels for 8% -> 1%
where the time goes in v3:
time: 33.9 us; the launch traced here: 33.5 us
  starting transfers between devices  17 us (50%)
  waiting for transfers between devices  8.64 us (25%)
  Pallas kernels  6.25 us (18%)
  local copies, waits for them, and re-layouts  0.94 us (3%)
  between operations  0.69 us (2%)
    all_to_all x1, starting transfers between devices, body(): got = lax.all_to_all(sent, 'xy', 0, 0, tiled=True)  5.34 us
    all_to_all x1, starting transfers between devices, body(): got_force = lax.all_to_all(sent, 'xy', 0, 0, tiled=True)  4.2 us
    ppermute x1, starting transfers between devices, body(): emf_above = lax.ppermute(down, 'gz', ring('gz', -1))  3.82 us
    ppermute x1, starting transfers between devices, body(): above = lax.ppermute(down, 'gz', ring('gz', -1))  3.6 us
    ppermute x1, waiting for transfers between devices, body(): emf_below = lax.ppermute(up, 'gz', ring('gz', 1))  3.49 us
    ppermute x1, waiting for transfers between devices, body(): below = lax.ppermute(up, 'gz', ring('gz', 1))  3.48 us
    pallas_call x1, Pallas kernels, body(): call(functools.partial(restrict_kernel, p), [HBM] * 3, [(struct(p.n, p.r1...  2.77 us
    ppermute x1, waiting for transfers between devices, body(): above = lax.ppermute(down, 'gz', ring('gz', -1))  1.67 us
  transfers between devices with their start and end apart: 6, of which 3 were waited for; matrix products, arithmetic and copies ran while one was open for 0% of the time, Pallas kernels for 1%

profile of v3, /device:TPU:0, one launch (start us, length us, event | category | flops | bytes accessed | tf_op | source)
XLA Modules:
  0.0 33.5 jit_solution(17623120639269192810)
XLA Ops:
  0.6 2.8 %restrict.1 = (f32[8,40,256]{2,1,0:T(8,128)}, bf16[192,192]{1,0:T(8,128)(2,1)}, f32[2,16,512]{2,1,0:T(8,128)}, f32[2,16,512]{2,1,0:T(8,128)}) custom-call(f32[3,4,32,1024]{3,2,1,0:T(8,128)} %v_ref.1, s32[1,32]{1,0:T(1,128)} %bitcast.1, f32[3,2,16,512]{3,2,1,0:T(8,128)} %b_ref), custom_call_target="tpu_custom_call" | custom-call | flops 16777216 | bytes 1048576 | tf_op jit(solution)/shard_map/restrict/pallas_call | solution.py:400
  3.4 0.0 copy-start
  3.4 5.3 %all-to-all-start = ((f32[8,40,256]{2,1,0:T(8,128)}), f32[8,40,256]{2,1,0:T(8,128)S(1)}, u32[]{:S(2)}, u32[]{:S(2)}) async-start(f32[8,40,256]{2,1,0:T(8,128)} %get-tuple-element.14), calls=%async_computation | async-start | bytes 655360 | tf_op jit(solution)/shard_map/all_to_all | solution.py:420
  8.8 3.6 %collective-permute-start.1 = (f32[2,16,512]{2,1,0:T(8,128)}, f32[2,16,512]{2,1,0:T(8,128)S(1)}, u32[]{:S(2)}, u32[]{:S(2)}) collective-permute-start(f32[2,16,512]{2,1,0:T(8,128)} %get-tuple-element.19), channel_id=1, source_target_pairs={{0,3},{1,0},{2,1},{3,2},{4,7},{5,4},{6,5},{7,6},{8,11},{9,8},{10,9... | collective-permute-start | bytes 196616 | tf_op jit(solution)/shard_map/ppermute | solution.py:422
  12.4 0.0 collective-permute-start
  12.4 0.0 copy-start.1
  12.4 0.9 %copy-done.1 = f32[3,2,16,512]{3,2,1,0:T(8,128)S(1)} copy-done((f32[3,2,16,512]{3,2,1,0:T(8,128)S(1)}, f32[3,2,16,512]{3,2,1,0:T(8,128)}, u32[]{:S(2)}) %copy-start.1) | copy-done | bytes 196632
  13.3 0.0 copy-start.2
  13.3 0.2 interior.1
  13.5 1.7 %collective-permute-done.1.hi_ref = f32[2,16,512]{2,1,0:T(8,128)S(1)} collective-permute-done((f32[2,16,512]{2,1,0:T(8,128)}, f32[2,16,512]{2,1,0:T(8,128)S(1)}, u32[]{:S(2)}, u32[]{:S(2)}) %collective-permute-start.1) | collective-permute-done | bytes 65568 | tf_op jit(solution)/shard_map/ppermute | solution.py:422
  15.2 3.5 %collective-permute-done.lo_ref = f32[2,16,512]{2,1,0:T(8,128)S(1)} collective-permute-done((f32[2,16,512]{2,1,0:T(8,128)}, f32[2,16,512]{2,1,0:T(8,128)S(1)}, u32[]{:S(2)}, u32[]{:S(2)}) %collective-permute-start) | collective-permute-done | bytes 65568 | tf_op jit(solution)/shard_map/ppermute | solution.py:421
  18.6 0.0 all-to-all-done.r_ref
  18.6 1.5 %field.1 = (f32[8,32,256]{2,1,0:T(8,128)}, f32[3,2,16,512]{3,2,1,0:T(8,128)S(1)}, f32[3,16,512]{2,1,0:T(8,128)S(1)}, f32[3,16,512]{2,1,0:T(8,128)S(1)}) custom-call(f32[8,40,256]{2,1,0:T(8,128)S(1)} %all-to-all-done.r_ref, f32[3,2,16,512]{3,2,1,0:T(8,128)S(1)} %get-tuple-element.17.b_ref, f32[3,2,16,512]{3,2,1,0:T(8,128)S(1)} %get-tuple-element.18.j_ref, ...), custom_call_target="tpu_custom_call" | custom-call | flops 16777216 | bytes 1048576 | tf_op jit(solution)/shard_map/field/pallas_call | solution.py:427
  20.2 4.2 %all-to-all-start.1 = ((f32[8,32,256]{2,1,0:T(8,128)}), f32[8,32,256]{2,1,0:T(8,128)S(1)}, u32[]{:S(2)}, u32[]{:S(2)}) async-start(f32[8,32,256]{2,1,0:T(8,128)} %get-tuple-element.20), calls=%async_computation.1 | async-start | bytes 524288 | tf_op jit(solution)/shard_map/all_to_all | solution.py:439
  24.4 0.0 collective-permute-start.2
  24.4 3.8 %collective-permute-start.3 = (f32[3,16,512]{2,1,0:T(8,128)S(1)}, f32[3,16,512]{2,1,0:T(8,128)S(1)}, u32[]{:S(2)}, u32[]{:S(2)}) collective-permute-start(f32[3,16,512]{2,1,0:T(8,128)S(1)} %get-tuple-element.25), channel_id=1, source_target_pairs={{0,3},{1,0},{2,1},{3,2},{4,7},{5,4},{6,5},{7,6},{8,11},{9,8},{10,9... | collective-permute-start | bytes 294920 | tf_op jit(solution)/shard_map/ppermute | solution.py:441
  28.2 0.1 local.1.n_ref
  28.3 3.5 %collective-permute-done.2.lo_ref = f32[3,16,512]{2,1,0:T(8,128)S(1)} collective-permute-done((f32[3,16,512]{2,1,0:T(8,128)S(1)}, f32[3,16,512]{2,1,0:T(8,128)S(1)}, u32[]{:S(2)}, u32[]{:S(2)}) %collective-permute-start.2) | collective-permute-done | bytes 98336 | tf_op jit(solution)/shard_map/ppermute | solution.py:440
  31.8 0.0 collective-permute-done.3.hi_ref
  31.8 0.0 all-to-all-done.1.r_ref
  31.8 0.0 copy-done
  31.8 0.0 copy-done.2
  31.8 1.6 %finish.1 = (f32[3,4,32,1024]{3,2,1,0:T(8,128)}, f32[3,2,16,512]{3,2,1,0:T(8,128)}) custom-call(f32[8,32,256]{2,1,0:T(8,128)S(1)} %all-to-all-done.1.r_ref, bf16[192,192]{1,0:T(8,128)(2,1)S(1)} %copy-done.2, f32[3,4,32,1024]{3,2,1,0:T(8,128)S(1)} %copy-done, f32[3,2,16,512]{3,2,1,0:T(8,128)S(1)} %local.1.n_ref, ...), custom_call_target="tpu_custom_call" | custom-call | flops 16777216 | bytes 1048576 | tf_op jit(solution)/shard_map/finish/pallas_call | solution.py:446
Async XLA Ops:
  3.4 28.4 %copy-start = (f32[3,4,32,1024]{3,2,1,0:T(8,128)S(1)}, f32[3,4,32,1024]{3,2,1,0:T(8,128)}, u32[]{:S(2)}) copy-start(f32[3,4,32,1024]{3,2,1,0:T(8,128)} %v_ref.1) | copy-start | bytes 4718596
  3.4 15.2 %all-to-all-start = ((f32[8,40,256]{2,1,0:T(8,128)}), f32[8,40,256]{2,1,0:T(8,128)S(1)}, u32[]{:S(2)}, u32[]{:S(2)}) async-start(f32[8,40,256]{2,1,0:T(8,128)} %get-tuple-element.14), calls=%async_computation | async-start | bytes 655360 | tf_op jit(solution)/shard_map/all_to_all | solution.py:420
  8.8 6.4 %collective-permute-start.1 = (f32[2,16,512]{2,1,0:T(8,128)}, f32[2,16,512]{2,1,0:T(8,128)S(1)}, u32[]{:S(2)}, u32[]{:S(2)}) collective-permute-start(f32[2,16,512]{2,1,0:T(8,128)} %get-tuple-element.19), channel_id=1, source_target_pairs={{0,3},{1,0},{2,1},{3,2},{4,7},{5,4},{6,5},{7,6},{8,11},{9,8},{10,9... | collective-permute-start | bytes 196616 | tf_op jit(solution)/shard_map/ppermute | solution.py:422
  12.4 6.3 %collective-permute-start = (f32[2,16,512]{2,1,0:T(8,128)}, f32[2,16,512]{2,1,0:T(8,128)S(1)}, u32[]{:S(2)}, u32[]{:S(2)}) collective-permute-start(f32[2,16,512]{2,1,0:T(8,128)} %get-tuple-element.15), channel_id=1, source_target_pairs={{0,1},{1,2},{2,3},{3,0},{4,5},{5,6},{6,7},{7,4},{8,9},{9,10},{10,1... | collective-permute-start | bytes 196616 | tf_op jit(solution)/shard_map/ppermute | solution.py:421
  12.4 0.9 %copy-start.1 = (f32[3,2,16,512]{3,2,1,0:T(8,128)S(1)}, f32[3,2,16,512]{3,2,1,0:T(8,128)}, u32[]{:S(2)}) copy-start(f32[3,2,16,512]{3,2,1,0:T(8,128)} %b_ref) | copy-start | bytes 589828
  13.3 18.5 %copy-start.2 = (bf16[192,192]{1,0:T(8,128)(2,1)S(1)}, bf16[192,192]{1,0:T(8,128)(2,1)}, u32[]{:S(2)}) copy-start(bf16[192,192]{1,0:T(8,128)(2,1)} %get-tuple-element.21.g_ref) | copy-start | bytes 221188
  20.2 11.7 %all-to-all-start.1 = ((f32[8,32,256]{2,1,0:T(8,128)}), f32[8,32,256]{2,1,0:T(8,128)S(1)}, u32[]{:S(2)}, u32[]{:S(2)}) async-start(f32[8,32,256]{2,1,0:T(8,128)} %get-tuple-element.20), calls=%async_computation.1 | async-start | bytes 524288 | tf_op jit(solution)/shard_map/all_to_all | solution.py:439
  24.4 7.5 %collective-permute-start.2 = (f32[3,16,512]{2,1,0:T(8,128)S(1)}, f32[3,16,512]{2,1,0:T(8,128)S(1)}, u32[]{:S(2)}, u32[]{:S(2)}) collective-permute-start(f32[3,16,512]{2,1,0:T(8,128)S(1)} %get-tuple-element.24), channel_id=1, source_target_pairs={{0,1},{1,2},{2,3},{3,0},{4,5},{5,6},{6,7},{7,4},{8,9},{9,10},{10,1... | collective-permute-start | bytes 294920 | tf_op jit(solution)/shard_map/ppermute | solution.py:440
  24.4 7.5 %collective-permute-start.3 = (f32[3,16,512]{2,1,0:T(8,128)S(1)}, f32[3,16,512]{2,1,0:T(8,128)S(1)}, u32[]{:S(2)}, u32[]{:S(2)}) collective-permute-start(f32[3,16,512]{2,1,0:T(8,128)S(1)} %get-tuple-element.25), channel_id=1, source_target_pairs={{0,3},{1,0},{2,1},{3,2},{4,7},{5,4},{6,5},{7,6},{8,11},{9,8},{10,9... | collective-permute-start | bytes 294920 | tf_op jit(solution)/shard_map/ppermute | solution.py:441

commit v4 on v3

--- a/solution.py
+++ b/solution.py
@@ -75,7 +75,7 @@
     return r, i >> log2(p.k), i & (p.k - 1)
 
 
-def restrict_kernel(p, v_hbm, t_hbm, b_hbm, out_ref, g3_ref, up_ref, down_ref, v_ref, t_ref, b_ref, last, first, sems):
+def restrict_kernel(p, v_hbm, t_hbm, b_hbm, out_ref, up_ref, down_ref, v_ref, t_ref, b_ref, last, first, sems):
     n, k, s = p.n, p.k, p.slots
     me = lax.axis_index("xy")
     t_copy = pltpu.make_async_copy(t_hbm, t_ref, sems.at[0])
@@ -87,7 +87,7 @@
     b_copy.start()
     t_copy.wait()
     table = t_ref[...]
-    q, q_s = send_positions(p, table)
+    q, _ = send_positions(p, table)
     lanes = p.cz * s
     rep = one_hot((iota((s, lanes), 1) & (s - 1)) == iota((s, lanes), 0))
     qt = dot(jnp.broadcast_to(q, (8, s)).astype(BF16), rep)[0:1]
@@ -96,12 +96,6 @@
     target = (iota(shape, 0) * k + (i & (k - 1))).astype(F32)
     g = one_hot(((i >> log2(k)) == (iota(shape, 2) >> log2(s))) & (target == qt.reshape(1, 1, lanes)))
     g = g.reshape(p.rows, lanes)
-    r_l, c_l, j_l = lane_route(p)
-    shape = (p.cz, s, p.rows)
-    g3 = (iota(shape, 0) == c_l.reshape(1, 1, p.rows)) & (
-        q_s.reshape(1, s, 1) == (r_l * k + j_l).astype(F32).reshape(1, 1, p.rows)
-    )
-    g3_ref[...] = one_hot(g3).reshape(p.cz * s, p.rows)
     col = jnp.broadcast_to((table & (p.bcols - 1)).astype(F32), (s, s))
     qi = iota((s, s), 0).astype(F32)
     col_q = jnp.sum(jnp.where(qi == jnp.broadcast_to(q, (s, s)), col, 0.0), axis=1, keepdims=True)
@@ -123,8 +117,11 @@
         v_copies[c].wait()
         z_sum = jnp.concatenate([v_ref[c, 2 * z] + v_ref[c, 2 * z + 1] for z in range(p.zc)], axis=0)
         hi, lo = split(z_sum)
+        m = p.zc * s
         ws = [slice(h * half_fine, (h + 1) * half_fine) for h in range(2)]
-        parts.append(jnp.concatenate([dot(hi[:, w], sel) + dot(lo[:, w], sel) for w in ws], axis=1))
+        out = dot(jnp.concatenate([x[:, w] for w in ws for x in (hi, lo)], axis=0), sel)
+        halves = [out[2 * h * m : (2 * h + 1) * m] + out[(2 * h + 1) * m : (2 * h + 2) * m] for h in range(2)]
+        parts.append(jnp.concatenate(halves, axis=1))
     hi, lo = split(jnp.concatenate(parts, axis=0) * 0.125)
     out_ref[:, : p.ru, :] = (dot(g, hi) + dot(g, lo)).reshape(n, p.ru, p.area)
     b_copy.wait()
@@ -204,7 +201,15 @@
     return jnp.concatenate([ref[src, pl.ds(at + h, 1), :] for h in range(p.wrap)], axis=1)
 
 
-def interior_kernel(p, b_ref, copy_ref, j_ref, next_ref):
+def interior_kernel(p, b_ref, t_ref, copy_ref, j_ref, next_ref, g3_ref):
+    s, k = p.slots, p.k
+    _, q_s = send_positions(p, t_ref[...])
+    r_l, c_l, j_l = lane_route(p)
+    shape = (p.cz, s, p.rows)
+    g3 = (iota(shape, 0) == c_l.reshape(1, 1, p.rows)) & (
+        q_s.reshape(1, s, 1) == (r_l * k + j_l).astype(F32).reshape(1, 1, p.rows)
+    )
+    g3_ref[...] = one_hot(g3).reshape(p.cz * s, p.rows)
     zero = jnp.zeros((p.ny, p.nx), F32)
     for z in range(p.zc):
         b = [b_ref[c, z] for c in range(3)]
@@ -332,18 +337,22 @@
     sel = one_hot(coarse == c)
     hi, lo = split(r_ref[:, : p.ru, :].reshape(p.rows, p.area) * 0.1)
     g = g_ref[...]
+    sel = jnp.concatenate([sel, sel], axis=0)
     hi, lo = dot(g, hi).astype(BF16), dot(g, lo).astype(BF16)
+    ws = [slice(h * half_area, (h + 1) * half_area) for h in range(2)]
+    pairs = [jnp.concatenate([hi[:, w], lo[:, w]], axis=1) for w in ws]
     s = p.slots
+    m = zc * s
     copies = []
     for c in range(3):
+        at = slice(c * m, (c + 1) * m)
+        add = dot(jnp.concatenate([x[at] for x in pairs], axis=0), sel)
         for z in range(zc):
-            at = slice((c * zc + z) * s, (c * zc + z + 1) * s)
             for h in range(2):
-                w = slice(h * half_area, (h + 1) * half_area)
                 fw = slice(h * half_fine, (h + 1) * half_fine)
-                add = dot(hi[at, w], sel) + dot(lo[at, w], sel)
+                part = add[h * m + z * s : h * m + (z + 1) * s]
                 for d in range(2):
-                    vel[c, 2 * z + d, :, fw] = v_ref[c, 2 * z + d, :, fw] + add
+                    vel[c, 2 * z + d, :, fw] = v_ref[c, 2 * z + d, :, fw] + part
         copies.append(pltpu.make_async_copy(vel.at[c], vel_hbm.at[c], sems.at[c]))
         copies[-1].start()
     me = lax.axis_index("xy")
@@ -375,14 +384,13 @@
     return jax.ShapeDtypeStruct(shape, dtype)
 
 
-def call(kernel, ins, outs, name, scratch=(), grant=20 << 20):
+def call(kernel, ins, outs, scratch=(), grant=20 << 20):
     return pl.pallas_call(
         kernel,
         out_shape=[o for o, _ in outs],
         in_specs=ins,
         out_specs=[spec for _, spec in outs],
         scratch_shapes=list(scratch),
-        name=name,
         cost_estimate=pl.CostEstimate(flops=1 << 24, bytes_accessed=1 << 20, transcendentals=0),
         compiler_params=pltpu.CompilerParams(vmem_limit_bytes=grant),
     )
@@ -391,22 +399,27 @@
 def ring(axis, step):
     n = lax.axis_size(axis)
     return [(i, (i + step) % n) for i in range(n)]
+
+
+def planes(up, down):
+    below = lax.ppermute(up, "gz", ring("gz", 1))
+    above = lax.ppermute(down, "gz", ring("gz", -1))
+    return below, above
 
 
 def body(velocity, magnetic, slot_block_table):
     p = Plan(velocity.shape, magnetic.shape, lax.axis_size("xy"))
     plane = (p.ny, p.nx)
     dma = pltpu.SemaphoreType.DMA
-    sent, g3, up, down = call(
+    table = slot_block_table.reshape(1, p.slots)
+    sent, up, down = call(
         functools.partial(restrict_kernel, p),
         [HBM] * 3,
         [
             (struct(p.n, p.r1, p.area), VMEM),
-            (struct(p.cz * p.slots, p.rows, dtype=BF16), VMEM),
             (struct(2, *plane), VMEM),
             (struct(2, *plane), VMEM),
         ],
-        "restrict",
         [
             pltpu.VMEM(velocity.shape, F32),
             pltpu.VMEM((1, p.slots), jnp.int32),
@@ -416,14 +429,15 @@
             dma((5,)),
         ],
         ALL_VMEM,
-    )(velocity, slot_block_table.reshape(1, p.slots), magnetic)
+    )(velocity, table, magnetic)
     got = lax.all_to_all(sent, "xy", 0, 0, tiled=True)
-    below = lax.ppermute(up, "gz", ring("gz", 1))
-    above = lax.ppermute(down, "gz", ring("gz", -1))
-    held, _ = lax.optimization_barrier((magnetic, up))
-    field, current, diffused = call(
-        functools.partial(interior_kernel, p), [VMEM], [(struct(*magnetic.shape), VMEM)] * 3, "interior"
-    )(held)
+    below, above = planes(up, down)
+    held, held_table, _ = lax.optimization_barrier((magnetic, table, up))
+    field, current, diffused, g3 = call(
+        functools.partial(interior_kernel, p),
+        [VMEM] * 2,
+        [(struct(*magnetic.shape), VMEM)] * 3 + [(struct(p.cz * p.slots, p.rows, dtype=BF16), VMEM)],
+    )(held, held_table)
     sent, emf, up, down = call(
         functools.partial(field_kernel, p),
         [VMEM] * 5,
@@ -433,21 +447,18 @@
             (struct(3, *plane), VMEM),
             (struct(3, *plane), VMEM),
         ],
-        "field",
         [pltpu.VMEM((2, p.re, p.area), F32)],
     )(got, field, current, below, above)
     got_force = lax.all_to_all(sent, "xy", 0, 0, tiled=True)
-    emf_below = lax.ppermute(up, "gz", ring("gz", 1))
-    emf_above = lax.ppermute(down, "gz", ring("gz", -1))
+    emf_below, emf_above = planes(up, down)
     (partial,) = call(
-        functools.partial(local_kernel, p), [VMEM] * 5, [(struct(*magnetic.shape), VMEM)], "local"
+        functools.partial(local_kernel, p), [VMEM] * 5, [(struct(*magnetic.shape), VMEM)]
     )(got, diffused, below, above, emf)
     return tuple(
         call(
             functools.partial(finish_kernel, p),
             [VMEM] * 6,
             [(struct(*velocity.shape), HBM), (struct(*magnetic.shape), HBM)],
-            "finish",
             [pltpu.VMEM(velocity.shape, F32), pltpu.VMEM(magnetic.shape, F32), dma((4,))],
         )(got_force, g3, velocity, partial, emf_below, emf_above)
     )

time: 33.9 us -> 33.8 us (level)
  waiting for transfers between devices: 8.64 us -> 7.95 us
  local copies, waits for them, and re-layouts: 0.94 us -> 1.59 us
    ppermute x4, waiting for transfers between devices: 8.64 us -> 7.94 us  [the longest x2 6.97 us: planes(): below = lax.ppermute(up, 'gz', ring('gz', 1))]
    unnamed x6, local copies, waits for them, and re-layouts: 0.94 us -> 1.59 us
where the time goes in v4:
time: 33.8 us; the launch traced here: 33.4 us
  starting transfers between devices  17 us (50%)
  waiting for transfers between devices  7.95 us (24%)
  Pallas kernels  6.23 us (18%)
  local copies, waits for them, and re-layouts  1.59 us (5%)
  between operations  0.68 us (2%)
    ppermute x2, starting transfers between devices, planes(): above = lax.ppermute(down, 'gz', ring('gz', -1))  7.41 us
    ppermute x2, waiting for transfers between devices, planes(): below = lax.ppermute(up, 'gz', ring('gz', 1))  6.97 us
    all_to_all x1, starting transfers between devices, body(): got = lax.all_to_all(sent, 'xy', 0, 0, tiled=True)  5.35 us
    all_to_all x1, starting transfers between devices, body(): got_force = lax.all_to_all(sent, 'xy', 0, 0, tiled=True)  4.2 us
    pallas_call x1, Pallas kernels, body(): call(functools.partial(restrict_kernel, p), [HBM] * 3, [(struct(p.n, p.r1...  2.8 us
    unnamed x6, local copies, waits for them, and re-layouts  1.59 us
    pallas_call x1, Pallas kernels, body(): call(functools.partial(finish_kernel, p), [VMEM] * 6, [(struct(*velocity....  1.55 us
    pallas_call x1, Pallas kernels, body(): call(functools.partial(field_kernel, p), [VMEM] * 5, [(struct(p.n, p.r2,...  1.51 us
  transfers between devices with their start and end apart: 6, of which 3 were waited for; matrix products, arithmetic and copies ran while one was open for 0% of the time, Pallas kernels for 1%

profile of v4, /device:TPU:0, one launch (start us, length us, event | category | flops | bytes accessed | tf_op | source)
XLA Modules:
  0.0 33.4 jit_solution(4679300910839984005)
XLA Ops:
  0.6 2.8 %shard_map.50 = (f32[8,40,256]{2,1,0:T(8,128)}, f32[2,16,512]{2,1,0:T(8,128)}, f32[2,16,512]{2,1,0:T(8,128)}) custom-call(f32[3,4,32,1024]{3,2,1,0:T(8,128)} %v_ref.1, s32[1,32]{1,0:T(1,128)} %bitcast.1, f32[3,2,16,512]{3,2,1,0:T(8,128)} %b_ref), custom_call_target="tpu_custom_call" | custom-call | flops 16777216 | bytes 1048576 | tf_op jit(solution)/shard_map/pallas_call | solution.py:415
  3.4 0.0 copy-start
  3.5 5.3 %all-to-all-start = ((f32[8,40,256]{2,1,0:T(8,128)}), f32[8,40,256]{2,1,0:T(8,128)S(1)}, u32[]{:S(2)}, u32[]{:S(2)}) async-start(f32[8,40,256]{2,1,0:T(8,128)} %get-tuple-element.15), calls=%async_computation | async-start | bytes 655360 | tf_op jit(solution)/shard_map/all_to_all | solution.py:433
  8.8 3.6 %collective-permute-start.1 = (f32[2,16,512]{2,1,0:T(8,128)}, f32[2,16,512]{2,1,0:T(8,128)S(1)}, u32[]{:S(2)}, u32[]{:S(2)}) collective-permute-start(f32[2,16,512]{2,1,0:T(8,128)} %get-tuple-element.21), channel_id=1, source_target_pairs={{0,3},{1,0},{2,1},{3,2},{4,7},{5,4},{6,5},{7,6},{8,11},{9,8},{10,9... | collective-permute-start | bytes 196616 | tf_op jit(solution)/shard_map/ppermute | solution.py:406
  12.4 0.0 collective-permute-start
  12.4 0.0 copy-start.1
  12.4 0.9 %copy-done.1 = f32[3,2,16,512]{3,2,1,0:T(8,128)S(1)} copy-done((f32[3,2,16,512]{3,2,1,0:T(8,128)S(1)}, f32[3,2,16,512]{3,2,1,0:T(8,128)}, u32[]{:S(2)}) %copy-start.1) | copy-done | bytes 196632
  13.3 0.0 copy-start.2
  13.3 0.7 %copy-done.2 = s32[32]{0:T(128)S(1)} copy-done((s32[32]{0:T(128)S(1)}, s32[32]{0:T(128)}, u32[]{:S(2)}) %copy-start.2) | copy-done | bytes 152
  14.0 0.2 shard_map.51
  14.2 1.0 %collective-permute-done.1.hi_ref = f32[2,16,512]{2,1,0:T(8,128)S(1)} collective-permute-done((f32[2,16,512]{2,1,0:T(8,128)}, f32[2,16,512]{2,1,0:T(8,128)S(1)}, u32[]{:S(2)}, u32[]{:S(2)}) %collective-permute-start.1) | collective-permute-done | bytes 65568 | tf_op jit(solution)/shard_map/ppermute | solution.py:406
  15.2 3.5 %collective-permute-done.lo_ref = f32[2,16,512]{2,1,0:T(8,128)S(1)} collective-permute-done((f32[2,16,512]{2,1,0:T(8,128)}, f32[2,16,512]{2,1,0:T(8,128)S(1)}, u32[]{:S(2)}, u32[]{:S(2)}) %collective-permute-start) | collective-permute-done | bytes 65568 | tf_op jit(solution)/shard_map/ppermute | solution.py:405
  18.7 0.0 all-to-all-done.r_ref
  18.7 1.5 %shard_map.52 = (f32[8,32,256]{2,1,0:T(8,128)}, f32[3,2,16,512]{3,2,1,0:T(8,128)S(1)}, f32[3,16,512]{2,1,0:T(8,128)S(1)}, f32[3,16,512]{2,1,0:T(8,128)S(1)}) custom-call(f32[8,40,256]{2,1,0:T(8,128)S(1)} %all-to-all-done.r_ref, f32[3,2,16,512]{3,2,1,0:T(8,128)S(1)} %get-tuple-element.19.b_ref, f32[3,2,16,512]{3,2,1,0:T(8,128)S(1)} %get-tuple-element.20.j_ref, ...), custom_call_target="tpu_custom_call" | custom-call | flops 16777216 | bytes 1048576 | tf_op jit(solution)/shard_map/pallas_call | solution.py:441
  20.2 4.2 %all-to-all-start.1 = ((f32[8,32,256]{2,1,0:T(8,128)}), f32[8,32,256]{2,1,0:T(8,128)S(1)}, u32[]{:S(2)}, u32[]{:S(2)}) async-start(f32[8,32,256]{2,1,0:T(8,128)} %get-tuple-element.22), calls=%async_computation.1 | async-start | bytes 524288 | tf_op jit(solution)/shard_map/all_to_all | solution.py:452
  24.4 0.0 collective-permute-start.2
  24.4 3.8 %collective-permute-start.3 = (f32[3,16,512]{2,1,0:T(8,128)S(1)}, f32[3,16,512]{2,1,0:T(8,128)S(1)}, u32[]{:S(2)}, u32[]{:S(2)}) collective-permute-start(f32[3,16,512]{2,1,0:T(8,128)S(1)} %get-tuple-element.27), channel_id=1, source_target_pairs={{0,3},{1,0},{2,1},{3,2},{4,7},{5,4},{6,5},{7,6},{8,11},{9,8},{10,9... | collective-permute-start | bytes 294920 | tf_op jit(solution)/shard_map/ppermute | solution.py:406
  28.2 0.1 shard_map.53.n_ref
  28.4 3.5 %collective-permute-done.2.lo_ref = f32[3,16,512]{2,1,0:T(8,128)S(1)} collective-permute-done((f32[3,16,512]{2,1,0:T(8,128)S(1)}, f32[3,16,512]{2,1,0:T(8,128)S(1)}, u32[]{:S(2)}, u32[]{:S(2)}) %collective-permute-start.2) | collective-permute-done | bytes 98336 | tf_op jit(solution)/shard_map/ppermute | solution.py:405
  31.8 0.0 collective-permute-done.3.hi_ref
  31.8 0.0 all-to-all-done.1.r_ref
  31.9 0.0 copy-done
  31.9 1.5 %shard_map.54 = (f32[3,4,32,1024]{3,2,1,0:T(8,128)}, f32[3,2,16,512]{3,2,1,0:T(8,128)}) custom-call(f32[8,32,256]{2,1,0:T(8,128)S(1)} %all-to-all-done.1.r_ref, bf16[192,192]{1,0:T(8,128)(2,1)S(1)} %get-tuple-element.23.g_ref, f32[3,4,32,1024]{3,2,1,0:T(8,128)S(1)} %copy-done, f32[3,2,16,512]{3,2,1,0:T(8,128)S(1)} %shard_map.53.n_ref, ...), custom_call_target="tpu_custom_call" | custom-call | flops 16777216 | bytes 1048576 | tf_op jit(solution)/shard_map/pallas_call | solution.py:458
Async XLA Ops:
  3.4 28.4 %copy-start = (f32[3,4,32,1024]{3,2,1,0:T(8,128)S(1)}, f32[3,4,32,1024]{3,2,1,0:T(8,128)}, u32[]{:S(2)}) copy-start(f32[3,4,32,1024]{3,2,1,0:T(8,128)} %v_ref.1) | copy-start | bytes 4718596
  3.5 15.2 %all-to-all-start = ((f32[8,40,256]{2,1,0:T(8,128)}), f32[8,40,256]{2,1,0:T(8,128)S(1)}, u32[]{:S(2)}, u32[]{:S(2)}) async-start(f32[8,40,256]{2,1,0:T(8,128)} %get-tuple-element.15), calls=%async_computation | async-start | bytes 655360 | tf_op jit(solution)/shard_map/all_to_all | solution.py:433
  8.8 6.4 %collective-permute-start.1 = (f32[2,16,512]{2,1,0:T(8,128)}, f32[2,16,512]{2,1,0:T(8,128)S(1)}, u32[]{:S(2)}, u32[]{:S(2)}) collective-permute-start(f32[2,16,512]{2,1,0:T(8,128)} %get-tuple-element.21), channel_id=1, source_target_pairs={{0,3},{1,0},{2,1},{3,2},{4,7},{5,4},{6,5},{7,6},{8,11},{9,8},{10,9... | collective-permute-start | bytes 196616 | tf_op jit(solution)/shard_map/ppermute | solution.py:406
  12.4 6.3 %collective-permute-start = (f32[2,16,512]{2,1,0:T(8,128)}, f32[2,16,512]{2,1,0:T(8,128)S(1)}, u32[]{:S(2)}, u32[]{:S(2)}) collective-permute-start(f32[2,16,512]{2,1,0:T(8,128)} %get-tuple-element.16), channel_id=1, source_target_pairs={{0,1},{1,2},{2,3},{3,0},{4,5},{5,6},{6,7},{7,4},{8,9},{9,10},{10,1... | collective-permute-start | bytes 196616 | tf_op jit(solution)/shard_map/ppermute | solution.py:405
  12.4 0.9 %copy-start.1 = (f32[3,2,16,512]{3,2,1,0:T(8,128)S(1)}, f32[3,2,16,512]{3,2,1,0:T(8,128)}, u32[]{:S(2)}) copy-start(f32[3,2,16,512]{3,2,1,0:T(8,128)} %b_ref) | copy-start | bytes 589828
  13.3 0.7 %copy-start.2 = (s32[32]{0:T(128)S(1)}, s32[32]{0:T(128)}, u32[]{:S(2)}) copy-start(s32[32]{0:T(128)} %param.5) | copy-start | bytes 388
  20.2 11.7 %all-to-all-start.1 = ((f32[8,32,256]{2,1,0:T(8,128)}), f32[8,32,256]{2,1,0:T(8,128)S(1)}, u32[]{:S(2)}, u32[]{:S(2)}) async-start(f32[8,32,256]{2,1,0:T(8,128)} %get-tuple-element.22), calls=%async_computation.1 | async-start | bytes 524288 | tf_op jit(solution)/shard_map/all_to_all | solution.py:452
  24.4 7.5 %collective-permute-start.2 = (f32[3,16,512]{2,1,0:T(8,128)S(1)}, f32[3,16,512]{2,1,0:T(8,128)S(1)}, u32[]{:S(2)}, u32[]{:S(2)}) collective-permute-start(f32[3,16,512]{2,1,0:T(8,128)S(1)} %get-tuple-element.26), channel_id=1, source_target_pairs={{0,1},{1,2},{2,3},{3,0},{4,5},{5,6},{6,7},{7,4},{8,9},{9,10},{10,1... | collective-permute-start | bytes 294920 | tf_op jit(solution)/shard_map/ppermute | solution.py:405
  24.4 7.5 %collective-permute-start.3 = (f32[3,16,512]{2,1,0:T(8,128)S(1)}, f32[3,16,512]{2,1,0:T(8,128)S(1)}, u32[]{:S(2)}, u32[]{:S(2)}) collective-permute-start(f32[3,16,512]{2,1,0:T(8,128)S(1)} %get-tuple-element.27), channel_id=1, source_target_pairs={{0,3},{1,0},{2,1},{3,2},{4,7},{5,4},{6,5},{7,6},{8,11},{9,8},{10,9... | collective-permute-start | bytes 294920 | tf_op jit(solution)/shard_map/ppermute | solution.py:406

commit v5 on v4

--- a/solution.py
+++ b/solution.py
@@ -47,10 +47,10 @@
         self.half = self.edge // 2
         self.area = self.half * self.half
         self.bcols = self.nx // self.half
-        self.cz = 3 * self.zc
-        self.ru = -(-self.cz * self.k // 8) * 8
-        self.rows = n * self.ru
-        self.rb = self.cz * self.nx // self.area
+        self.rc = -(-self.zc * self.k // 8) * 8
+        self.ru = 3 * self.rc
+        self.rows = n * self.rc
+        self.rb = 3 * self.zc * self.nx // self.area
         self.r1 = -(-(self.ru + self.rb + 1) // 8) * 8
         self.re = 2 * self.zc * self.nx // self.area
         self.r2 = -(-(self.ru + self.re) // 8) * 8
@@ -68,30 +68,41 @@
     return q, q_s
 
 
+def select(g, x):
+    hi, lo = split(x)
+    out = dot(g, jnp.concatenate([hi, lo], axis=1))
+    return out[:, : x.shape[1]] + out[:, x.shape[1] :]
+
+
 def lane_route(p):
-    lane = iota((1, p.rows), 1)
-    r = jnp.floor((lane.astype(F32) + 0.5) * (1.0 / p.ru)).astype(jnp.int32)
-    i = lane - r * p.ru
-    return r, i >> log2(p.k), i & (p.k - 1)
-
-
-def restrict_kernel(p, v_hbm, t_hbm, b_hbm, out_ref, up_ref, down_ref, v_ref, t_ref, b_ref, last, first, sems):
-    n, k, s = p.n, p.k, p.slots
+    lane = iota((1, 1, p.rows), 2)
+    i = lane & (p.rc - 1)
+    return lane >> log2(p.rc), i >> log2(p.k), i & (p.k - 1)
+
+
+def restrict_kernel(p, v_hbm, t_hbm, b_hbm, out_hbm, up_hbm, down_hbm, v_ref, t_ref, b_ref, out, last, first, sems):
+    n, k, s, zc = p.n, p.k, p.slots, p.zc
     me = lax.axis_index("xy")
     t_copy = pltpu.make_async_copy(t_hbm, t_ref, sems.at[0])
     b_copy = pltpu.make_async_copy(b_hbm, b_ref, sems.at[1])
     v_copies = [pltpu.make_async_copy(v_hbm.at[c], v_ref.at[c], sems.at[2 + c]) for c in range(3)]
     t_copy.start()
+    b_copy.start()
     for copy in v_copies:
         copy.start()
-    b_copy.start()
+    half_fine = p.edge * p.edge // 2
+    half_area = p.area // 2
+    f, c = iota((half_fine, half_area), 0), iota((half_fine, half_area), 1)
+    e = log2(p.edge)
+    coarse = ((f >> (e + 1)) << (e - 1)) + ((f & (p.edge - 1)) >> 1)
+    sel = one_hot(coarse == c)
     t_copy.wait()
     table = t_ref[...]
     q, _ = send_positions(p, table)
-    lanes = p.cz * s
+    lanes = zc * s
     rep = one_hot((iota((s, lanes), 1) & (s - 1)) == iota((s, lanes), 0))
     qt = dot(jnp.broadcast_to(q, (8, s)).astype(BF16), rep)[0:1]
-    shape = (n, p.ru, lanes)
+    shape = (n, p.rc, lanes)
     i = iota(shape, 1)
     target = (iota(shape, 0) * k + (i & (k - 1))).astype(F32)
     g = one_hot(((i >> log2(k)) == (iota(shape, 2) >> log2(s))) & (target == qt.reshape(1, 1, lanes)))
@@ -105,38 +116,41 @@
     cols = dot(gather, spread)
     at = p.ru + p.rb
     for r in range(n):
-        out_ref[r, at : at + 1, :] = cols[r : r + 1]
-    half_fine = p.edge * p.edge // 2
-    half_area = p.area // 2
-    f, c = iota((half_fine, half_area), 0), iota((half_fine, half_area), 1)
-    e = log2(p.edge)
-    coarse = ((f >> (e + 1)) << (e - 1)) + ((f & (p.edge - 1)) >> 1)
-    sel = one_hot(coarse == c)
-    parts = []
+        out[r, at : at + 1, :] = cols[r : r + 1]
+    b_copy.wait()
+    sends = [
+        pltpu.make_async_copy(b_ref.at[0:2, zc - 1], up_hbm, sems.at[5]),
+        pltpu.make_async_copy(b_ref.at[0:2, 0], down_hbm, sems.at[6]),
+    ]
     for c in range(3):
-        v_copies[c].wait()
-        z_sum = jnp.concatenate([v_ref[c, 2 * z] + v_ref[c, 2 * z + 1] for z in range(p.zc)], axis=0)
-        hi, lo = split(z_sum)
-        m = p.zc * s
-        ws = [slice(h * half_fine, (h + 1) * half_fine) for h in range(2)]
-        out = dot(jnp.concatenate([x[:, w] for w in ws for x in (hi, lo)], axis=0), sel)
-        halves = [out[2 * h * m : (2 * h + 1) * m] + out[(2 * h + 1) * m : (2 * h + 2) * m] for h in range(2)]
-        parts.append(jnp.concatenate(halves, axis=1))
-    hi, lo = split(jnp.concatenate(parts, axis=0) * 0.125)
-    out_ref[:, : p.ru, :] = (dot(g, hi) + dot(g, lo)).reshape(n, p.ru, p.area)
-    b_copy.wait()
-    for c in range(3):
-        for z in range(p.zc):
+        for z in range(zc):
             for h in range(p.wrap):
-                at = (c * p.zc + z) * p.wrap + h
+                at = (c * zc + z) * p.wrap + h
                 w = slice(h * p.area, (h + 1) * p.area)
                 last[at : at + 1, :] = b_ref[c, z, p.ny - 1 : p.ny, w]
                 first[at : at + 1, :] = b_ref[c, z, 0:1, w]
     nxt = lax.rem(me + 1, n)
     for r in range(n):
-        out_ref[r, p.ru : p.ru + p.rb, :] = jnp.where(r == nxt, last[: p.rb], first[: p.rb])
-    up_ref[...] = b_ref[0:2, p.zc - 1]
-    down_ref[...] = b_ref[0:2, 0]
+        out[r, p.ru : p.ru + p.rb, :] = jnp.where(r == nxt, last[: p.rb], first[: p.rb])
+    tail = pl.ds(p.ru, p.r1 - p.ru)
+    sends.append(pltpu.make_async_copy(out.at[:, tail, :], out_hbm.at[:, tail, :], sems.at[7]))
+    for send in sends:
+        send.start()
+    m = zc * s
+    ws = [slice(h * half_fine, (h + 1) * half_fine) for h in range(2)]
+    for c in range(3):
+        v_copies[c].wait()
+        z_sum = jnp.concatenate([v_ref[c, 2 * z] + v_ref[c, 2 * z + 1] for z in range(zc)], axis=0)
+        hi, lo = split(z_sum)
+        o = dot(jnp.concatenate([x[:, w] for w in ws for x in (hi, lo)], axis=0), sel)
+        u = [o[2 * h * m : (2 * h + 1) * m] + o[(2 * h + 1) * m : (2 * h + 2) * m] for h in range(2)]
+        u = jnp.concatenate(u, axis=1) * 0.125
+        out[:, c * p.rc : (c + 1) * p.rc, :] = select(g, u).reshape(n, p.rc, p.area)
+        rows = pl.ds(c * p.rc, p.rc)
+        sends.append(pltpu.make_async_copy(out.at[:, rows, :], out_hbm.at[:, rows, :], sems.at[8 + c]))
+        sends[-1].start()
+    for send in sends:
+        send.wait()
 
 
 def tile_transpose(p, t):
@@ -204,12 +218,10 @@
 def interior_kernel(p, b_ref, t_ref, copy_ref, j_ref, next_ref, g3_ref):
     s, k = p.slots, p.k
     _, q_s = send_positions(p, t_ref[...])
-    r_l, c_l, j_l = lane_route(p)
-    shape = (p.cz, s, p.rows)
-    g3 = (iota(shape, 0) == c_l.reshape(1, 1, p.rows)) & (
-        q_s.reshape(1, s, 1) == (r_l * k + j_l).astype(F32).reshape(1, 1, p.rows)
-    )
-    g3_ref[...] = one_hot(g3).reshape(p.cz * s, p.rows)
+    r_l, z_l, j_l = lane_route(p)
+    shape = (p.zc, s, p.rows)
+    g3 = (iota(shape, 0) == z_l) & (q_s.reshape(1, s, 1) == (r_l * k + j_l).astype(F32))
+    g3_ref[...] = one_hot(g3).reshape(p.zc * s, p.rows)
     zero = jnp.zeros((p.ny, p.nx), F32)
     for z in range(p.zc):
         b = [b_ref[c, z] for c in range(3)]
@@ -232,37 +244,22 @@
     return north, jnp.where(y == 0, row_of(p, ref, prv, at), 0.0)
 
 
-def field_kernel(p, r_ref, b_ref, j_ref, lo_ref, hi_ref, out_ref, e_ref, up_ref, down_ref, e_rows):
+def field_kernel(p, r_ref, b_ref, j_ref, lo_ref, hi_ref, out_hbm, e_ref, up_ref, down_ref, out, e_rows, sems):
     n, k, zc = p.n, p.k, p.zc
     me = lax.axis_index("xy")
     nxt, prv = lax.rem(me + 1, n), lax.rem(me + n - 1, n)
+    b = [[b_ref[c, z] for z in range(zc)] for c in range(3)]
     cols = r_ref[:, p.ru + p.rb, :]
-    r_l, c_l, _ = lane_route(p)
-    shape = (n, p.rows)
-    col_l = jnp.sum(jnp.where(iota(shape, 0) == r_l, cols[:, : p.rows], 0.0), axis=0, keepdims=True)
-    shape = (p.cz, p.bcols, p.rows)
-    g2 = one_hot(
-        (iota(shape, 0) == c_l.reshape(1, 1, p.rows))
-        & (iota(shape, 1).astype(F32) == col_l.reshape(1, 1, p.rows))
-    ).reshape(p.cz * p.bcols, p.rows)
-    shape = (n, p.ru, 128)
+    shape = (n, p.rc, 128)
     col_s = jnp.sum(
         jnp.where((iota(shape, 1) & (k - 1)) == iota(shape, 2), cols[:, None, :128], 0.0), axis=2, keepdims=True
     )
-    lanes = p.cz * p.bcols
-    shape = (n, p.ru, lanes)
+    shape = (n, p.rc, zc * p.bcols)
     lane = iota(shape, 2)
-    g2t = one_hot(
+    g = one_hot(
         ((iota(shape, 1) >> log2(k)) == (lane >> log2(p.bcols)))
         & (col_s == (lane & (p.bcols - 1)).astype(F32))
-    ).reshape(p.rows, lanes)
-    hi, lo = split(r_ref[:, : p.ru, :].reshape(p.rows, p.area))
-    u_blk = dot(g2, hi) + dot(g2, lo)
-    u = [
-        [blocks_to_grid(p, u_blk[(c * zc + z) * p.bcols : (c * zc + z + 1) * p.bcols]) for z in range(zc)]
-        for c in range(3)
-    ]
-    b = [[b_ref[c, z] for z in range(zc)] for c in range(3)]
+    ).reshape(p.rows, zc * p.bcols)
     force = []
     zero = jnp.zeros((p.ny, p.nx), F32)
     for z in range(zc):
@@ -281,9 +278,26 @@
         j1 = j_ref[1, z] + dz[0] * 0.5
         j2 = j_ref[2, z] - dy[0] * 0.5
         force.append([j1 * bz[2] - j2 * bz[1], j2 * bz[0] - j0 * bz[2], j0 * bz[1] - j1 * bz[0]])
-    f_blk = jnp.concatenate([grid_to_blocks(p, force[z][c]) for c in range(3) for z in range(zc)], axis=0)
-    hi, lo = split(f_blk)
-    out_ref[:, : p.ru, :] = (dot(g2t, hi) + dot(g2t, lo)).reshape(n, p.ru, p.area)
+    sends = []
+    for c in range(3):
+        f_blk = jnp.concatenate([grid_to_blocks(p, force[z][c]) for z in range(zc)], axis=0)
+        out[:, c * p.rc : (c + 1) * p.rc, :] = select(g, f_blk).reshape(n, p.rc, p.area)
+        rows = pl.ds(c * p.rc, p.rc)
+        sends.append(pltpu.make_async_copy(out.at[:, rows, :], out_hbm.at[:, rows, :], sems.at[c]))
+        sends[-1].start()
+    p_l, z_l, _ = lane_route(p)
+    shape = (n, p.rows)
+    col_l = jnp.sum(
+        jnp.where(iota(shape, 0) == p_l.reshape(1, p.rows), cols[:, : p.rows], 0.0), axis=0, keepdims=True
+    )
+    shape = (zc, p.bcols, p.rows)
+    g = one_hot(
+        (iota(shape, 0) == z_l) & (iota(shape, 1).astype(F32) == col_l.reshape(1, 1, p.rows))
+    ).reshape(zc * p.bcols, p.rows)
+    u = []
+    for c in range(3):
+        blk = select(g, r_ref[:, c * p.rc : (c + 1) * p.rc, :].reshape(p.rows, p.area))
+        u.append([blocks_to_grid(p, blk[z * p.bcols : (z + 1) * p.bcols]) for z in range(zc)])
     for z in range(zc):
         uz, bz = [u[c][z] for c in range(3)], [b[c][z] for c in range(3)]
         ez = [uz[1] * bz[2] - uz[2] * bz[1], uz[2] * bz[0] - uz[0] * bz[2], uz[0] * bz[1] - uz[1] * bz[0]]
@@ -300,7 +314,12 @@
                 e_rows[0, at : at + 1, :] = ez[c][0:1, w]
                 e_rows[1, at : at + 1, :] = ez[c][p.ny - 1 : p.ny, w]
     for r in range(n):
-        out_ref[r, p.ru : p.ru + p.re, :] = jnp.where(r == nxt, e_rows[1], e_rows[0])
+        out[r, p.ru : p.ru + p.re, :] = jnp.where(r == nxt, e_rows[1], e_rows[0])
+    rows = pl.ds(p.ru, p.r2 - p.ru)
+    sends.append(pltpu.make_async_copy(out.at[:, rows, :], out_hbm.at[:, rows, :], sems.at[3]))
+    sends[-1].start()
+    for send in sends:
+        send.wait()
 
 
 def local_kernel(p, r_ref, b_ref, lo_ref, hi_ref, e_ref, next_ref):
@@ -335,18 +354,18 @@
     c, f = iota((half_area, half_fine), 0), iota((half_area, half_fine), 1)
     coarse = ((f >> (ex + 1)) << (ex - 1)) + ((f & (p.edge - 1)) >> 1)
     sel = one_hot(coarse == c)
-    hi, lo = split(r_ref[:, : p.ru, :].reshape(p.rows, p.area) * 0.1)
+    sel = jnp.concatenate([sel, sel], axis=0)
     g = g_ref[...]
-    sel = jnp.concatenate([sel, sel], axis=0)
-    hi, lo = dot(g, hi).astype(BF16), dot(g, lo).astype(BF16)
     ws = [slice(h * half_area, (h + 1) * half_area) for h in range(2)]
-    pairs = [jnp.concatenate([hi[:, w], lo[:, w]], axis=1) for w in ws]
     s = p.slots
     m = zc * s
     copies = []
     for c in range(3):
-        at = slice(c * m, (c + 1) * m)
-        add = dot(jnp.concatenate([x[at] for x in pairs], axis=0), sel)
+        hi, lo = split(r_ref[:, c * p.rc : (c + 1) * p.rc, :].reshape(p.rows, p.area) * 0.1)
+        parts = dot(g, jnp.concatenate([hi, lo], axis=1)).astype(BF16)
+        hi, lo = parts[:, : p.area], parts[:, p.area :]
+        pairs = [jnp.concatenate([hi[:, w], lo[:, w]], axis=1) for w in ws]
+        add = dot(jnp.concatenate(pairs, axis=0), sel)
         for z in range(zc):
             for h in range(2):
                 fw = slice(h * half_fine, (h + 1) * half_fine)
@@ -415,18 +434,15 @@
     sent, up, down = call(
         functools.partial(restrict_kernel, p),
         [HBM] * 3,
-        [
-            (struct(p.n, p.r1, p.area), VMEM),
-            (struct(2, *plane), VMEM),
-            (struct(2, *plane), VMEM),
-        ],
+        [(struct(p.n, p.r1, p.area), HBM), (struct(2, *plane), HBM), (struct(2, *plane), HBM)],
         [
             pltpu.VMEM(velocity.shape, F32),
             pltpu.VMEM((1, p.slots), jnp.int32),
             pltpu.VMEM(magnetic.shape, F32),
+            pltpu.VMEM((p.n, p.r1, p.area), F32),
             pltpu.VMEM((-(-p.rb // 8) * 8, p.area), F32),
             pltpu.VMEM((-(-p.rb // 8) * 8, p.area), F32),
-            dma((5,)),
+            dma((11,)),
         ],
         ALL_VMEM,
     )(velocity, table, magnetic)
@@ -436,18 +452,18 @@
     field, current, diffused, g3 = call(
         functools.partial(interior_kernel, p),
         [VMEM] * 2,
-        [(struct(*magnetic.shape), VMEM)] * 3 + [(struct(p.cz * p.slots, p.rows, dtype=BF16), VMEM)],
+        [(struct(*magnetic.shape), VMEM)] * 3 + [(struct(p.zc * p.slots, p.rows, dtype=BF16), VMEM)],
     )(held, held_table)
     sent, emf, up, down = call(
         functools.partial(field_kernel, p),
         [VMEM] * 5,
         [
-            (struct(p.n, p.r2, p.area), VMEM),
+            (struct(p.n, p.r2, p.area), HBM),
             (struct(*magnetic.shape), VMEM),
             (struct(3, *plane), VMEM),
             (struct(3, *plane), VMEM),
         ],
-        [pltpu.VMEM((2, p.re, p.area), F32)],
+        [pltpu.VMEM((p.n, p.r2, p.area), F32), pltpu.VMEM((2, p.re, p.area), F32), dma((4,))],
     )(got, field, current, below, above)
     got_force = lax.all_to_all(sent, "xy", 0, 0, tiled=True)
     emf_below, emf_above = planes(up, down)

time: 33.8 us -> 34.1 us (level)
  no operation moved by 1% of the time
where the time goes in v5:
time: 34.1 us; the launch traced here: 33.7 us
  starting transfers between devices  17 us (50%)
  waiting for transfers between devices  7.95 us (23%)
  Pallas kernels  6.5 us (19%)
  local copies, waits for them, and re-layouts  1.59 us (5%)
  between operations  0.69 us (2%)
    ppermute x2, starting transfers between devices, planes(): above = lax.ppermute(down, 'gz', ring('gz', -1))  7.42 us
    ppermute x2, waiting for transfers between devices, planes(): below = lax.ppermute(up, 'gz', ring('gz', 1))  6.97 us
    all_to_all x1, starting transfers between devices, body(): got = lax.all_to_all(sent, 'xy', 0, 0, tiled=True)  5.34 us
    all_to_all x1, starting transfers between devices, body(): got_force = lax.all_to_all(sent, 'xy', 0, 0, tiled=True)  4.21 us
    pallas_call x1, Pallas kernels, body(): call(functools.partial(restrict_kernel, p), [HBM] * 3, [(struct(p.n, p.r1...  3.01 us
    pallas_call x1, Pallas kernels, body(): call(functools.partial(field_kernel, p), [VMEM] * 5, [(struct(p.n, p.r2,...  1.6 us
    unnamed x6, local copies, waits for them, and re-layouts  1.59 us
    pallas_call x1, Pallas kernels, body(): call(functools.partial(finish_kernel, p), [VMEM] * 6, [(struct(*velocity....  1.53 us
  transfers between devices with their start and end apart: 6, of which 3 were waited for; matrix products, arithmetic and copies ran while one was open for 0% of the time, Pallas kernels for 1%

profile of v5, /device:TPU:0, one launch (start us, length us, event | category | flops | bytes accessed | tf_op | source)
XLA Modules:
  0.0 33.7 jit_solution(16253179891317672579)
XLA Ops:
  0.6 3.0 %shard_map.50 = (f32[8,40,256]{2,1,0:T(8,128)}, f32[2,16,512]{2,1,0:T(8,128)}, f32[2,16,512]{2,1,0:T(8,128)}) custom-call(f32[3,4,32,1024]{3,2,1,0:T(8,128)} %v_ref.1, s32[1,32]{1,0:T(1,128)} %bitcast.1, f32[3,2,16,512]{3,2,1,0:T(8,128)} %b_ref), custom_call_target="tpu_custom_call" | custom-call | flops 16777216 | bytes 1048576 | tf_op jit(solution)/shard_map/pallas_call | solution.py:434
  3.6 0.0 copy-start
  3.7 5.3 %all-to-all-start = ((f32[8,40,256]{2,1,0:T(8,128)}), f32[8,40,256]{2,1,0:T(8,128)S(1)}, u32[]{:S(2)}, u32[]{:S(2)}) async-start(f32[8,40,256]{2,1,0:T(8,128)} %get-tuple-element.15), calls=%async_computation | async-start | bytes 655360 | tf_op jit(solution)/shard_map/all_to_all | solution.py:449
  9.0 3.6 %collective-permute-start.1 = (f32[2,16,512]{2,1,0:T(8,128)}, f32[2,16,512]{2,1,0:T(8,128)S(1)}, u32[]{:S(2)}, u32[]{:S(2)}) collective-permute-start(f32[2,16,512]{2,1,0:T(8,128)} %get-tuple-element.21), channel_id=1, source_target_pairs={{0,3},{1,0},{2,1},{3,2},{4,7},{5,4},{6,5},{7,6},{8,11},{9,8},{10,9... | collective-permute-start | bytes 196616 | tf_op jit(solution)/shard_map/ppermute | solution.py:425
  12.6 0.0 collective-permute-start
  12.6 0.0 copy-start.1
  12.6 0.9 %copy-done.1 = f32[3,2,16,512]{3,2,1,0:T(8,128)S(1)} copy-done((f32[3,2,16,512]{3,2,1,0:T(8,128)S(1)}, f32[3,2,16,512]{3,2,1,0:T(8,128)}, u32[]{:S(2)}) %copy-start.1) | copy-done | bytes 196632
  13.5 0.0 copy-start.2
  13.5 0.7 %copy-done.2 = s32[32]{0:T(128)S(1)} copy-done((s32[32]{0:T(128)S(1)}, s32[32]{0:T(128)}, u32[]{:S(2)}) %copy-start.2) | copy-done | bytes 152
  14.2 0.2 shard_map.51
  14.4 1.0 %collective-permute-done.1.hi_ref = f32[2,16,512]{2,1,0:T(8,128)S(1)} collective-permute-done((f32[2,16,512]{2,1,0:T(8,128)}, f32[2,16,512]{2,1,0:T(8,128)S(1)}, u32[]{:S(2)}, u32[]{:S(2)}) %collective-permute-start.1) | collective-permute-done | bytes 65568 | tf_op jit(solution)/shard_map/ppermute | solution.py:425
  15.4 3.5 %collective-permute-done.lo_ref = f32[2,16,512]{2,1,0:T(8,128)S(1)} collective-permute-done((f32[2,16,512]{2,1,0:T(8,128)}, f32[2,16,512]{2,1,0:T(8,128)S(1)}, u32[]{:S(2)}, u32[]{:S(2)}) %collective-permute-start) | collective-permute-done | bytes 65568 | tf_op jit(solution)/shard_map/ppermute | solution.py:424
  18.9 0.0 all-to-all-done.r_ref
  18.9 1.6 %shard_map.52 = (f32[8,32,256]{2,1,0:T(8,128)}, f32[3,2,16,512]{3,2,1,0:T(8,128)S(1)}, f32[3,16,512]{2,1,0:T(8,128)S(1)}, f32[3,16,512]{2,1,0:T(8,128)S(1)}) custom-call(f32[8,40,256]{2,1,0:T(8,128)S(1)} %all-to-all-done.r_ref, f32[3,2,16,512]{3,2,1,0:T(8,128)S(1)} %get-tuple-element.19.b_ref, f32[3,2,16,512]{3,2,1,0:T(8,128)S(1)} %get-tuple-element.20.j_ref, ...), custom_call_target="tpu_custom_call" | custom-call | flops 16777216 | bytes 1048576 | tf_op jit(solution)/shard_map/pallas_call | solution.py:457
  20.5 4.2 %all-to-all-start.1 = ((f32[8,32,256]{2,1,0:T(8,128)}), f32[8,32,256]{2,1,0:T(8,128)S(1)}, u32[]{:S(2)}, u32[]{:S(2)}) async-start(f32[8,32,256]{2,1,0:T(8,128)} %get-tuple-element.22), calls=%async_computation.1 | async-start | bytes 524288 | tf_op jit(solution)/shard_map/all_to_all | solution.py:468
  24.7 0.0 collective-permute-start.2
  24.7 3.8 %collective-permute-start.3 = (f32[3,16,512]{2,1,0:T(8,128)S(1)}, f32[3,16,512]{2,1,0:T(8,128)S(1)}, u32[]{:S(2)}, u32[]{:S(2)}) collective-permute-start(f32[3,16,512]{2,1,0:T(8,128)S(1)} %get-tuple-element.27), channel_id=1, source_target_pairs={{0,3},{1,0},{2,1},{3,2},{4,7},{5,4},{6,5},{7,6},{8,11},{9,8},{10,9... | collective-permute-start | bytes 294920 | tf_op jit(solution)/shard_map/ppermute | solution.py:425
  28.5 0.1 shard_map.53.n_ref
  28.7 3.5 %collective-permute-done.2.lo_ref = f32[3,16,512]{2,1,0:T(8,128)S(1)} collective-permute-done((f32[3,16,512]{2,1,0:T(8,128)S(1)}, f32[3,16,512]{2,1,0:T(8,128)S(1)}, u32[]{:S(2)}, u32[]{:S(2)}) %collective-permute-start.2) | collective-permute-done | bytes 98336 | tf_op jit(solution)/shard_map/ppermute | solution.py:424
  32.2 0.0 collective-permute-done.3.hi_ref
  32.2 0.0 all-to-all-done.1.r_ref
  32.2 0.0 copy-done
  32.2 1.5 %shard_map.54 = (f32[3,4,32,1024]{3,2,1,0:T(8,128)}, f32[3,2,16,512]{3,2,1,0:T(8,128)}) custom-call(f32[8,32,256]{2,1,0:T(8,128)S(1)} %all-to-all-done.1.r_ref, bf16[64,64]{1,0:T(8,128)(2,1)S(1)} %get-tuple-element.23.g_ref, f32[3,4,32,1024]{3,2,1,0:T(8,128)S(1)} %copy-done, f32[3,2,16,512]{3,2,1,0:T(8,128)S(1)} %shard_map.53.n_ref, ...), custom_call_target="tpu_custom_call" | custom-call | flops 16777216 | bytes 1048576 | tf_op jit(solution)/shard_map/pallas_call | solution.py:474
Async XLA Ops:
  3.6 28.5 %copy-start = (f32[3,4,32,1024]{3,2,1,0:T(8,128)S(1)}, f32[3,4,32,1024]{3,2,1,0:T(8,128)}, u32[]{:S(2)}) copy-start(f32[3,4,32,1024]{3,2,1,0:T(8,128)} %v_ref.1) | copy-start | bytes 4718596
  3.7 15.2 %all-to-all-start = ((f32[8,40,256]{2,1,0:T(8,128)}), f32[8,40,256]{2,1,0:T(8,128)S(1)}, u32[]{:S(2)}, u32[]{:S(2)}) async-start(f32[8,40,256]{2,1,0:T(8,128)} %get-tuple-element.15), calls=%async_computation | async-start | bytes 655360 | tf_op jit(solution)/shard_map/all_to_all | solution.py:449
  9.0 6.4 %collective-permute-start.1 = (f32[2,16,512]{2,1,0:T(8,128)}, f32[2,16,512]{2,1,0:T(8,128)S(1)}, u32[]{:S(2)}, u32[]{:S(2)}) collective-permute-start(f32[2,16,512]{2,1,0:T(8,128)} %get-tuple-element.21), channel_id=1, source_target_pairs={{0,3},{1,0},{2,1},{3,2},{4,7},{5,4},{6,5},{7,6},{8,11},{9,8},{10,9... | collective-permute-start | bytes 196616 | tf_op jit(solution)/shard_map/ppermute | solution.py:425
  12.6 6.3 %collective-permute-start = (f32[2,16,512]{2,1,0:T(8,128)}, f32[2,16,512]{2,1,0:T(8,128)S(1)}, u32[]{:S(2)}, u32[]{:S(2)}) collective-permute-start(f32[2,16,512]{2,1,0:T(8,128)} %get-tuple-element.16), channel_id=1, source_target_pairs={{0,1},{1,2},{2,3},{3,0},{4,5},{5,6},{6,7},{7,4},{8,9},{9,10},{10,1... | collective-permute-start | bytes 196616 | tf_op jit(solution)/shard_map/ppermute | solution.py:424
  12.6 0.9 %copy-start.1 = (f32[3,2,16,512]{3,2,1,0:T(8,128)S(1)}, f32[3,2,16,512]{3,2,1,0:T(8,128)}, u32[]{:S(2)}) copy-start(f32[3,2,16,512]{3,2,1,0:T(8,128)} %b_ref) | copy-start | bytes 589828
  13.5 0.7 %copy-start.2 = (s32[32]{0:T(128)S(1)}, s32[32]{0:T(128)}, u32[]{:S(2)}) copy-start(s32[32]{0:T(128)} %param.5) | copy-start | bytes 388
  20.5 11.7 %all-to-all-start.1 = ((f32[8,32,256]{2,1,0:T(8,128)}), f32[8,32,256]{2,1,0:T(8,128)S(1)}, u32[]{:S(2)}, u32[]{:S(2)}) async-start(f32[8,32,256]{2,1,0:T(8,128)} %get-tuple-element.22), calls=%async_computation.1 | async-start | bytes 524288 | tf_op jit(solution)/shard_map/all_to_all | solution.py:468
  24.7 7.5 %collective-permute-start.2 = (f32[3,16,512]{2,1,0:T(8,128)S(1)}, f32[3,16,512]{2,1,0:T(8,128)S(1)}, u32[]{:S(2)}, u32[]{:S(2)}) collective-permute-start(f32[3,16,512]{2,1,0:T(8,128)S(1)} %get-tuple-element.26), channel_id=1, source_target_pairs={{0,1},{1,2},{2,3},{3,0},{4,5},{5,6},{6,7},{7,4},{8,9},{9,10},{10,1... | collective-permute-start | bytes 294920 | tf_op jit(solution)/shard_map/ppermute | solution.py:424
  24.7 7.5 %collective-permute-start.3 = (f32[3,16,512]{2,1,0:T(8,128)S(1)}, f32[3,16,512]{2,1,0:T(8,128)S(1)}, u32[]{:S(2)}, u32[]{:S(2)}) collective-permute-start(f32[3,16,512]{2,1,0:T(8,128)S(1)} %get-tuple-element.27), channel_id=1, source_target_pairs={{0,3},{1,0},{2,1},{3,2},{4,7},{5,4},{6,5},{7,6},{8,11},{9,8},{10,9... | collective-permute-start | bytes 294920 | tf_op jit(solution)/shard_map/ppermute | solution.py:425

commit v6 on v5

--- a/solution.py
+++ b/solution.py
@@ -57,6 +57,10 @@
         self.wrap = self.nx // self.area
 
 
+def mirror(i):
+    return (i & ~7) | ((8 - (i & 7)) & 7)
+
+
 def send_positions(p, table):
     s = p.slots
     row = jnp.broadcast_to((table >> log2(p.bcols)).astype(F32), (s, s))
@@ -94,7 +98,7 @@
     half_area = p.area // 2
     f, c = iota((half_fine, half_area), 0), iota((half_fine, half_area), 1)
     e = log2(p.edge)
-    coarse = ((f >> (e + 1)) << (e - 1)) + ((f & (p.edge - 1)) >> 1)
+    coarse = (mirror(f >> (e + 1)) << (e - 1)) + ((f & (p.edge - 1)) >> 1)
     sel = one_hot(coarse == c)
     t_copy.wait()
     table = t_ref[...]
@@ -136,6 +140,7 @@
     sends.append(pltpu.make_async_copy(out.at[:, tail, :], out_hbm.at[:, tail, :], sems.at[7]))
     for send in sends:
         send.start()
+    averages = []
     m = zc * s
     ws = [slice(h * half_fine, (h + 1) * half_fine) for h in range(2)]
     for c in range(3):
@@ -144,8 +149,9 @@
         hi, lo = split(z_sum)
         o = dot(jnp.concatenate([x[:, w] for w in ws for x in (hi, lo)], axis=0), sel)
         u = [o[2 * h * m : (2 * h + 1) * m] + o[(2 * h + 1) * m : (2 * h + 2) * m] for h in range(2)]
-        u = jnp.concatenate(u, axis=1) * 0.125
-        out[:, c * p.rc : (c + 1) * p.rc, :] = select(g, u).reshape(n, p.rc, p.area)
+        averages.append(jnp.concatenate(u, axis=1) * 0.125)
+    for c in range(3):
+        out[:, c * p.rc : (c + 1) * p.rc, :] = select(g, averages[c]).reshape(n, p.rc, p.area)
         rows = pl.ds(c * p.rc, p.rc)
         sends.append(pltpu.make_async_copy(out.at[:, rows, :], out_hbm.at[:, rows, :], sems.at[8 + c]))
         sends[-1].start()
@@ -154,15 +160,11 @@
 
 
 def tile_transpose(p, t):
-    ax = t.ndim - 2
-    s, g = iota(t.shape, ax), iota(t.shape, ax + 1) >> log2(p.half)
+    g = iota(t.shape, 1) >> log2(p.half)
+    t = pltpu.roll(t, 0, 1, stride=p.half, stride_axis=0)
     for b in (1, 2, 4):
-        w = b * p.half
-        up = pltpu.roll(pltpu.roll(t, 8 - b, ax), w, ax + 1)
-        dn = up if b == 4 else pltpu.roll(pltpu.roll(t, b, ax), 128 - w, ax + 1)
-        sb, gb = (s & b) != 0, (g & b) != 0
-        t = jnp.where(sb == gb, t, jnp.where(gb, up, dn))
-    return t
+        t = jnp.where((g & b) != 0, pltpu.roll(t, 8 - b, 0), t)
+    return pltpu.roll(t, 0, 1, stride=p.half, stride_axis=0)
 
 
 def blocks_to_grid(p, blk):
@@ -244,7 +246,7 @@
     return north, jnp.where(y == 0, row_of(p, ref, prv, at), 0.0)
 
 
-def field_kernel(p, r_ref, b_ref, j_ref, lo_ref, hi_ref, out_hbm, e_ref, up_ref, down_ref, out, e_rows, sems):
+def field_kernel(p, r_ref, b_ref, j_ref, lo_ref, hi_ref, out, e_ref, up_ref, down_ref, e_rows):
     n, k, zc = p.n, p.k, p.zc
     me = lax.axis_index("xy")
     nxt, prv = lax.rem(me + 1, n), lax.rem(me + n - 1, n)
@@ -258,7 +260,7 @@
     lane = iota(shape, 2)
     g = one_hot(
         ((iota(shape, 1) >> log2(k)) == (lane >> log2(p.bcols)))
-        & (col_s == (lane & (p.bcols - 1)).astype(F32))
+        & (col_s == mirror(lane & (p.bcols - 1)).astype(F32))
     ).reshape(p.rows, zc * p.bcols)
     force = []
     zero = jnp.zeros((p.ny, p.nx), F32)
@@ -278,13 +280,9 @@
         j1 = j_ref[1, z] + dz[0] * 0.5
         j2 = j_ref[2, z] - dy[0] * 0.5
         force.append([j1 * bz[2] - j2 * bz[1], j2 * bz[0] - j0 * bz[2], j0 * bz[1] - j1 * bz[0]])
-    sends = []
     for c in range(3):
         f_blk = jnp.concatenate([grid_to_blocks(p, force[z][c]) for z in range(zc)], axis=0)
         out[:, c * p.rc : (c + 1) * p.rc, :] = select(g, f_blk).reshape(n, p.rc, p.area)
-        rows = pl.ds(c * p.rc, p.rc)
-        sends.append(pltpu.make_async_copy(out.at[:, rows, :], out_hbm.at[:, rows, :], sems.at[c]))
-        sends[-1].start()
     p_l, z_l, _ = lane_route(p)
     shape = (n, p.rows)
     col_l = jnp.sum(
@@ -315,11 +313,6 @@
                 e_rows[1, at : at + 1, :] = ez[c][p.ny - 1 : p.ny, w]
     for r in range(n):
         out[r, p.ru : p.ru + p.re, :] = jnp.where(r == nxt, e_rows[1], e_rows[0])
-    rows = pl.ds(p.ru, p.r2 - p.ru)
-    sends.append(pltpu.make_async_copy(out.at[:, rows, :], out_hbm.at[:, rows, :], sems.at[3]))
-    sends[-1].start()
-    for send in sends:
-        send.wait()
 
 
 def local_kernel(p, r_ref, b_ref, lo_ref, hi_ref, e_ref, next_ref):
@@ -346,8 +339,8 @@
             next_ref[c, z] = b_ref[c, z] + 0.05 * total
 
 
-def finish_kernel(p, r_ref, g_ref, v_ref, n_ref, lo_ref, hi_ref, vel_hbm, mag_hbm, vel, mag, sems):
-    n, zc = p.n, p.zc
+def widen_kernel(p, r_ref, g_ref, v_ref, vel_hbm, vel, sems):
+    zc = p.zc
     half_fine = p.edge * p.edge // 2
     half_area = p.area // 2
     ex = log2(p.edge)
@@ -374,6 +367,12 @@
                     vel[c, 2 * z + d, :, fw] = v_ref[c, 2 * z + d, :, fw] + part
         copies.append(pltpu.make_async_copy(vel.at[c], vel_hbm.at[c], sems.at[c]))
         copies[-1].start()
+    for copy in copies:
+        copy.wait()
+
+
+def finish_kernel(p, r_ref, n_ref, lo_ref, hi_ref, mag):
+    n, zc = p.n, p.zc
     me = lax.axis_index("xy")
     nxt, prv = lax.rem(me + 1, n), lax.rem(me + n - 1, n)
 
@@ -393,10 +392,6 @@
         mag[0, z] = n_ref[0, z] + 0.05 * (dy(1, z) - dz[1])
         mag[1, z] = n_ref[1, z] + 0.05 * dz[0]
         mag[2, z] = n_ref[2, z] + 0.05 * (outer - dy(0, z))
-    copies.append(pltpu.make_async_copy(mag, mag_hbm, sems.at[3]))
-    copies[-1].start()
-    for copy in copies:
-        copy.wait()
 
 
 def struct(*shape, dtype=F32):
@@ -458,26 +453,28 @@
         functools.partial(field_kernel, p),
         [VMEM] * 5,
         [
-            (struct(p.n, p.r2, p.area), HBM),
+            (struct(p.n, p.r2, p.area), VMEM),
             (struct(*magnetic.shape), VMEM),
             (struct(3, *plane), VMEM),
             (struct(3, *plane), VMEM),
         ],
-        [pltpu.VMEM((p.n, p.r2, p.area), F32), pltpu.VMEM((2, p.re, p.area), F32), dma((4,))],
+        [pltpu.VMEM((2, p.re, p.area), F32)],
     )(got, field, current, below, above)
     got_force = lax.all_to_all(sent, "xy", 0, 0, tiled=True)
     emf_below, emf_above = planes(up, down)
     (partial,) = call(
         functools.partial(local_kernel, p), [VMEM] * 5, [(struct(*magnetic.shape), VMEM)]
     )(got, diffused, below, above, emf)
-    return tuple(
-        call(
-            functools.partial(finish_kernel, p),
-            [VMEM] * 6,
-            [(struct(*velocity.shape), HBM), (struct(*magnetic.shape), HBM)],
-            [pltpu.VMEM(velocity.shape, F32), pltpu.VMEM(magnetic.shape, F32), dma((4,))],
-        )(got_force, g3, velocity, partial, emf_below, emf_above)
-    )
+    (updated,) = call(
+        functools.partial(widen_kernel, p),
+        [VMEM] * 3,
+        [(struct(*velocity.shape), HBM)],
+        [pltpu.VMEM(velocity.shape, F32), dma((3,))],
+    )(got_force, g3, velocity)
+    (finished,) = call(
+        functools.partial(finish_kernel, p), [VMEM] * 4, [(struct(*magnetic.shape), VMEM)]
+    )(got_force, partial, emf_below, emf_above)
+    return updated, finished
 
 
 def solution(mesh):

time: 34.1 us -> 33.6 us (0.985)
  waiting for transfers between devices: 7.95 us -> 7.39 us
    ppermute x2, waiting for transfers between devices: 6.97 us -> 3.48 us  [planes(): below = lax.ppermute(up, 'gz', ring('gz', 1))]
    all_to_all x1, waiting for transfers between devices: 0.01 us -> 2.93 us  [body(): got_force = lax.all_to_all(sent, 'xy', 0, 0, tiled=True)]
    pallas_call x1 -> x2, Pallas kernels: 1.53 us -> 2.18 us  [the longest x1 1.46 us: body(): call(functools.partial(widen_kernel, p), [VMEM] * 3, [(struct(*velocity.s...]
  transfers between devices with their start and end apart: 6 -> 6, of which waited for: 3 -> 3; matrix products, arithmetic and copies ran while one was open for 0% -> 0% of each run, Pallas kernels for 1% -> 5%
where the time goes in v6:
time: 33.6 us; the launch traced here: 33.2 us
  starting transfers between devices  17 us (51%)
  waiting for transfers between devices  7.39 us (22%)
  Pallas kernels  6.6 us (20%)
  local copies, waits for them, and re-layouts  1.59 us (5%)
  between operations  0.7 us (2%)
    ppermute x2, starting transfers between devices, planes(): above = lax.ppermute(down, 'gz', ring('gz', -1))  7.41 us
    all_to_all x1, starting transfers between devices, body(): got = lax.all_to_all(sent, 'xy', 0, 0, tiled=True)  5.34 us
    all_to_all x1, starting transfers between devices, body(): got_force = lax.all_to_all(sent, 'xy', 0, 0, tiled=True)  4.2 us
    ppermute x2, waiting for transfers between devices, planes(): below = lax.ppermute(up, 'gz', ring('gz', 1))  3.48 us
    all_to_all x1, waiting for transfers between devices, body(): got_force = lax.all_to_all(sent, 'xy', 0, 0, tiled=True)  2.93 us
    pallas_call x1, Pallas kernels, body(): call(functools.partial(restrict_kernel, p), [HBM] * 3, [(struct(p.n, p.r1...  2.72 us
    unnamed x6, local copies, waits for them, and re-layouts  1.59 us
    pallas_call x1, Pallas kernels, body(): call(functools.partial(widen_kernel, p), [VMEM] * 3, [(struct(*velocity.s...  1.46 us
  transfers between devices with their start and end apart: 6, of which 3 were waited for; matrix products, arithmetic and copies ran while one was open for 0% of the time, Pallas kernels for 5%

profile of v6, /device:TPU:0, one launch (start us, length us, event | category | flops | bytes accessed | tf_op | source)
XLA Modules:
  0.0 33.2 jit_solution(15105017730421721455)
XLA Ops:
  0.6 2.7 %shard_map.50 = (f32[8,40,256]{2,1,0:T(8,128)}, f32[2,16,512]{2,1,0:T(8,128)}, f32[2,16,512]{2,1,0:T(8,128)}) custom-call(f32[3,4,32,1024]{3,2,1,0:T(8,128)} %v_ref.1, s32[1,32]{1,0:T(1,128)} %bitcast.1, f32[3,2,16,512]{3,2,1,0:T(8,128)} %b_ref), custom_call_target="tpu_custom_call" | custom-call | flops 16777216 | bytes 1048576 | tf_op jit(solution)/shard_map/pallas_call | solution.py:429
  3.4 0.0 copy-start
  3.4 5.3 %all-to-all-start = ((f32[8,40,256]{2,1,0:T(8,128)}), f32[8,40,256]{2,1,0:T(8,128)S(1)}, u32[]{:S(2)}, u32[]{:S(2)}) async-start(f32[8,40,256]{2,1,0:T(8,128)} %get-tuple-element.15), calls=%async_computation | async-start | bytes 655360 | tf_op jit(solution)/shard_map/all_to_all | solution.py:444
  8.7 3.6 %collective-permute-start.1 = (f32[2,16,512]{2,1,0:T(8,128)}, f32[2,16,512]{2,1,0:T(8,128)S(1)}, u32[]{:S(2)}, u32[]{:S(2)}) collective-permute-start(f32[2,16,512]{2,1,0:T(8,128)} %get-tuple-element.21), channel_id=1, source_target_pairs={{0,3},{1,0},{2,1},{3,2},{4,7},{5,4},{6,5},{7,6},{8,11},{9,8},{10,9... | collective-permute-start | bytes 196616 | tf_op jit(solution)/shard_map/ppermute | solution.py:420
  12.3 0.0 collective-permute-start
  12.3 0.0 copy-start.1
  12.3 0.9 %copy-done.1 = f32[3,2,16,512]{3,2,1,0:T(8,128)S(1)} copy-done((f32[3,2,16,512]{3,2,1,0:T(8,128)S(1)}, f32[3,2,16,512]{3,2,1,0:T(8,128)}, u32[]{:S(2)}) %copy-start.1) | copy-done | bytes 196632
  13.2 0.0 copy-start.2
  13.2 0.7 %copy-done.2 = s32[32]{0:T(128)S(1)} copy-done((s32[32]{0:T(128)S(1)}, s32[32]{0:T(128)}, u32[]{:S(2)}) %copy-start.2) | copy-done | bytes 152
  13.9 0.2 shard_map.51
  14.1 1.0 %collective-permute-done.1.hi_ref = f32[2,16,512]{2,1,0:T(8,128)S(1)} collective-permute-done((f32[2,16,512]{2,1,0:T(8,128)}, f32[2,16,512]{2,1,0:T(8,128)S(1)}, u32[]{:S(2)}, u32[]{:S(2)}) %collective-permute-start.1) | collective-permute-done | bytes 65568 | tf_op jit(solution)/shard_map/ppermute | solution.py:420
  15.1 3.5 %collective-permute-done.lo_ref = f32[2,16,512]{2,1,0:T(8,128)S(1)} collective-permute-done((f32[2,16,512]{2,1,0:T(8,128)}, f32[2,16,512]{2,1,0:T(8,128)S(1)}, u32[]{:S(2)}, u32[]{:S(2)}) %collective-permute-start) | collective-permute-done | bytes 65568 | tf_op jit(solution)/shard_map/ppermute | solution.py:419
  18.6 0.0 all-to-all-done.r_ref
  18.6 1.3 %shard_map.52 = (f32[8,32,256]{2,1,0:T(8,128)}, f32[3,2,16,512]{3,2,1,0:T(8,128)S(1)}, f32[3,16,512]{2,1,0:T(8,128)S(1)}, f32[3,16,512]{2,1,0:T(8,128)S(1)}) custom-call(f32[8,40,256]{2,1,0:T(8,128)S(1)} %all-to-all-done.r_ref, f32[3,2,16,512]{3,2,1,0:T(8,128)S(1)} %get-tuple-element.19.b_ref, f32[3,2,16,512]{3,2,1,0:T(8,128)S(1)} %get-tuple-element.20.j_ref, ...), custom_call_target="tpu_custom_call" | custom-call | flops 16777216 | bytes 1048576 | tf_op jit(solution)/shard_map/pallas_call | solution.py:452
  19.9 4.2 %all-to-all-start.1 = ((f32[8,32,256]{2,1,0:T(8,128)}), f32[8,32,256]{2,1,0:T(8,128)S(1)}, u32[]{:S(2)}, u32[]{:S(2)}) async-start(f32[8,32,256]{2,1,0:T(8,128)} %get-tuple-element.22), calls=%async_computation.1 | async-start | bytes 524288 | tf_op jit(solution)/shard_map/all_to_all | solution.py:463
  24.1 0.0 collective-permute-start.2
  24.1 3.8 %collective-permute-start.3 = (f32[3,16,512]{2,1,0:T(8,128)S(1)}, f32[3,16,512]{2,1,0:T(8,128)S(1)}, u32[]{:S(2)}, u32[]{:S(2)}) collective-permute-start(f32[3,16,512]{2,1,0:T(8,128)S(1)} %get-tuple-element.27), channel_id=1, source_target_pairs={{0,3},{1,0},{2,1},{3,2},{4,7},{5,4},{6,5},{7,6},{8,11},{9,8},{10,9... | collective-permute-start | bytes 294920 | tf_op jit(solution)/shard_map/ppermute | solution.py:420
  28.0 0.1 shard_map.54.n_ref
  28.1 2.9 %all-to-all-done.1.r_ref = f32[8,32,256]{2,1,0:T(8,128)S(1)} async-done(((f32[8,32,256]{2,1,0:T(8,128)}), f32[8,32,256]{2,1,0:T(8,128)S(1)}, u32[]{:S(2)}, u32[]{:S(2)}) %all-to-all-start.1) | async-done | bytes 262176 | tf_op jit(solution)/shard_map/all_to_all | solution.py:463
  31.0 0.0 copy-done
  31.0 1.5 %shard_map.53 = f32[3,4,32,1024]{3,2,1,0:T(8,128)} custom-call(f32[8,32,256]{2,1,0:T(8,128)S(1)} %all-to-all-done.1.r_ref, bf16[64,64]{1,0:T(8,128)(2,1)S(1)} %get-tuple-element.23.g_ref, f32[3,4,32,1024]{3,2,1,0:T(8,128)S(1)} %copy-done), custom_call_target="tpu_custom_call" | custom-call | flops 16777216 | bytes 1048576 | tf_op jit(solution)/shard_map/pallas_call | solution.py:468
  32.5 0.0 collective-permute-done.2.lo_ref
  32.5 0.0 collective-permute-done.3.hi_ref
  32.5 0.7 %shard_map.55 = f32[3,2,16,512]{3,2,1,0:T(8,128)} custom-call(f32[8,32,256]{2,1,0:T(8,128)S(1)} %all-to-all-done.1.r_ref, f32[3,2,16,512]{3,2,1,0:T(8,128)S(1)} %shard_map.54.n_ref, f32[3,16,512]{2,1,0:T(8,128)S(1)} %collective-permute-done.2.lo_ref, f32[3,16,512]{2,1,0:T(8,128)S(1)} %collective-permute-done.3.hi_ref), custom_call_target="tpu_custom_call" | custom-call | flops 16777216 | bytes 1048576 | tf_op jit(solution)/shard_map/pallas_call | solution.py:474
Async XLA Ops:
  3.4 27.7 %copy-start = (f32[3,4,32,1024]{3,2,1,0:T(8,128)S(1)}, f32[3,4,32,1024]{3,2,1,0:T(8,128)}, u32[]{:S(2)}) copy-start(f32[3,4,32,1024]{3,2,1,0:T(8,128)} %v_ref.1) | copy-start | bytes 4718596
  3.4 15.2 %all-to-all-start = ((f32[8,40,256]{2,1,0:T(8,128)}), f32[8,40,256]{2,1,0:T(8,128)S(1)}, u32[]{:S(2)}, u32[]{:S(2)}) async-start(f32[8,40,256]{2,1,0:T(8,128)} %get-tuple-element.15), calls=%async_computation | async-start | bytes 655360 | tf_op jit(solution)/shard_map/all_to_all | solution.py:444
  8.7 6.4 %collective-permute-start.1 = (f32[2,16,512]{2,1,0:T(8,128)}, f32[2,16,512]{2,1,0:T(8,128)S(1)}, u32[]{:S(2)}, u32[]{:S(2)}) collective-permute-start(f32[2,16,512]{2,1,0:T(8,128)} %get-tuple-element.21), channel_id=1, source_target_pairs={{0,3},{1,0},{2,1},{3,2},{4,7},{5,4},{6,5},{7,6},{8,11},{9,8},{10,9... | collective-permute-start | bytes 196616 | tf_op jit(solution)/shard_map/ppermute | solution.py:420
  12.3 6.3 %collective-permute-start = (f32[2,16,512]{2,1,0:T(8,128)}, f32[2,16,512]{2,1,0:T(8,128)S(1)}, u32[]{:S(2)}, u32[]{:S(2)}) collective-permute-start(f32[2,16,512]{2,1,0:T(8,128)} %get-tuple-element.16), channel_id=1, source_target_pairs={{0,1},{1,2},{2,3},{3,0},{4,5},{5,6},{6,7},{7,4},{8,9},{9,10},{10,1... | collective-permute-start | bytes 196616 | tf_op jit(solution)/shard_map/ppermute | solution.py:419
  12.3 0.9 %copy-start.1 = (f32[3,2,16,512]{3,2,1,0:T(8,128)S(1)}, f32[3,2,16,512]{3,2,1,0:T(8,128)}, u32[]{:S(2)}) copy-start(f32[3,2,16,512]{3,2,1,0:T(8,128)} %b_ref) | copy-start | bytes 589828
  13.2 0.7 %copy-start.2 = (s32[32]{0:T(128)S(1)}, s32[32]{0:T(128)}, u32[]{:S(2)}) copy-start(s32[32]{0:T(128)} %param.5) | copy-start | bytes 388
  19.9 11.1 %all-to-all-start.1 = ((f32[8,32,256]{2,1,0:T(8,128)}), f32[8,32,256]{2,1,0:T(8,128)S(1)}, u32[]{:S(2)}, u32[]{:S(2)}) async-start(f32[8,32,256]{2,1,0:T(8,128)} %get-tuple-element.22), calls=%async_computation.1 | async-start | bytes 524288 | tf_op jit(solution)/shard_map/all_to_all | solution.py:463
  24.1 8.4 %collective-permute-start.2 = (f32[3,16,512]{2,1,0:T(8,128)S(1)}, f32[3,16,512]{2,1,0:T(8,128)S(1)}, u32[]{:S(2)}, u32[]{:S(2)}) collective-permute-start(f32[3,16,512]{2,1,0:T(8,128)S(1)} %get-tuple-element.26), channel_id=1, source_target_pairs={{0,1},{1,2},{2,3},{3,0},{4,5},{5,6},{6,7},{7,4},{8,9},{9,10},{10,1... | collective-permute-start | bytes 294920 | tf_op jit(solution)/shard_map/ppermute | solution.py:419
  24.1 8.4 %collective-permute-start.3 = (f32[3,16,512]{2,1,0:T(8,128)S(1)}, f32[3,16,512]{2,1,0:T(8,128)S(1)}, u32[]{:S(2)}, u32[]{:S(2)}) collective-permute-start(f32[3,16,512]{2,1,0:T(8,128)S(1)} %get-tuple-element.27), channel_id=1, source_target_pairs={{0,3},{1,0},{2,1},{3,2},{4,7},{5,4},{6,5},{7,6},{8,11},{9,8},{10,9... | collective-permute-start | bytes 294920 | tf_op jit(solution)/shard_map/ppermute | solution.py:420

commit v7 on v6

--- a/solution.py
+++ b/solution.py
@@ -50,11 +50,8 @@
         self.rc = -(-self.zc * self.k // 8) * 8
         self.ru = 3 * self.rc
         self.rows = n * self.rc
-        self.rb = 3 * self.zc * self.nx // self.area
-        self.r1 = -(-(self.ru + self.rb + 1) // 8) * 8
-        self.re = 2 * self.zc * self.nx // self.area
-        self.r2 = -(-(self.ru + self.re) // 8) * 8
-        self.wrap = self.nx // self.area
+        self.r1 = self.ru + 8
+        self.ry = -(-3 * self.zc // 8) * 8
 
 
 def mirror(i):
@@ -73,27 +70,24 @@
 
 
 def select(g, x):
-    hi, lo = split(x)
-    out = dot(g, jnp.concatenate([hi, lo], axis=1))
-    return out[:, : x.shape[1]] + out[:, x.shape[1] :]
-
-
-def lane_route(p):
-    lane = iota((1, 1, p.rows), 2)
+    return dot(g, jnp.concatenate(split(x), axis=0))
+
+
+def lane_route(p, times=1):
+    lane = iota((1, 1, times * p.rows), 2)
     i = lane & (p.rc - 1)
-    return lane >> log2(p.rc), i >> log2(p.k), i & (p.k - 1)
-
-
-def restrict_kernel(p, v_hbm, t_hbm, b_hbm, out_hbm, up_hbm, down_hbm, v_ref, t_ref, b_ref, out, last, first, sems):
+    return (lane >> log2(p.rc)) & (p.n - 1), i >> log2(p.k), i & (p.k - 1)
+
+
+def restrict_kernel(p, v_hbm, t_hbm, b_hbm, out_hbm, up_hbm, down_hbm, last_hbm, first_hbm, v_ref, t_ref, b_ref, out, last, first, sems):
     n, k, s, zc = p.n, p.k, p.slots, p.zc
-    me = lax.axis_index("xy")
     t_copy = pltpu.make_async_copy(t_hbm, t_ref, sems.at[0])
     b_copy = pltpu.make_async_copy(b_hbm, b_ref, sems.at[1])
     v_copies = [pltpu.make_async_copy(v_hbm.at[c], v_ref.at[c], sems.at[2 + c]) for c in range(3)]
     t_copy.start()
-    b_copy.start()
     for copy in v_copies:
         copy.start()
+    b_copy.start()
     half_fine = p.edge * p.edge // 2
     half_area = p.area // 2
     f, c = iota((half_fine, half_area), 0), iota((half_fine, half_area), 1)
@@ -103,13 +97,13 @@
     t_copy.wait()
     table = t_ref[...]
     q, _ = send_positions(p, table)
-    lanes = zc * s
+    lanes = 2 * zc * s
     rep = one_hot((iota((s, lanes), 1) & (s - 1)) == iota((s, lanes), 0))
     qt = dot(jnp.broadcast_to(q, (8, s)).astype(BF16), rep)[0:1]
     shape = (n, p.rc, lanes)
     i = iota(shape, 1)
     target = (iota(shape, 0) * k + (i & (k - 1))).astype(F32)
-    g = one_hot(((i >> log2(k)) == (iota(shape, 2) >> log2(s))) & (target == qt.reshape(1, 1, lanes)))
+    g = one_hot(((i >> log2(k)) == ((iota(shape, 2) >> log2(s)) & (zc - 1))) & (target == qt.reshape(1, 1, lanes)))
     g = g.reshape(p.rows, lanes)
     col = jnp.broadcast_to((table & (p.bcols - 1)).astype(F32), (s, s))
     qi = iota((s, s), 0).astype(F32)
@@ -118,9 +112,19 @@
     spread = jnp.where((qa & (k - 1)) == (la & (k - 1)), col_q, 0.0).astype(BF16)
     gather = one_hot((iota((n, s), 1) >> log2(k)) == iota((n, s), 0))
     cols = dot(gather, spread)
-    at = p.ru + p.rb
     for r in range(n):
-        out[r, at : at + 1, :] = cols[r : r + 1]
+        out[r, p.ru : p.ru + 1, :] = cols[r : r + 1]
+    averages = []
+    m = zc * s
+    ws = [slice(h * half_fine, (h + 1) * half_fine) for h in range(2)]
+    for c in range(3):
+        v_copies[c].wait()
+        u = []
+        for w in ws:
+            z_sum = [v_ref[c, 2 * z, :, w] + v_ref[c, 2 * z + 1, :, w] for z in range(zc)]
+            o = dot(jnp.concatenate(split(jnp.concatenate(z_sum, axis=0)), axis=0), sel)
+            u.append(o[:m] + o[m:])
+        averages.append(jnp.concatenate(u, axis=1) * 0.125)
     b_copy.wait()
     sends = [
         pltpu.make_async_copy(b_ref.at[0:2, zc - 1], up_hbm, sems.at[5]),
@@ -128,28 +132,15 @@
     ]
     for c in range(3):
         for z in range(zc):
-            for h in range(p.wrap):
-                at = (c * zc + z) * p.wrap + h
-                w = slice(h * p.area, (h + 1) * p.area)
-                last[at : at + 1, :] = b_ref[c, z, p.ny - 1 : p.ny, w]
-                first[at : at + 1, :] = b_ref[c, z, 0:1, w]
-    nxt = lax.rem(me + 1, n)
-    for r in range(n):
-        out[r, p.ru : p.ru + p.rb, :] = jnp.where(r == nxt, last[: p.rb], first[: p.rb])
+            at = c * zc + z
+            last[at : at + 1, :] = b_ref[c, z, p.ny - 1 : p.ny, :]
+            first[at : at + 1, :] = b_ref[c, z, 0:1, :]
+    sends.append(pltpu.make_async_copy(last, last_hbm, sems.at[11]))
+    sends.append(pltpu.make_async_copy(first, first_hbm, sems.at[12]))
     tail = pl.ds(p.ru, p.r1 - p.ru)
     sends.append(pltpu.make_async_copy(out.at[:, tail, :], out_hbm.at[:, tail, :], sems.at[7]))
     for send in sends:
         send.start()
-    averages = []
-    m = zc * s
-    ws = [slice(h * half_fine, (h + 1) * half_fine) for h in range(2)]
-    for c in range(3):
-        v_copies[c].wait()
-        z_sum = jnp.concatenate([v_ref[c, 2 * z] + v_ref[c, 2 * z + 1] for z in range(zc)], axis=0)
-        hi, lo = split(z_sum)
-        o = dot(jnp.concatenate([x[:, w] for w in ws for x in (hi, lo)], axis=0), sel)
-        u = [o[2 * h * m : (2 * h + 1) * m] + o[(2 * h + 1) * m : (2 * h + 2) * m] for h in range(2)]
-        averages.append(jnp.concatenate(u, axis=1) * 0.125)
     for c in range(3):
         out[:, c * p.rc : (c + 1) * p.rc, :] = select(g, averages[c]).reshape(n, p.rc, p.area)
         rows = pl.ds(c * p.rc, p.rc)
@@ -211,10 +202,6 @@
 
 def y_prev(f, halo):
     return jnp.where(iota(f.shape, 0) == 0, halo, pltpu.roll(f, 1, 0))
-
-
-def row_of(p, ref, src, at):
-    return jnp.concatenate([ref[src, pl.ds(at + h, 1), :] for h in range(p.wrap)], axis=1)
 
 
 def interior_kernel(p, b_ref, t_ref, copy_ref, j_ref, next_ref, g3_ref):
@@ -240,35 +227,33 @@
             copy_ref[c, z] = b[c]
 
 
-def edge_rows(p, ref, nxt, prv, at):
+def edge_rows(p, n_ref, s_ref, at):
     y = iota((p.ny, p.nx), 0)
-    north = jnp.where(y == p.ny - 1, row_of(p, ref, nxt, at), 0.0)
-    return north, jnp.where(y == 0, row_of(p, ref, prv, at), 0.0)
-
-
-def field_kernel(p, r_ref, b_ref, j_ref, lo_ref, hi_ref, out, e_ref, up_ref, down_ref, e_rows):
+    north = jnp.where(y == p.ny - 1, n_ref[at : at + 1, :], 0.0)
+    return north, jnp.where(y == 0, s_ref[at : at + 1, :], 0.0)
+
+
+def field_kernel(p, r_ref, b_ref, j_ref, lo_ref, hi_ref, n_ref, s_ref, out, e_ref, up_ref, down_ref, last, first):
     n, k, zc = p.n, p.k, p.zc
-    me = lax.axis_index("xy")
-    nxt, prv = lax.rem(me + 1, n), lax.rem(me + n - 1, n)
     b = [[b_ref[c, z] for z in range(zc)] for c in range(3)]
-    cols = r_ref[:, p.ru + p.rb, :]
+    cols = r_ref[:, p.ru, :]
     shape = (n, p.rc, 128)
     col_s = jnp.sum(
         jnp.where((iota(shape, 1) & (k - 1)) == iota(shape, 2), cols[:, None, :128], 0.0), axis=2, keepdims=True
     )
-    shape = (n, p.rc, zc * p.bcols)
+    shape = (n, p.rc, 2 * zc * p.bcols)
     lane = iota(shape, 2)
     g = one_hot(
-        ((iota(shape, 1) >> log2(k)) == (lane >> log2(p.bcols)))
+        ((iota(shape, 1) >> log2(k)) == ((lane >> log2(p.bcols)) & (zc - 1)))
         & (col_s == mirror(lane & (p.bcols - 1)).astype(F32))
-    ).reshape(p.rows, zc * p.bcols)
+    ).reshape(p.rows, 2 * zc * p.bcols)
     force = []
     zero = jnp.zeros((p.ny, p.nx), F32)
     for z in range(zc):
         bz = [b[c][z] for c in range(3)]
         dy = {}
         for c in (0, 2):
-            north, south = edge_rows(p, r_ref, nxt, prv, p.ru + (c * zc + z) * p.wrap)
+            north, south = edge_rows(p, n_ref, s_ref, c * zc + z)
             dy[c] = north - south
         dz = [zero, zero]
         for c in range(2):
@@ -283,15 +268,18 @@
     for c in range(3):
         f_blk = jnp.concatenate([grid_to_blocks(p, force[z][c]) for z in range(zc)], axis=0)
         out[:, c * p.rc : (c + 1) * p.rc, :] = select(g, f_blk).reshape(n, p.rc, p.area)
-    p_l, z_l, _ = lane_route(p)
-    shape = (n, p.rows)
+    times = 2 if 2 * p.rows <= p.area else 1
+    width = times * p.rows
+    p_l, z_l, _ = lane_route(p, times)
+    shape = (n, width)
     col_l = jnp.sum(
-        jnp.where(iota(shape, 0) == p_l.reshape(1, p.rows), cols[:, : p.rows], 0.0), axis=0, keepdims=True
+        jnp.where(iota(shape, 0) == p_l.reshape(1, width), cols[:, :width], 0.0), axis=0, keepdims=True
     )
-    shape = (zc, p.bcols, p.rows)
+    shape = (zc, p.bcols, width)
     g = one_hot(
-        (iota(shape, 0) == z_l) & (iota(shape, 1).astype(F32) == col_l.reshape(1, 1, p.rows))
-    ).reshape(zc * p.bcols, p.rows)
+        (iota(shape, 0) == z_l) & (iota(shape, 1).astype(F32) == col_l.reshape(1, 1, width))
+    ).reshape(zc * p.bcols, width)
+    g = jnp.concatenate([g] * (2 // times), axis=1)
     u = []
     for c in range(3):
         blk = select(g, r_ref[:, c * p.rc : (c + 1) * p.rc, :].reshape(p.rows, p.area))
@@ -306,19 +294,13 @@
         if z == 0:
             down_ref[0], down_ref[1], down_ref[2] = ez[0], ez[1], bz[2]
         for i, c in enumerate((0, 2)):
-            for h in range(p.wrap):
-                at = (i * zc + z) * p.wrap + h
-                w = slice(h * p.area, (h + 1) * p.area)
-                e_rows[0, at : at + 1, :] = ez[c][0:1, w]
-                e_rows[1, at : at + 1, :] = ez[c][p.ny - 1 : p.ny, w]
-    for r in range(n):
-        out[r, p.ru : p.ru + p.re, :] = jnp.where(r == nxt, e_rows[1], e_rows[0])
-
-
-def local_kernel(p, r_ref, b_ref, lo_ref, hi_ref, e_ref, next_ref):
-    n, zc = p.n, p.zc
-    me = lax.axis_index("xy")
-    nxt, prv = lax.rem(me + 1, n), lax.rem(me + n - 1, n)
+            at = i * zc + z
+            first[at : at + 1, :] = ez[c][0:1]
+            last[at : at + 1, :] = ez[c][p.ny - 1 : p.ny]
+
+
+def local_kernel(p, b_ref, lo_ref, hi_ref, n_ref, s_ref, e_ref, next_ref):
+    zc = p.zc
     zero = jnp.zeros((p.ny, p.nx), F32)
     for z in range(zc):
         e = [e_ref[c, z] for c in range(3)]
@@ -330,7 +312,7 @@
             (x_next(e[1]) - x_prev(e[1])) - (y_next(e[0], 0.0) - y_prev(e[0], 0.0)),
         ]
         for c in range(3):
-            north, south = edge_rows(p, r_ref, nxt, prv, p.ru + (c * zc + z) * p.wrap)
+            north, south = edge_rows(p, n_ref, s_ref, c * zc + z)
             total = curl[c] + north + south
             if c < 2 and z == 0:
                 total = total + lo_ref[c]
@@ -371,13 +353,11 @@
         copy.wait()
 
 
-def finish_kernel(p, r_ref, n_ref, lo_ref, hi_ref, mag):
-    n, zc = p.n, p.zc
-    me = lax.axis_index("xy")
-    nxt, prv = lax.rem(me + 1, n), lax.rem(me + n - 1, n)
+def finish_kernel(p, m_ref, lo_ref, hi_ref, n_ref, s_ref, mag):
+    zc = p.zc
 
     def dy(i, z):
-        north, south = edge_rows(p, r_ref, nxt, prv, p.ru + (i * zc + z) * p.wrap)
+        north, south = edge_rows(p, n_ref, s_ref, i * zc + z)
         return north - south
 
     for z in range(zc):
@@ -389,9 +369,9 @@
         if z == 0:
             dz = [dz[c] - lo_ref[c] for c in range(2)]
             outer = outer + lo_ref[2]
-        mag[0, z] = n_ref[0, z] + 0.05 * (dy(1, z) - dz[1])
-        mag[1, z] = n_ref[1, z] + 0.05 * dz[0]
-        mag[2, z] = n_ref[2, z] + 0.05 * (outer - dy(0, z))
+        mag[0, z] = m_ref[0, z] + 0.05 * (dy(1, z) - dz[1])
+        mag[1, z] = m_ref[1, z] + 0.05 * dz[0]
+        mag[2, z] = m_ref[2, z] + 0.05 * (outer - dy(0, z))
 
 
 def struct(*shape, dtype=F32):
@@ -415,10 +395,12 @@
     return [(i, (i + step) % n) for i in range(n)]
 
 
-def planes(up, down):
+def exchange(up, down, last, first):
     below = lax.ppermute(up, "gz", ring("gz", 1))
     above = lax.ppermute(down, "gz", ring("gz", -1))
-    return below, above
+    south = lax.ppermute(last, "xy", ring("xy", 1))
+    north = lax.ppermute(first, "xy", ring("xy", -1))
+    return below, above, north, south
 
 
 def body(velocity, magnetic, slot_block_table):
@@ -426,54 +408,51 @@
     plane = (p.ny, p.nx)
     dma = pltpu.SemaphoreType.DMA
     table = slot_block_table.reshape(1, p.slots)
-    sent, up, down = call(
+    sent, up, down, last, first = call(
         functools.partial(restrict_kernel, p),
         [HBM] * 3,
-        [(struct(p.n, p.r1, p.area), HBM), (struct(2, *plane), HBM), (struct(2, *plane), HBM)],
+        [(struct(p.n, p.r1, p.area), HBM)] + [(struct(2, *plane), HBM)] * 2 + [(struct(p.ry, p.nx), HBM)] * 2,
         [
             pltpu.VMEM(velocity.shape, F32),
             pltpu.VMEM((1, p.slots), jnp.int32),
             pltpu.VMEM(magnetic.shape, F32),
             pltpu.VMEM((p.n, p.r1, p.area), F32),
-            pltpu.VMEM((-(-p.rb // 8) * 8, p.area), F32),
-            pltpu.VMEM((-(-p.rb // 8) * 8, p.area), F32),
-            dma((11,)),
+            pltpu.VMEM((p.ry, p.nx), F32),
+            pltpu.VMEM((p.ry, p.nx), F32),
+            dma((13,)),
         ],
         ALL_VMEM,
     )(velocity, table, magnetic)
     got = lax.all_to_all(sent, "xy", 0, 0, tiled=True)
-    below, above = planes(up, down)
+    below, above, north, south = exchange(up, down, last, first)
     held, held_table, _ = lax.optimization_barrier((magnetic, table, up))
     field, current, diffused, g3 = call(
         functools.partial(interior_kernel, p),
         [VMEM] * 2,
         [(struct(*magnetic.shape), VMEM)] * 3 + [(struct(p.zc * p.slots, p.rows, dtype=BF16), VMEM)],
     )(held, held_table)
-    sent, emf, up, down = call(
+    sent, emf, up, down, last, first = call(
         functools.partial(field_kernel, p),
-        [VMEM] * 5,
-        [
-            (struct(p.n, p.r2, p.area), VMEM),
-            (struct(*magnetic.shape), VMEM),
-            (struct(3, *plane), VMEM),
-            (struct(3, *plane), VMEM),
-        ],
-        [pltpu.VMEM((2, p.re, p.area), F32)],
-    )(got, field, current, below, above)
+        [VMEM] * 7,
+        [(struct(p.n, p.ru, p.area), VMEM), (struct(*magnetic.shape), VMEM)]
+        + [(struct(3, *plane), VMEM)] * 2
+        + [(struct(p.ry, p.nx), VMEM)] * 2,
+    )(got, field, current, below, above, north, south)
     got_force = lax.all_to_all(sent, "xy", 0, 0, tiled=True)
-    emf_below, emf_above = planes(up, down)
+    outer = exchange(up, down, last, first)
     (partial,) = call(
-        functools.partial(local_kernel, p), [VMEM] * 5, [(struct(*magnetic.shape), VMEM)]
-    )(got, diffused, below, above, emf)
+        functools.partial(local_kernel, p), [VMEM] * 6, [(struct(*magnetic.shape), VMEM)]
+    )(diffused, below, above, north, south, emf)
     (updated,) = call(
         functools.partial(widen_kernel, p),
         [VMEM] * 3,
         [(struct(*velocity.shape), HBM)],
         [pltpu.VMEM(velocity.shape, F32), dma((3,))],
     )(got_force, g3, velocity)
+    partial, _ = lax.optimization_barrier((partial, updated))
     (finished,) = call(
-        functools.partial(finish_kernel, p), [VMEM] * 4, [(struct(*magnetic.shape), VMEM)]
-    )(got_force, partial, emf_below, emf_above)
+        functools.partial(finish_kernel, p), [VMEM] * 5, [(struct(*magnetic.shape), VMEM)]
+    )(partial, *outer)
     return updated, finished
 
 

time: 33.6 us -> 34.9 us (1.039)
  starting transfers between devices: 17 us -> 21 us
  waiting for transfers between devices: 7.39 us -> 4.89 us
    ppermute x4 -> x8, starting transfers between devices: 7.42 us -> 11.9 us  [the longest x2 7.42 us: exchange(): above = lax.ppermute(down, 'gz', ring('gz', -1))]
    all_to_all x1, waiting for transfers between devices: 2.93 us -> 0.14 us  [body(): got_force = lax.all_to_all(sent, 'xy', 0, 0, tiled=True)]
    all_to_all x1, starting transfers between devices: 4.2 us -> 3.82 us  [body(): got_force = lax.all_to_all(sent, 'xy', 0, 0, tiled=True)]
    ppermute x4 -> x8, waiting for transfers between devices: 4.46 us -> 4.75 us  [the longest x2 4.73 us: exchange(): south = lax.ppermute(last, 'xy', ring('xy', 1))]
  transfers between devices with their start and end apart: 6 -> 10, of which waited for: 3 -> 3; matrix products, arithmetic and copies ran while one was open for 0% -> 0% of each run, Pallas kernels for 5% -> 5%
where the time goes in v7:
time: 34.9 us; the launch traced here: 34.6 us
  starting transfers between devices  21 us (60%)
  Pallas kernels  6.33 us (18%)
  waiting for transfers between devices  4.89 us (14%)
  local copies, waits for them, and re-layouts  1.59 us (5%)
  between operations  0.71 us (2%)
    ppermute x2, starting transfers between devices, exchange(): above = lax.ppermute(down, 'gz', ring('gz', -1))  7.42 us
    all_to_all x1, starting transfers between devices, body(): got = lax.all_to_all(sent, 'xy', 0, 0, tiled=True)  5.34 us
    ppermute x2, waiting for transfers between devices, exchange(): south = lax.ppermute(last, 'xy', ring('xy', 1))  4.73 us
    ppermute x2, starting transfers between devices, exchange(): north = lax.ppermute(first, 'xy', ring('xy', -1))  4.45 us
    all_to_all x1, starting transfers between devices, body(): got_force = lax.all_to_all(sent, 'xy', 0, 0, tiled=True)  3.82 us
    pallas_call x1, Pallas kernels, body(): call(functools.partial(restrict_kernel, p), [HBM] * 3, [(struct(p.n, p.r1...  2.67 us
    unnamed x6, local copies, waits for them, and re-layouts  1.59 us
    pallas_call x1, Pallas kernels, body(): call(functools.partial(widen_kernel, p), [VMEM] * 3, [(struct(*velocity.s...  1.46 us
  transfers between devices with their start and end apart: 10, of which 3 were waited for; matrix products, arithmetic and copies ran while one was open for 0% of the time, Pallas kernels for 5%

profile of v7, /device:TPU:0, one launch (start us, length us, event | category | flops | bytes accessed | tf_op | source)
XLA Modules:
  0.0 34.6 jit_solution(6466164462742946066)
XLA Ops:
  0.6 2.7 %shard_map.50 = (f32[8,32,256]{2,1,0:T(8,128)}, f32[2,16,512]{2,1,0:T(8,128)}, f32[2,16,512]{2,1,0:T(8,128)}, f32[8,512]{1,0:T(8,128)}, f32[8,512]{1,0:T(8,128)}) custom-call(f32[3,4,32,1024]{3,2,1,0:T(8,128)} %v_ref.1, s32[1,32]{1,0:T(1,128)} %bitcast.1, f32[3,2,16,512]{3,2,1,0:T(8,128)} %b_ref), custom_call_target="tpu_custom_call" | custom-call | flops 16777216 | bytes 1048576 | tf_op jit(solution)/shard_map/pallas_call | solution.py:411
  3.3 0.0 copy-start
  3.3 5.3 %all-to-all-start = ((f32[8,32,256]{2,1,0:T(8,128)}), f32[8,32,256]{2,1,0:T(8,128)S(1)}, u32[]{:S(2)}, u32[]{:S(2)}) async-start(f32[8,32,256]{2,1,0:T(8,128)} %get-tuple-element.20), calls=%async_computation | async-start | bytes 524288 | tf_op jit(solution)/shard_map/all_to_all | solution.py:426
  8.7 3.6 %collective-permute-start.1 = (f32[2,16,512]{2,1,0:T(8,128)}, f32[2,16,512]{2,1,0:T(8,128)S(1)}, u32[]{:S(2)}, u32[]{:S(2)}) collective-permute-start(f32[2,16,512]{2,1,0:T(8,128)} %get-tuple-element.26), channel_id=1, source_target_pairs={{0,3},{1,0},{2,1},{3,2},{4,7},{5,4},{6,5},{7,6},{8,11},{9,8},{10,9... | collective-permute-start | bytes 196616 | tf_op jit(solution)/shard_map/ppermute | solution.py:400
  12.3 0.0 collective-permute-start
  12.3 2.4 %collective-permute-start.2 = (f32[8,512]{1,0:T(8,128)}, f32[8,512]{1,0:T(8,128)S(1)}, u32[]{:S(2)}, u32[]{:S(2)}) collective-permute-start(f32[8,512]{1,0:T(8,128)} %get-tuple-element.27), channel_id=1, source_target_pairs={{0,28},{4,0},{8,4},{12,8},{16,12},{20,16},{24,20},{28,24},{1,29},{... | collective-permute-start | bytes 49160 | tf_op jit(solution)/shard_map/ppermute | solution.py:402
  14.6 0.0 collective-permute-start.3
  14.6 0.9 %copy-done.1 = f32[3,2,16,512]{3,2,1,0:T(8,128)S(1)} copy-done((f32[3,2,16,512]{3,2,1,0:T(8,128)S(1)}, f32[3,2,16,512]{3,2,1,0:T(8,128)}, u32[]{:S(2)}) %copy-start.1) | copy-done | bytes 196632
  15.6 0.7 %copy-done.2 = s32[32]{0:T(128)S(1)} copy-done((s32[32]{0:T(128)S(1)}, s32[32]{0:T(128)}, u32[]{:S(2)}) %copy-start.2) | copy-done | bytes 152
  16.2 0.2 shard_map.51
  16.5 2.4 %collective-permute-done.3.s_ref = f32[8,512]{1,0:T(8,128)S(1)} collective-permute-done((f32[8,512]{1,0:T(8,128)}, f32[8,512]{1,0:T(8,128)S(1)}, u32[]{:S(2)}, u32[]{:S(2)}) %collective-permute-start.3) | collective-permute-done | bytes 16416 | tf_op jit(solution)/shard_map/ppermute | solution.py:401
  18.9 0.0 collective-permute-done.1.hi_ref
  18.9 1.1 %shard_map.52 = (f32[8,24,256]{2,1,0:T(8,128)}, f32[3,2,16,512]{3,2,1,0:T(8,128)S(1)}, f32[3,16,512]{2,1,0:T(8,128)S(1)}, f32[3,16,512]{2,1,0:T(8,128)S(1)}, f32[8,512]{1,0:T(8,128)S(1)}, /*index=5*/f32[8,512]{1,0:T(8,128)S(1)}) custom-call(f32[8,32,256]{2,1,0:T(8,128)S(1)} %all-to-all-done.r_ref, f32[3,2,16,512]{3,2,1,0:T(8,128)S(1)} %get-tuple-element.24.b_ref, ...), custom_call_target="tpu_custom_call" | custom-call | flops 16777216 | bytes 1048576 | tf_op jit(solution)/shard_map/pallas_call | solution.py:434
  20.0 3.8 %all-to-all-start.1 = ((f32[8,24,256]{2,1,0:T(8,128)}), f32[8,24,256]{2,1,0:T(8,128)S(1)}, u32[]{:S(2)}, u32[]{:S(2)}) async-start(f32[8,24,256]{2,1,0:T(8,128)} %get-tuple-element.29), calls=%async_computation.1 | async-start | bytes 393216 | tf_op jit(solution)/shard_map/all_to_all | solution.py:441
  23.9 3.8 %collective-permute-start.5 = (f32[3,16,512]{2,1,0:T(8,128)S(1)}, f32[3,16,512]{2,1,0:T(8,128)S(1)}, u32[]{:S(2)}, u32[]{:S(2)}) collective-permute-start(f32[3,16,512]{2,1,0:T(8,128)S(1)} %get-tuple-element.35), channel_id=1, source_target_pairs={{0,3},{1,0},{2,1},{3,2},{4,7},{5,4},{6,5},{7,6},{8,11},{9,8},{10,9... | collective-permute-start | bytes 294920 | tf_op jit(solution)/shard_map/ppermute | solution.py:400
  27.7 2.1 %collective-permute-start.6 = (f32[8,512]{1,0:T(8,128)S(1)}, f32[8,512]{1,0:T(8,128)S(1)}, u32[]{:S(2)}, u32[]{:S(2)}) collective-permute-start(f32[8,512]{1,0:T(8,128)S(1)} %get-tuple-element.36), channel_id=1, source_target_pairs={{0,28},{4,0},{8,4},{12,8},{16,12},{20,16},{24,20},{28,24},{1,29},{... | collective-permute-start | bytes 49160 | tf_op jit(solution)/shard_map/ppermute | solution.py:402
  29.8 0.1 shard_map.54.m_ref
  29.9 0.1 all-to-all-done.1.r_ref
  30.1 1.5 %shard_map.53 = f32[3,4,32,1024]{3,2,1,0:T(8,128)} custom-call(f32[8,24,256]{2,1,0:T(8,128)S(1)} %all-to-all-done.1.r_ref, bf16[64,64]{1,0:T(8,128)(2,1)S(1)} %get-tuple-element.30.g_ref, f32[3,4,32,1024]{3,2,1,0:T(8,128)S(1)} %copy-done), custom_call_target="tpu_custom_call" | custom-call | flops 16777216 | bytes 1048576 | tf_op jit(solution)/shard_map/pallas_call | solution.py:446
  31.5 0.0 collective-permute-done.6.n_ref
  31.5 2.3 %collective-permute-done.7.s_ref = f32[8,512]{1,0:T(8,128)S(1)} collective-permute-done((f32[8,512]{1,0:T(8,128)S(1)}, f32[8,512]{1,0:T(8,128)S(1)}, u32[]{:S(2)}, u32[]{:S(2)}) %collective-permute-start.7) | collective-permute-done | bytes 16416 | tf_op jit(solution)/shard_map/ppermute | solution.py:401
  33.8 0.0 collective-permute-done.4.lo_ref
  33.8 0.0 collective-permute-done.5.hi_ref
  33.8 0.7 %shard_map.55 = f32[3,2,16,512]{3,2,1,0:T(8,128)} custom-call(f32[3,2,16,512]{3,2,1,0:T(8,128)S(1)} %shard_map.54.m_ref, f32[3,16,512]{2,1,0:T(8,128)S(1)} %collective-permute-done.4.lo_ref, f32[3,16,512]{2,1,0:T(8,128)S(1)} %collective-permute-done.5.hi_ref, f32[8,512]{1,0:T(8,128)S(1)} %collective-permute-done.6.n_ref, ...), custom_call_target="tpu_custom_call" | custom-call | flops 16777216 | bytes 1048576 | tf_op jit(solution)/shard_map/pallas_call | solution.py:453
  (8 shorter events, 0.0 us)
Async XLA Ops:
  3.3 26.8 %copy-start = (f32[3,4,32,1024]{3,2,1,0:T(8,128)S(1)}, f32[3,4,32,1024]{3,2,1,0:T(8,128)}, u32[]{:S(2)}) copy-start(f32[3,4,32,1024]{3,2,1,0:T(8,128)} %v_ref.1) | copy-start | bytes 4718596
  3.3 15.6 %all-to-all-start = ((f32[8,32,256]{2,1,0:T(8,128)}), f32[8,32,256]{2,1,0:T(8,128)S(1)}, u32[]{:S(2)}, u32[]{:S(2)}) async-start(f32[8,32,256]{2,1,0:T(8,128)} %get-tuple-element.20), calls=%async_computation | async-start | bytes 524288 | tf_op jit(solution)/shard_map/all_to_all | solution.py:426
  8.7 10.2 %collective-permute-start.1 = (f32[2,16,512]{2,1,0:T(8,128)}, f32[2,16,512]{2,1,0:T(8,128)S(1)}, u32[]{:S(2)}, u32[]{:S(2)}) collective-permute-start(f32[2,16,512]{2,1,0:T(8,128)} %get-tuple-element.26), channel_id=1, source_target_pairs={{0,3},{1,0},{2,1},{3,2},{4,7},{5,4},{6,5},{7,6},{8,11},{9,8},{10,9... | collective-permute-start | bytes 196616 | tf_op jit(solution)/shard_map/ppermute | solution.py:400
  12.3 6.6 %collective-permute-start = (f32[2,16,512]{2,1,0:T(8,128)}, f32[2,16,512]{2,1,0:T(8,128)S(1)}, u32[]{:S(2)}, u32[]{:S(2)}) collective-permute-start(f32[2,16,512]{2,1,0:T(8,128)} %get-tuple-element.21), channel_id=1, source_target_pairs={{0,1},{1,2},{2,3},{3,0},{4,5},{5,6},{6,7},{7,4},{8,9},{9,10},{10,1... | collective-permute-start | bytes 196616 | tf_op jit(solution)/shard_map/ppermute | solution.py:399
  12.3 4.2 %collective-permute-start.2 = (f32[8,512]{1,0:T(8,128)}, f32[8,512]{1,0:T(8,128)S(1)}, u32[]{:S(2)}, u32[]{:S(2)}) collective-permute-start(f32[8,512]{1,0:T(8,128)} %get-tuple-element.27), channel_id=1, source_target_pairs={{0,28},{4,0},{8,4},{12,8},{16,12},{20,16},{24,20},{28,24},{1,29},{... | collective-permute-start | bytes 49160 | tf_op jit(solution)/shard_map/ppermute | solution.py:402
  14.6 4.3 %collective-permute-start.3 = (f32[8,512]{1,0:T(8,128)}, f32[8,512]{1,0:T(8,128)S(1)}, u32[]{:S(2)}, u32[]{:S(2)}) collective-permute-start(f32[8,512]{1,0:T(8,128)} %get-tuple-element.28), channel_id=1, source_target_pairs={{0,4},{4,8},{8,12},{12,16},{16,20},{20,24},{24,28},{28,0},{1,5},{5... | collective-permute-start | bytes 49160 | tf_op jit(solution)/shard_map/ppermute | solution.py:401
  14.6 0.9 %copy-start.1 = (f32[3,2,16,512]{3,2,1,0:T(8,128)S(1)}, f32[3,2,16,512]{3,2,1,0:T(8,128)}, u32[]{:S(2)}) copy-start(f32[3,2,16,512]{3,2,1,0:T(8,128)} %b_ref) | copy-start | bytes 589828
  15.6 0.7 %copy-start.2 = (s32[32]{0:T(128)S(1)}, s32[32]{0:T(128)}, u32[]{:S(2)}) copy-start(s32[32]{0:T(128)} %param.5) | copy-start | bytes 388
  20.0 10.0 %all-to-all-start.1 = ((f32[8,24,256]{2,1,0:T(8,128)}), f32[8,24,256]{2,1,0:T(8,128)S(1)}, u32[]{:S(2)}, u32[]{:S(2)}) async-start(f32[8,24,256]{2,1,0:T(8,128)} %get-tuple-element.29), calls=%async_computation.1 | async-start | bytes 393216 | tf_op jit(solution)/shard_map/all_to_all | solution.py:441
  23.9 10.0 %collective-permute-start.4 = (f32[3,16,512]{2,1,0:T(8,128)S(1)}, f32[3,16,512]{2,1,0:T(8,128)S(1)}, u32[]{:S(2)}, u32[]{:S(2)}) collective-permute-start(f32[3,16,512]{2,1,0:T(8,128)S(1)} %get-tuple-element.34), channel_id=1, source_target_pairs={{0,1},{1,2},{2,3},{3,0},{4,5},{5,6},{6,7},{7,4},{8,9},{9,10},{10,1... | collective-permute-start | bytes 294920 | tf_op jit(solution)/shard_map/ppermute | solution.py:399
  23.9 10.0 %collective-permute-start.5 = (f32[3,16,512]{2,1,0:T(8,128)S(1)}, f32[3,16,512]{2,1,0:T(8,128)S(1)}, u32[]{:S(2)}, u32[]{:S(2)}) collective-permute-start(f32[3,16,512]{2,1,0:T(8,128)S(1)} %get-tuple-element.35), channel_id=1, source_target_pairs={{0,3},{1,0},{2,1},{3,2},{4,7},{5,4},{6,5},{7,6},{8,11},{9,8},{10,9... | collective-permute-start | bytes 294920 | tf_op jit(solution)/shard_map/ppermute | solution.py:400
  27.7 3.9 %collective-permute-start.6 = (f32[8,512]{1,0:T(8,128)S(1)}, f32[8,512]{1,0:T(8,128)S(1)}, u32[]{:S(2)}, u32[]{:S(2)}) collective-permute-start(f32[8,512]{1,0:T(8,128)S(1)} %get-tuple-element.36), channel_id=1, source_target_pairs={{0,28},{4,0},{8,4},{12,8},{16,12},{20,16},{24,20},{28,24},{1,29},{... | collective-permute-start | bytes 49160 | tf_op jit(solution)/shard_map/ppermute | solution.py:402
  29.8 4.1 %collective-permute-start.7 = (f32[8,512]{1,0:T(8,128)S(1)}, f32[8,512]{1,0:T(8,128)S(1)}, u32[]{:S(2)}, u32[]{:S(2)}) collective-permute-start(f32[8,512]{1,0:T(8,128)S(1)} %get-tuple-element.37), channel_id=1, source_target_pairs={{0,4},{4,8},{8,12},{12,16},{16,20},{20,24},{24,28},{28,0},{1,5},{5... | collective-permute-start | bytes 49160 | tf_op jit(solution)/shard_map/ppermute | solution.py:401

commit v8 on v6

--- a/solution.py
+++ b/solution.py
@@ -84,7 +84,7 @@
     return lane >> log2(p.rc), i >> log2(p.k), i & (p.k - 1)
 
 
-def restrict_kernel(p, v_hbm, t_hbm, b_hbm, out_hbm, up_hbm, down_hbm, v_ref, t_ref, b_ref, out, last, first, sems):
+def restrict_kernel(p, v_hbm, t_hbm, b_hbm, out_hbm, up_hbm, down_hbm, up2_hbm, down2_hbm, v_ref, t_ref, b_ref, out, last, first, sems):
     n, k, s, zc = p.n, p.k, p.slots, p.zc
     me = lax.axis_index("xy")
     t_copy = pltpu.make_async_copy(t_hbm, t_ref, sems.at[0])
@@ -125,6 +125,8 @@
     sends = [
         pltpu.make_async_copy(b_ref.at[0:2, zc - 1], up_hbm, sems.at[5]),
         pltpu.make_async_copy(b_ref.at[0:2, 0], down_hbm, sems.at[6]),
+        pltpu.make_async_copy(b_ref.at[2, zc - 1], up2_hbm, sems.at[11]),
+        pltpu.make_async_copy(b_ref.at[2, 0], down2_hbm, sems.at[12]),
     ]
     for c in range(3):
         for z in range(zc):
@@ -217,13 +219,7 @@
     return jnp.concatenate([ref[src, pl.ds(at + h, 1), :] for h in range(p.wrap)], axis=1)
 
 
-def interior_kernel(p, b_ref, t_ref, copy_ref, j_ref, next_ref, g3_ref):
-    s, k = p.slots, p.k
-    _, q_s = send_positions(p, t_ref[...])
-    r_l, z_l, j_l = lane_route(p)
-    shape = (p.zc, s, p.rows)
-    g3 = (iota(shape, 0) == z_l) & (q_s.reshape(1, s, 1) == (r_l * k + j_l).astype(F32))
-    g3_ref[...] = one_hot(g3).reshape(p.zc * s, p.rows)
+def interior_kernel(p, b_ref, copy_ref, j_ref, next_ref):
     zero = jnp.zeros((p.ny, p.nx), F32)
     for z in range(p.zc):
         b = [b_ref[c, z] for c in range(3)]
@@ -302,9 +298,9 @@
         for c in range(3):
             e_ref[c, z] = ez[c]
         if z == zc - 1:
-            up_ref[0], up_ref[1], up_ref[2] = ez[0], ez[1], bz[2]
+            up_ref[0], up_ref[1] = ez[0], ez[1]
         if z == 0:
-            down_ref[0], down_ref[1], down_ref[2] = ez[0], ez[1], bz[2]
+            down_ref[0], down_ref[1] = ez[0], ez[1]
         for i, c in enumerate((0, 2)):
             for h in range(p.wrap):
                 at = (i * zc + z) * p.wrap + h
@@ -315,7 +311,13 @@
         out[r, p.ru : p.ru + p.re, :] = jnp.where(r == nxt, e_rows[1], e_rows[0])
 
 
-def local_kernel(p, r_ref, b_ref, lo_ref, hi_ref, e_ref, next_ref):
+def local_kernel(p, r_ref, b_ref, lo_ref, hi_ref, lo2_ref, hi2_ref, e_ref, t_ref, next_ref, g3_ref):
+    s, k = p.slots, p.k
+    _, q_s = send_positions(p, t_ref[...])
+    r_l, z_l, j_l = lane_route(p)
+    shape = (p.zc, s, p.rows)
+    g3 = (iota(shape, 0) == z_l) & (q_s.reshape(1, s, 1) == (r_l * k + j_l).astype(F32))
+    g3_ref[...] = one_hot(g3).reshape(p.zc * s, p.rows)
     n, zc = p.n, p.zc
     me = lax.axis_index("xy")
     nxt, prv = lax.rem(me + 1, n), lax.rem(me + n - 1, n)
@@ -332,15 +334,15 @@
         for c in range(3):
             north, south = edge_rows(p, r_ref, nxt, prv, p.ru + (c * zc + z) * p.wrap)
             total = curl[c] + north + south
-            if c < 2 and z == 0:
-                total = total + lo_ref[c]
-            if c < 2 and z == zc - 1:
-                total = total + hi_ref[c]
+            if z == 0:
+                total = total + (lo_ref[c] if c < 2 else lo2_ref[...])
+            if z == zc - 1:
+                total = total + (hi_ref[c] if c < 2 else hi2_ref[...])
             next_ref[c, z] = b_ref[c, z] + 0.05 * total
 
 
-def widen_kernel(p, r_ref, g_ref, v_ref, vel_hbm, vel, sems):
-    zc = p.zc
+def finish_kernel(p, r_ref, g_ref, v_ref, n_ref, lo_ref, hi_ref, vel_hbm, mag_hbm, vel, mag, sems):
+    n, zc = p.n, p.zc
     half_fine = p.edge * p.edge // 2
     half_area = p.area // 2
     ex = log2(p.edge)
@@ -367,12 +369,6 @@
                     vel[c, 2 * z + d, :, fw] = v_ref[c, 2 * z + d, :, fw] + part
         copies.append(pltpu.make_async_copy(vel.at[c], vel_hbm.at[c], sems.at[c]))
         copies[-1].start()
-    for copy in copies:
-        copy.wait()
-
-
-def finish_kernel(p, r_ref, n_ref, lo_ref, hi_ref, mag):
-    n, zc = p.n, p.zc
     me = lax.axis_index("xy")
     nxt, prv = lax.rem(me + 1, n), lax.rem(me + n - 1, n)
 
@@ -382,16 +378,17 @@
 
     for z in range(zc):
         dz = [jnp.zeros((p.ny, p.nx), F32)] * 2
-        outer = dz[0]
         if z == zc - 1:
             dz = [dz[c] + hi_ref[c] for c in range(2)]
-            outer = outer + hi_ref[2]
         if z == 0:
             dz = [dz[c] - lo_ref[c] for c in range(2)]
-            outer = outer + lo_ref[2]
         mag[0, z] = n_ref[0, z] + 0.05 * (dy(1, z) - dz[1])
         mag[1, z] = n_ref[1, z] + 0.05 * dz[0]
-        mag[2, z] = n_ref[2, z] + 0.05 * (outer - dy(0, z))
+        mag[2, z] = n_ref[2, z] - 0.05 * dy(0, z)
+    copies.append(pltpu.make_async_copy(mag, mag_hbm, sems.at[3]))
+    copies[-1].start()
+    for copy in copies:
+        copy.wait()
 
 
 def struct(*shape, dtype=F32):
@@ -426,10 +423,10 @@
     plane = (p.ny, p.nx)
     dma = pltpu.SemaphoreType.DMA
     table = slot_block_table.reshape(1, p.slots)
-    sent, up, down = call(
+    sent, up, down, up2, down2 = call(
         functools.partial(restrict_kernel, p),
         [HBM] * 3,
-        [(struct(p.n, p.r1, p.area), HBM), (struct(2, *plane), HBM), (struct(2, *plane), HBM)],
+        [(struct(p.n, p.r1, p.area), HBM)] + [(struct(2, *plane), HBM)] * 2 + [(struct(*plane), HBM)] * 2,
         [
             pltpu.VMEM(velocity.shape, F32),
             pltpu.VMEM((1, p.slots), jnp.int32),
@@ -437,44 +434,44 @@
             pltpu.VMEM((p.n, p.r1, p.area), F32),
             pltpu.VMEM((-(-p.rb // 8) * 8, p.area), F32),
             pltpu.VMEM((-(-p.rb // 8) * 8, p.area), F32),
-            dma((11,)),
+            dma((13,)),
         ],
         ALL_VMEM,
     )(velocity, table, magnetic)
     got = lax.all_to_all(sent, "xy", 0, 0, tiled=True)
     below, above = planes(up, down)
-    held, held_table, _ = lax.optimization_barrier((magnetic, table, up))
-    field, current, diffused, g3 = call(
-        functools.partial(interior_kernel, p),
-        [VMEM] * 2,
-        [(struct(*magnetic.shape), VMEM)] * 3 + [(struct(p.zc * p.slots, p.rows, dtype=BF16), VMEM)],
-    )(held, held_table)
+    below2, above2 = planes(up2, down2)
+    held, _ = lax.optimization_barrier((magnetic, up))
+    field, current, diffused = call(
+        functools.partial(interior_kernel, p), [VMEM], [(struct(*magnetic.shape), VMEM)] * 3
+    )(held)
     sent, emf, up, down = call(
         functools.partial(field_kernel, p),
         [VMEM] * 5,
         [
             (struct(p.n, p.r2, p.area), VMEM),
             (struct(*magnetic.shape), VMEM),
-            (struct(3, *plane), VMEM),
-            (struct(3, *plane), VMEM),
+            (struct(2, *plane), VMEM),
+            (struct(2, *plane), VMEM),
         ],
         [pltpu.VMEM((2, p.re, p.area), F32)],
     )(got, field, current, below, above)
     got_force = lax.all_to_all(sent, "xy", 0, 0, tiled=True)
     emf_below, emf_above = planes(up, down)
-    (partial,) = call(
-        functools.partial(local_kernel, p), [VMEM] * 5, [(struct(*magnetic.shape), VMEM)]
-    )(got, diffused, below, above, emf)
-    (updated,) = call(
-        functools.partial(widen_kernel, p),
-        [VMEM] * 3,
-        [(struct(*velocity.shape), HBM)],
-        [pltpu.VMEM(velocity.shape, F32), dma((3,))],
-    )(got_force, g3, velocity)
-    (finished,) = call(
-        functools.partial(finish_kernel, p), [VMEM] * 4, [(struct(*magnetic.shape), VMEM)]
-    )(got_force, partial, emf_below, emf_above)
-    return updated, finished
+    held_table, _ = lax.optimization_barrier((table, up))
+    partial, g3 = call(
+        functools.partial(local_kernel, p),
+        [VMEM] * 8,
+        [(struct(*magnetic.shape), VMEM), (struct(p.zc * p.slots, p.rows, dtype=BF16), VMEM)],
+    )(got, diffused, below, above, below2, above2, emf, held_table)
+    return tuple(
+        call(
+            functools.partial(finish_kernel, p),
+            [VMEM] * 6,
+            [(struct(*velocity.shape), HBM), (struct(*magnetic.shape), HBM)],
+            [pltpu.VMEM(velocity.shape, F32), pltpu.VMEM(magnetic.shape, F32), dma((4,))],
+        )(got_force, g3, velocity, partial, emf_below, emf_above)
+    )
 
 
 def solution(mesh):

time: 33.6 us -> 34 us (1.012)
  starting transfers between devices: 17 us -> 19 us
  local copies, waits for them, and re-layouts: 1.59 us -> 0.95 us
  Pallas kernels: 6.6 us -> 5.98 us
  waiting for transfers between devices: 7.39 us -> 7.04 us
    all_to_all x1, waiting for transfers between devices: 2.93 us -> 0.01 us  [body(): got_force = lax.all_to_all(sent, 'xy', 0, 0, tiled=True)]
    ppermute x2 -> x3, waiting for transfers between devices: 3.48 us -> 5.37 us  [planes(): below = lax.ppermute(up, 'gz', ring('gz', 1))]
    ppermute x2 -> x3, starting transfers between devices: 0.01 us -> 1.45 us  [planes(): below = lax.ppermute(up, 'gz', ring('gz', 1))]
    ppermute x2 -> x3, waiting for transfers between devices: 0.98 us -> 1.67 us  [planes(): above = lax.ppermute(down, 'gz', ring('gz', -1))]
    pallas_call x4 -> x3, Pallas kernels: 2.54 us -> 1.9 us  [the longest x1 1.53 us: body(): call(functools.partial(finish_kernel, p), [VMEM] * 6, [(struct(*velocity....]
    unnamed x6 -> x10, local copies, waits for them, and re-layouts: 1.59 us -> 0.95 us
    ppermute x2 -> x3, starting transfers between devices: 7.41 us -> 8 us  [planes(): above = lax.ppermute(down, 'gz', ring('gz', -1))]
  transfers between devices with their start and end apart: 6 -> 8, of which waited for: 3 -> 3; matrix products, arithmetic and copies ran while one was open for 0% -> 0% of each run, Pallas kernels for 5% -> 1%
where the time goes in v8:
time: 34 us; the launch traced here: 33.7 us
  starting transfers between devices  19 us (56%)
  waiting for transfers between devices  7.04 us (21%)
  Pallas kernels  5.98 us (18%)
  local copies, waits for them, and re-layouts  0.95 us (3%)
  between operations  0.71 us (2%)
    ppermute x3, starting transfers between devices, planes(): above = lax.ppermute(down, 'gz', ring('gz', -1))  8 us
    ppermute x3, waiting for transfers between devices, planes(): below = lax.ppermute(up, 'gz', ring('gz', 1))  5.37 us
    all_to_all x1, starting transfers between devices, body(): got = lax.all_to_all(sent, 'xy', 0, 0, tiled=True)  5.34 us
    all_to_all x1, starting transfers between devices, body(): got_force = lax.all_to_all(sent, 'xy', 0, 0, tiled=True)  4.2 us
    pallas_call x1, Pallas kernels, body(): call(functools.partial(restrict_kernel, p), [HBM] * 3, [(struct(p.n, p.r1...  2.73 us
    ppermute x3, waiting for transfers between devices, planes(): above = lax.ppermute(down, 'gz', ring('gz', -1))  1.67 us
    pallas_call x1, Pallas kernels, body(): call(functools.partial(finish_kernel, p), [VMEM] * 6, [(struct(*velocity....  1.53 us
    ppermute x3, starting transfers between devices, planes(): below = lax.ppermute(up, 'gz', ring('gz', 1))  1.45 us
  transfers between devices with their start and end apart: 8, of which 3 were waited for; matrix products, arithmetic and copies ran while one was open for 0% of the time, Pallas kernels for 1%

profile of v8, /device:TPU:0, one launch (start us, length us, event | category | flops | bytes accessed | tf_op | source)
XLA Modules:
  0.0 33.7 jit_solution(13380235823617311178)
XLA Ops:
  0.6 2.7 %shard_map.50 = (f32[8,40,256]{2,1,0:T(8,128)}, f32[2,16,512]{2,1,0:T(8,128)}, f32[2,16,512]{2,1,0:T(8,128)}, f32[16,512]{1,0:T(8,128)}, f32[16,512]{1,0:T(8,128)}) custom-call(f32[3,4,32,1024]{3,2,1,0:T(8,128)} %v_ref.1, s32[1,32]{1,0:T(1,128)} %bitcast.1, f32[3,2,16,512]{3,2,1,0:T(8,128)} %b_ref), custom_call_target="tpu_custom_call" | custom-call | flops 16777216 | bytes 1048576 | tf_op jit(solution)/shard_map/pallas_call | solution.py:426
  3.4 0.0 copy-start.2
  3.4 0.0 copy-start
  3.4 5.3 %all-to-all-start = ((f32[8,40,256]{2,1,0:T(8,128)}), f32[8,40,256]{2,1,0:T(8,128)S(1)}, u32[]{:S(2)}, u32[]{:S(2)}) async-start(f32[8,40,256]{2,1,0:T(8,128)} %get-tuple-element.18), calls=%async_computation | async-start | bytes 655360 | tf_op jit(solution)/shard_map/all_to_all | solution.py:441
  8.7 3.6 %collective-permute-start.1 = (f32[2,16,512]{2,1,0:T(8,128)}, f32[2,16,512]{2,1,0:T(8,128)S(1)}, u32[]{:S(2)}, u32[]{:S(2)}) collective-permute-start(f32[2,16,512]{2,1,0:T(8,128)} %get-tuple-element.23), channel_id=1, source_target_pairs={{0,3},{1,0},{2,1},{3,2},{4,7},{5,4},{6,5},{7,6},{8,11},{9,8},{10,9... | collective-permute-start | bytes 196616 | tf_op jit(solution)/shard_map/ppermute | solution.py:417
  12.3 0.0 collective-permute-start
  12.3 0.9 %copy-done.1 = f32[3,2,16,512]{3,2,1,0:T(8,128)S(1)} copy-done((f32[3,2,16,512]{3,2,1,0:T(8,128)S(1)}, f32[3,2,16,512]{3,2,1,0:T(8,128)}, u32[]{:S(2)}) %copy-start.1) | copy-done | bytes 196632
  13.3 0.2 shard_map.51
  13.5 1.7 %collective-permute-done.1.hi_ref = f32[2,16,512]{2,1,0:T(8,128)S(1)} collective-permute-done((f32[2,16,512]{2,1,0:T(8,128)}, f32[2,16,512]{2,1,0:T(8,128)S(1)}, u32[]{:S(2)}, u32[]{:S(2)}) %collective-permute-start.1) | collective-permute-done | bytes 65568 | tf_op jit(solution)/shard_map/ppermute | solution.py:417
  15.1 3.5 %collective-permute-done.lo_ref = f32[2,16,512]{2,1,0:T(8,128)S(1)} collective-permute-done((f32[2,16,512]{2,1,0:T(8,128)}, f32[2,16,512]{2,1,0:T(8,128)S(1)}, u32[]{:S(2)}, u32[]{:S(2)}) %collective-permute-start) | collective-permute-done | bytes 65568 | tf_op jit(solution)/shard_map/ppermute | solution.py:416
  18.6 0.0 all-to-all-done.r_ref
  18.6 1.3 %shard_map.52 = (f32[8,32,256]{2,1,0:T(8,128)}, f32[3,2,16,512]{3,2,1,0:T(8,128)S(1)}, f32[2,16,512]{2,1,0:T(8,128)S(1)}, f32[2,16,512]{2,1,0:T(8,128)S(1)}) custom-call(f32[8,40,256]{2,1,0:T(8,128)S(1)} %all-to-all-done.r_ref, f32[3,2,16,512]{3,2,1,0:T(8,128)S(1)} %get-tuple-element.21.b_ref, f32[3,2,16,512]{3,2,1,0:T(8,128)S(1)} %get-tuple-element.22.j_ref, ...), custom_call_target="tpu_custom_call" | custom-call | flops 16777216 | bytes 1048576 | tf_op jit(solution)/shard_map/pallas_call | solution.py:448
  20.0 4.2 %all-to-all-start.1 = ((f32[8,32,256]{2,1,0:T(8,128)}), f32[8,32,256]{2,1,0:T(8,128)S(1)}, u32[]{:S(2)}, u32[]{:S(2)}) async-start(f32[8,32,256]{2,1,0:T(8,128)} %get-tuple-element.24), calls=%async_computation.1 | async-start | bytes 524288 | tf_op jit(solution)/shard_map/all_to_all | solution.py:459
  24.2 0.6 %collective-permute-start.5 = (f32[2,16,512]{2,1,0:T(8,128)S(1)}, f32[2,16,512]{2,1,0:T(8,128)S(1)}, u32[]{:S(2)}, u32[]{:S(2)}) collective-permute-start(f32[2,16,512]{2,1,0:T(8,128)S(1)} %get-tuple-element.33), channel_id=1, source_target_pairs={{0,3},{1,0},{2,1},{3,2},{4,7},{5,4},{6,5},{7,6},{8,11},{9,8},{10,9... | collective-permute-start | bytes 196616 | tf_op jit(solution)/shard_map/ppermute | solution.py:417
  24.8 1.4 %collective-permute-start.4 = (f32[2,16,512]{2,1,0:T(8,128)S(1)}, f32[2,16,512]{2,1,0:T(8,128)S(1)}, u32[]{:S(2)}, u32[]{:S(2)}) collective-permute-start(f32[2,16,512]{2,1,0:T(8,128)S(1)} %get-tuple-element.29), channel_id=1, source_target_pairs={{0,1},{1,2},{2,3},{3,0},{4,5},{5,6},{6,7},{7,4},{8,9},{9,10},{10,1... | collective-permute-start | bytes 196616 | tf_op jit(solution)/shard_map/ppermute | solution.py:416
  26.2 0.0 collective-permute-start.2
  26.2 3.8 %collective-permute-start.3 = (f32[16,512]{1,0:T(8,128)S(1)}, f32[16,512]{1,0:T(8,128)S(1)}, u32[]{:S(2)}, u32[]{:S(2)}) collective-permute-start(f32[16,512]{1,0:T(8,128)S(1)} %copy-done.3), channel_id=1, source_target_pairs={{0,3},{1,0},{2,1},{3,2},{4,7},{5,4},{6,5},{7,6},{8,11},{9,8},{10,9... | collective-permute-start | bytes 98312 | tf_op jit(solution)/shard_map/ppermute | solution.py:417
  30.0 1.9 %collective-permute-done.2.lo2_ref = f32[16,512]{1,0:T(8,128)S(1)} collective-permute-done((f32[16,512]{1,0:T(8,128)S(1)}, f32[16,512]{1,0:T(8,128)S(1)}, u32[]{:S(2)}, u32[]{:S(2)}) %collective-permute-start.2) | collective-permute-done | bytes 32800 | tf_op jit(solution)/shard_map/ppermute | solution.py:416
  31.9 0.0 collective-permute-done.3.hi2_ref
  31.9 0.2 shard_map.53
  32.1 0.0 collective-permute-done.5.hi_ref
  32.1 0.0 collective-permute-done.4.lo_ref
  32.1 0.0 all-to-all-done.1.r_ref
  32.1 1.5 %shard_map.54 = (f32[3,4,32,1024]{3,2,1,0:T(8,128)}, f32[3,2,16,512]{3,2,1,0:T(8,128)}) custom-call(f32[8,32,256]{2,1,0:T(8,128)S(1)} %all-to-all-done.1.r_ref, bf16[64,64]{1,0:T(8,128)(2,1)S(1)} %get-tuple-element.31.g_ref, f32[3,4,32,1024]{3,2,1,0:T(8,128)S(1)} %copy-done, f32[3,2,16,512]{3,2,1,0:T(8,128)S(1)} %get-tuple-element.32.n_ref, ...), custom_call_target="tpu_custom_call" | custom-call | flops 16777216 | bytes 1048576 | tf_op jit(solution)/shard_map/pallas_call | solution.py:468
  (7 shorter events, 0.0 us)
Async XLA Ops:
  3.4 28.5 %copy-start.2 = (s32[32]{0:T(128)S(1)}, s32[32]{0:T(128)}, u32[]{:S(2)}) copy-start(s32[32]{0:T(128)} %param.5) | copy-start | bytes 388
  3.4 28.8 %copy-start = (f32[3,4,32,1024]{3,2,1,0:T(8,128)S(1)}, f32[3,4,32,1024]{3,2,1,0:T(8,128)}, u32[]{:S(2)}) copy-start(f32[3,4,32,1024]{3,2,1,0:T(8,128)} %v_ref.1) | copy-start | bytes 4718596
  3.4 15.2 %all-to-all-start = ((f32[8,40,256]{2,1,0:T(8,128)}), f32[8,40,256]{2,1,0:T(8,128)S(1)}, u32[]{:S(2)}, u32[]{:S(2)}) async-start(f32[8,40,256]{2,1,0:T(8,128)} %get-tuple-element.18), calls=%async_computation | async-start | bytes 655360 | tf_op jit(solution)/shard_map/all_to_all | solution.py:441
  8.7 6.4 %collective-permute-start.1 = (f32[2,16,512]{2,1,0:T(8,128)}, f32[2,16,512]{2,1,0:T(8,128)S(1)}, u32[]{:S(2)}, u32[]{:S(2)}) collective-permute-start(f32[2,16,512]{2,1,0:T(8,128)} %get-tuple-element.23), channel_id=1, source_target_pairs={{0,3},{1,0},{2,1},{3,2},{4,7},{5,4},{6,5},{7,6},{8,11},{9,8},{10,9... | collective-permute-start | bytes 196616 | tf_op jit(solution)/shard_map/ppermute | solution.py:417
  12.3 6.3 %collective-permute-start = (f32[2,16,512]{2,1,0:T(8,128)}, f32[2,16,512]{2,1,0:T(8,128)S(1)}, u32[]{:S(2)}, u32[]{:S(2)}) collective-permute-start(f32[2,16,512]{2,1,0:T(8,128)} %get-tuple-element.19), channel_id=1, source_target_pairs={{0,1},{1,2},{2,3},{3,0},{4,5},{5,6},{6,7},{7,4},{8,9},{9,10},{10,1... | collective-permute-start | bytes 196616 | tf_op jit(solution)/shard_map/ppermute | solution.py:416
  12.3 0.9 %copy-start.1 = (f32[3,2,16,512]{3,2,1,0:T(8,128)S(1)}, f32[3,2,16,512]{3,2,1,0:T(8,128)}, u32[]{:S(2)}) copy-start(f32[3,2,16,512]{3,2,1,0:T(8,128)} %b_ref) | copy-start | bytes 589828
  13.3 12.9 %copy-start.4 = (f32[16,512]{1,0:T(8,128)S(1)}, f32[16,512]{1,0:T(8,128)}, u32[]{:S(2)}) copy-start(f32[16,512]{1,0:T(8,128)} %get-tuple-element.26) | copy-start | bytes 98308
  13.3 12.9 %copy-start.3 = (f32[16,512]{1,0:T(8,128)S(1)}, f32[16,512]{1,0:T(8,128)}, u32[]{:S(2)}) copy-start(f32[16,512]{1,0:T(8,128)} %get-tuple-element.27) | copy-start | bytes 98308
  20.0 12.2 %all-to-all-start.1 = ((f32[8,32,256]{2,1,0:T(8,128)}), f32[8,32,256]{2,1,0:T(8,128)S(1)}, u32[]{:S(2)}, u32[]{:S(2)}) async-start(f32[8,32,256]{2,1,0:T(8,128)} %get-tuple-element.24), calls=%async_computation.1 | async-start | bytes 524288 | tf_op jit(solution)/shard_map/all_to_all | solution.py:459
  24.2 7.9 %collective-permute-start.5 = (f32[2,16,512]{2,1,0:T(8,128)S(1)}, f32[2,16,512]{2,1,0:T(8,128)S(1)}, u32[]{:S(2)}, u32[]{:S(2)}) collective-permute-start(f32[2,16,512]{2,1,0:T(8,128)S(1)} %get-tuple-element.33), channel_id=1, source_target_pairs={{0,3},{1,0},{2,1},{3,2},{4,7},{5,4},{6,5},{7,6},{8,11},{9,8},{10,9... | collective-permute-start | bytes 196616 | tf_op jit(solution)/shard_map/ppermute | solution.py:417
  24.8 7.4 %collective-permute-start.4 = (f32[2,16,512]{2,1,0:T(8,128)S(1)}, f32[2,16,512]{2,1,0:T(8,128)S(1)}, u32[]{:S(2)}, u32[]{:S(2)}) collective-permute-start(f32[2,16,512]{2,1,0:T(8,128)S(1)} %get-tuple-element.29), channel_id=1, source_target_pairs={{0,1},{1,2},{2,3},{3,0},{4,5},{5,6},{6,7},{7,4},{8,9},{9,10},{10,1... | collective-permute-start | bytes 196616 | tf_op jit(solution)/shard_map/ppermute | solution.py:416
  26.2 5.7 %collective-permute-start.2 = (f32[16,512]{1,0:T(8,128)S(1)}, f32[16,512]{1,0:T(8,128)S(1)}, u32[]{:S(2)}, u32[]{:S(2)}) collective-permute-start(f32[16,512]{1,0:T(8,128)S(1)} %copy-done.4), channel_id=1, source_target_pairs={{0,1},{1,2},{2,3},{3,0},{4,5},{5,6},{6,7},{7,4},{8,9},{9,10},{10,1... | collective-permute-start | bytes 98312 | tf_op jit(solution)/shard_map/ppermute | solution.py:416
  26.2 5.7 %collective-permute-start.3 = (f32[16,512]{1,0:T(8,128)S(1)}, f32[16,512]{1,0:T(8,128)S(1)}, u32[]{:S(2)}, u32[]{:S(2)}) collective-permute-start(f32[16,512]{1,0:T(8,128)S(1)} %copy-done.3), channel_id=1, source_target_pairs={{0,3},{1,0},{2,1},{3,2},{4,7},{5,4},{6,5},{7,6},{8,11},{9,8},{10,9... | collective-permute-start | bytes 98312 | tf_op jit(solution)/shard_map/ppermute | solution.py:417

commit v9 on v6

--- a/solution.py
+++ b/solution.py
@@ -51,10 +51,9 @@
         self.ru = 3 * self.rc
         self.rows = n * self.rc
         self.rb = 3 * self.zc * self.nx // self.area
-        self.r1 = -(-(self.ru + self.rb + 1) // 8) * 8
-        self.re = 2 * self.zc * self.nx // self.area
-        self.r2 = -(-(self.ru + self.re) // 8) * 8
+        self.r1 = -(-(self.ru + self.rb + 4) // 8) * 8
         self.wrap = self.nx // self.area
+        assert self.rc == 8 and self.area == 256 and self.half == 16
 
 
 def mirror(i):
@@ -76,6 +75,20 @@
     hi, lo = split(x)
     out = dot(g, jnp.concatenate([hi, lo], axis=1))
     return out[:, : x.shape[1]] + out[:, x.shape[1] :]
+
+
+def spin(t):
+    return pltpu.roll(t, 0, 1, stride=16, stride_axis=0)
+
+
+def lay_out(t, first):
+    t = spin(t)
+    here = (iota(t.shape, 1) >> 4) == ((iota(t.shape, 0) + first) & 7)
+    return jnp.sum(jnp.where(here, t, 0.0), axis=0, keepdims=True)
+
+
+def tile_lanes(x, width):
+    return x[:, :width] if width <= 128 else jnp.concatenate([x] * (width // 128), axis=1)
 
 
 def lane_route(p):
@@ -115,12 +128,16 @@
     qi = iota((s, s), 0).astype(F32)
     col_q = jnp.sum(jnp.where(qi == jnp.broadcast_to(q, (s, s)), col, 0.0), axis=1, keepdims=True)
     qa, la = iota((s, p.area), 0), iota((s, p.area), 1)
-    spread = jnp.where((qa & (k - 1)) == (la & (k - 1)), col_q, 0.0).astype(BF16)
+    place = jnp.where(la < 128, la, jnp.where(la < 192, -la, -1 - la)) & (k - 1)
+    spread = jnp.where((qa & (k - 1)) == place, col_q, 0.0).astype(BF16)
     gather = one_hot((iota((n, s), 1) >> log2(k)) == iota((n, s), 0))
     cols = dot(gather, spread)
     at = p.ru + p.rb
     for r in range(n):
-        out[r, at : at + 1, :] = cols[r : r + 1]
+        north, south = (r + 1) % n, (r - 1) % n
+        out[r, at : at + 1, :128] = cols[r : r + 1, :128]
+        outer = jnp.where(iota((1, 128), 1) < 64, cols[north : north + 1, 128:], cols[south : south + 1, 128:])
+        out[r, at : at + 1, 128:] = outer
     b_copy.wait()
     sends = [
         pltpu.make_async_copy(b_ref.at[0:2, zc - 1], up_hbm, sems.at[5]),
@@ -136,8 +153,8 @@
     nxt = lax.rem(me + 1, n)
     for r in range(n):
         out[r, p.ru : p.ru + p.rb, :] = jnp.where(r == nxt, last[: p.rb], first[: p.rb])
-    tail = pl.ds(p.ru, p.r1 - p.ru)
-    sends.append(pltpu.make_async_copy(out.at[:, tail, :], out_hbm.at[:, tail, :], sems.at[7]))
+    early = pl.ds(p.ru, 8)
+    sends.append(pltpu.make_async_copy(out.at[:, early, :], out_hbm.at[:, early, :], sems.at[7]))
     for send in sends:
         send.start()
     averages = []
@@ -151,10 +168,19 @@
         u = [o[2 * h * m : (2 * h + 1) * m] + o[(2 * h + 1) * m : (2 * h + 2) * m] for h in range(2)]
         averages.append(jnp.concatenate(u, axis=1) * 0.125)
     for c in range(3):
-        out[:, c * p.rc : (c + 1) * p.rc, :] = select(g, averages[c]).reshape(n, p.rc, p.area)
+        blocks = select(g, averages[c])
+        out[:, c * p.rc : (c + 1) * p.rc, :] = blocks.reshape(n, p.rc, p.area)
         rows = pl.ds(c * p.rc, p.rc)
         sends.append(pltpu.make_async_copy(out.at[:, rows, :], out_hbm.at[:, rows, :], sems.at[8 + c]))
         sends[-1].start()
+        at = p.ru + p.rb + 1 + c
+        for r in range(n):
+            tile = blocks[r * p.rc : (r + 1) * p.rc]
+            out[(r - 1) % n, at : at + 1, :128] = lay_out(tile[:, :128], 0)
+            out[(r + 1) % n, at : at + 1, 128:] = lay_out(tile[:, 128:], 1)
+    late = pl.ds(p.ru + 8, p.r1 - p.ru - 8)
+    sends.append(pltpu.make_async_copy(out.at[:, late, :], out_hbm.at[:, late, :], sems.at[11]))
+    sends[-1].start()
     for send in sends:
         send.wait()
 
@@ -246,7 +272,7 @@
     return north, jnp.where(y == 0, row_of(p, ref, prv, at), 0.0)
 
 
-def field_kernel(p, r_ref, b_ref, j_ref, lo_ref, hi_ref, out, e_ref, up_ref, down_ref, e_rows):
+def field_kernel(p, r_ref, b_ref, j_ref, lo_ref, hi_ref, out, e_ref, up_ref, down_ref):
     n, k, zc = p.n, p.k, p.zc
     me = lax.axis_index("xy")
     nxt, prv = lax.rem(me + 1, n), lax.rem(me + n - 1, n)
@@ -286,7 +312,7 @@
     p_l, z_l, _ = lane_route(p)
     shape = (n, p.rows)
     col_l = jnp.sum(
-        jnp.where(iota(shape, 0) == p_l.reshape(1, p.rows), cols[:, : p.rows], 0.0), axis=0, keepdims=True
+        jnp.where(iota(shape, 0) == p_l.reshape(1, p.rows), tile_lanes(cols[:, :128], p.rows), 0.0), axis=0, keepdims=True
     )
     shape = (zc, p.bcols, p.rows)
     g = one_hot(
@@ -305,14 +331,37 @@
             up_ref[0], up_ref[1], up_ref[2] = ez[0], ez[1], bz[2]
         if z == 0:
             down_ref[0], down_ref[1], down_ref[2] = ez[0], ez[1], bz[2]
-        for i, c in enumerate((0, 2)):
-            for h in range(p.wrap):
-                at = (i * zc + z) * p.wrap + h
-                w = slice(h * p.area, (h + 1) * p.area)
-                e_rows[0, at : at + 1, :] = ez[c][0:1, w]
-                e_rows[1, at : at + 1, :] = ez[c][p.ny - 1 : p.ny, w]
-    for r in range(n):
-        out[r, p.ru : p.ru + p.re, :] = jnp.where(r == nxt, e_rows[1], e_rows[0])
+
+
+def outer_velocity(p, r_ref):
+    n, zc = p.n, p.zc
+    at = p.ru + p.rb
+    x = r_ref[:, at, :][:, 128:]
+    spun = pltpu.roll(x, 64, 1)
+    low = iota(x.shape, 1) < 64
+    lane = iota((1, 1, p.rows), 2)
+    place = lane & 7
+    shape = (zc, p.bcols, p.rows)
+    sides = []
+    for d, (cols, i) in enumerate(((jnp.where(low, x, spun), (8 - place) & 7), (jnp.where(low, spun, x), 7 - place))):
+        device = iota((n, p.rows), 0) == (lane >> 3).reshape(1, p.rows)
+        col = jnp.sum(jnp.where(device, tile_lanes(cols, p.rows), 0.0), axis=0, keepdims=True)
+        g = one_hot(
+            (iota(shape, 0) == (i >> log2(p.k))) & (iota(shape, 1).astype(F32) == col.reshape(1, 1, p.rows))
+        ).reshape(zc * p.bcols, p.rows)
+        parts = []
+        for c in range(3):
+            m = r_ref[:, at + 1 + c, :][:, 128 * d : 128 * d + 128]
+            parts.append(jnp.concatenate([spin(jnp.broadcast_to(m[r : r + 1], (8, 128))) for r in range(n)], axis=0))
+        o = select(g, jnp.concatenate(parts, axis=1))
+        side = []
+        for c in range(3):
+            blocks = o[:, 128 * c : 128 * c + 128]
+            row = [lay_out(blocks[8 * t : 8 * t + 8], 0) for t in range(zc * p.bcols // 8)]
+            per = p.bcols // 8
+            side.append([jnp.concatenate(row[z * per : (z + 1) * per], axis=1) for z in range(zc)])
+        sides.append(side)
+    return sides
 
 
 def local_kernel(p, r_ref, b_ref, lo_ref, hi_ref, e_ref, next_ref):
@@ -320,14 +369,20 @@
     me = lax.axis_index("xy")
     nxt, prv = lax.rem(me + 1, n), lax.rem(me + n - 1, n)
     zero = jnp.zeros((p.ny, p.nx), F32)
+    outer_u = outer_velocity(p, r_ref)
     for z in range(zc):
         e = [e_ref[c, z] for c in range(3)]
+        e0, e2 = [], []
+        for u, device in zip(outer_u, (nxt, prv)):
+            b = [row_of(p, r_ref, device, p.ru + (c * zc + z) * p.wrap) for c in range(3)]
+            e0.append(u[1][z] * b[2] - u[2][z] * b[1])
+            e2.append(u[0][z] * b[1] - u[1][z] * b[0])
         above = [e_ref[c, z + 1] if z < zc - 1 else zero for c in range(2)]
         below = [e_ref[c, z - 1] if z > 0 else zero for c in range(2)]
         curl = [
-            (y_next(e[2], 0.0) - y_prev(e[2], 0.0)) - (above[1] - below[1]),
+            (y_next(e[2], e2[0]) - y_prev(e[2], e2[1])) - (above[1] - below[1]),
             (above[0] - below[0]) - (x_next(e[2]) - x_prev(e[2])),
-            (x_next(e[1]) - x_prev(e[1])) - (y_next(e[0], 0.0) - y_prev(e[0], 0.0)),
+            (x_next(e[1]) - x_prev(e[1])) - (y_next(e[0], e0[0]) - y_prev(e[0], e0[1])),
         ]
         for c in range(3):
             north, south = edge_rows(p, r_ref, nxt, prv, p.ru + (c * zc + z) * p.wrap)
@@ -371,15 +426,8 @@
         copy.wait()
 
 
-def finish_kernel(p, r_ref, n_ref, lo_ref, hi_ref, mag):
-    n, zc = p.n, p.zc
-    me = lax.axis_index("xy")
-    nxt, prv = lax.rem(me + 1, n), lax.rem(me + n - 1, n)
-
-    def dy(i, z):
-        north, south = edge_rows(p, r_ref, nxt, prv, p.ru + (i * zc + z) * p.wrap)
-        return north - south
-
+def finish_kernel(p, n_ref, lo_ref, hi_ref, mag):
+    zc = p.zc
     for z in range(zc):
         dz = [jnp.zeros((p.ny, p.nx), F32)] * 2
         outer = dz[0]
@@ -389,9 +437,9 @@
         if z == 0:
             dz = [dz[c] - lo_ref[c] for c in range(2)]
             outer = outer + lo_ref[2]
-        mag[0, z] = n_ref[0, z] + 0.05 * (dy(1, z) - dz[1])
+        mag[0, z] = n_ref[0, z] + 0.05 * -dz[1]
         mag[1, z] = n_ref[1, z] + 0.05 * dz[0]
-        mag[2, z] = n_ref[2, z] + 0.05 * (outer - dy(0, z))
+        mag[2, z] = n_ref[2, z] + 0.05 * outer
 
 
 def struct(*shape, dtype=F32):
@@ -437,7 +485,7 @@
             pltpu.VMEM((p.n, p.r1, p.area), F32),
             pltpu.VMEM((-(-p.rb // 8) * 8, p.area), F32),
             pltpu.VMEM((-(-p.rb // 8) * 8, p.area), F32),
-            dma((11,)),
+            dma((12,)),
         ],
         ALL_VMEM,
     )(velocity, table, magnetic)
@@ -453,12 +501,11 @@
         functools.partial(field_kernel, p),
         [VMEM] * 5,
         [
-            (struct(p.n, p.r2, p.area), VMEM),
+            (struct(p.n, p.ru, p.area), VMEM),
             (struct(*magnetic.shape), VMEM),
             (struct(3, *plane), VMEM),
             (struct(3, *plane), VMEM),
         ],
-        [pltpu.VMEM((2, p.re, p.area), F32)],
     )(got, field, current, below, above)
     got_force = lax.all_to_all(sent, "xy", 0, 0, tiled=True)
     emf_below, emf_above = planes(up, down)
@@ -471,9 +518,10 @@
         [(struct(*velocity.shape), HBM)],
         [pltpu.VMEM(velocity.shape, F32), dma((3,))],
     )(got_force, g3, velocity)
+    partial, _ = lax.optimization_barrier((partial, updated))
     (finished,) = call(
-        functools.partial(finish_kernel, p), [VMEM] * 4, [(struct(*magnetic.shape), VMEM)]
-    )(got_force, partial, emf_below, emf_above)
+        functools.partial(finish_kernel, p), [VMEM] * 3, [(struct(*magnetic.shape), VMEM)]
+    )(partial, emf_below, emf_above)
     return updated, finished
 
 

time: 33.6 us -> 32.8 us (0.976)
  waiting for transfers between devices: 7.39 us -> 6.42 us
    all_to_all x1, waiting for transfers between devices: 2.93 us -> 1.95 us  [body(): got_force = lax.all_to_all(sent, 'xy', 0, 0, tiled=True)]
  transfers between devices with their start and end apart: 6 -> 6, of which waited for: 3 -> 3; matrix products, arithmetic and copies ran while one was open for 0% -> 0% of each run, Pallas kernels for 5% -> 6%
where the time goes in v9:
time: 32.8 us; the launch traced here: 32.4 us
  starting transfers between devices  17 us (52%)
  Pallas kernels  6.71 us (20%)
  waiting for transfers between devices  6.42 us (20%)
  local copies, waits for them, and re-layouts  1.59 us (5%)
  between operations  0.7 us (2%)
    ppermute x2, starting transfers between devices, planes(): above = lax.ppermute(down, 'gz', ring('gz', -1))  7.42 us
    all_to_all x1, starting transfers between devices, body(): got = lax.all_to_all(sent, 'xy', 0, 0, tiled=True)  5.34 us
    all_to_all x1, starting transfers between devices, body(): got_force = lax.all_to_all(sent, 'xy', 0, 0, tiled=True)  4.2 us
    ppermute x2, waiting for transfers between devices, planes(): below = lax.ppermute(up, 'gz', ring('gz', 1))  3.48 us
    pallas_call x1, Pallas kernels, body(): call(functools.partial(restrict_kernel, p), [HBM] * 3, [(struct(p.n, p.r1...  2.8 us
    all_to_all x1, waiting for transfers between devices, body(): got_force = lax.all_to_all(sent, 'xy', 0, 0, tiled=True)  1.95 us
    unnamed x6, local copies, waits for them, and re-layouts  1.59 us
    pallas_call x1, Pallas kernels, body(): call(functools.partial(widen_kernel, p), [VMEM] * 3, [(struct(*velocity.s...  1.46 us
  transfers between devices with their start and end apart: 6, of which 3 were waited for; matrix products, arithmetic and copies ran while one was open for 0% of the time, Pallas kernels for 6%

profile of v9, /device:TPU:0, one launch (start us, length us, event | category | flops | bytes accessed | tf_op | source)
XLA Modules:
  0.0 32.4 jit_solution(9532155552915917534)
XLA Ops:
  0.6 2.8 %shard_map.50 = (f32[8,40,256]{2,1,0:T(8,128)}, f32[2,16,512]{2,1,0:T(8,128)}, f32[2,16,512]{2,1,0:T(8,128)}) custom-call(f32[3,4,32,1024]{3,2,1,0:T(8,128)} %v_ref.1, s32[1,32]{1,0:T(1,128)} %bitcast.1, f32[3,2,16,512]{3,2,1,0:T(8,128)} %b_ref), custom_call_target="tpu_custom_call" | custom-call | flops 16777216 | bytes 1048576 | tf_op jit(solution)/shard_map/pallas_call | solution.py:477
  3.4 0.0 copy-start
  3.4 5.3 %all-to-all-start = ((f32[8,40,256]{2,1,0:T(8,128)}), f32[8,40,256]{2,1,0:T(8,128)S(1)}, u32[]{:S(2)}, u32[]{:S(2)}) async-start(f32[8,40,256]{2,1,0:T(8,128)} %get-tuple-element.16), calls=%async_computation | async-start | bytes 655360 | tf_op jit(solution)/shard_map/all_to_all | solution.py:492
  8.8 3.6 %collective-permute-start.1 = (f32[2,16,512]{2,1,0:T(8,128)}, f32[2,16,512]{2,1,0:T(8,128)S(1)}, u32[]{:S(2)}, u32[]{:S(2)}) collective-permute-start(f32[2,16,512]{2,1,0:T(8,128)} %get-tuple-element.22), channel_id=1, source_target_pairs={{0,3},{1,0},{2,1},{3,2},{4,7},{5,4},{6,5},{7,6},{8,11},{9,8},{10,9... | collective-permute-start | bytes 196616 | tf_op jit(solution)/shard_map/ppermute | solution.py:468
  12.4 0.0 collective-permute-start
  12.4 0.0 copy-start.1
  12.4 0.9 %copy-done.1 = f32[3,2,16,512]{3,2,1,0:T(8,128)S(1)} copy-done((f32[3,2,16,512]{3,2,1,0:T(8,128)S(1)}, f32[3,2,16,512]{3,2,1,0:T(8,128)}, u32[]{:S(2)}) %copy-start.1) | copy-done | bytes 196632
  13.3 0.0 copy-start.2
  13.3 0.7 %copy-done.2 = s32[32]{0:T(128)S(1)} copy-done((s32[32]{0:T(128)S(1)}, s32[32]{0:T(128)}, u32[]{:S(2)}) %copy-start.2) | copy-done | bytes 152
  14.0 0.2 shard_map.51
  14.2 1.0 %collective-permute-done.1.hi_ref = f32[2,16,512]{2,1,0:T(8,128)S(1)} collective-permute-done((f32[2,16,512]{2,1,0:T(8,128)}, f32[2,16,512]{2,1,0:T(8,128)S(1)}, u32[]{:S(2)}, u32[]{:S(2)}) %collective-permute-start.1) | collective-permute-done | bytes 65568 | tf_op jit(solution)/shard_map/ppermute | solution.py:468
  15.2 3.5 %collective-permute-done.lo_ref = f32[2,16,512]{2,1,0:T(8,128)S(1)} collective-permute-done((f32[2,16,512]{2,1,0:T(8,128)}, f32[2,16,512]{2,1,0:T(8,128)S(1)}, u32[]{:S(2)}, u32[]{:S(2)}) %collective-permute-start) | collective-permute-done | bytes 65568 | tf_op jit(solution)/shard_map/ppermute | solution.py:467
  18.7 0.0 all-to-all-done.r_ref
  18.7 1.1 %shard_map.52 = (f32[8,24,256]{2,1,0:T(8,128)}, f32[3,2,16,512]{3,2,1,0:T(8,128)S(1)}, f32[3,16,512]{2,1,0:T(8,128)S(1)}, f32[3,16,512]{2,1,0:T(8,128)S(1)}) custom-call(f32[8,40,256]{2,1,0:T(8,128)S(1)} %all-to-all-done.r_ref, f32[3,2,16,512]{3,2,1,0:T(8,128)S(1)} %get-tuple-element.20.b_ref, f32[3,2,16,512]{3,2,1,0:T(8,128)S(1)} %get-tuple-element.21.j_ref, ...), custom_call_target="tpu_custom_call" | custom-call | flops 16777216 | bytes 1048576 | tf_op jit(solution)/shard_map/pallas_call | solution.py:500
  19.8 4.2 %all-to-all-start.1 = ((f32[8,24,256]{2,1,0:T(8,128)}), f32[8,24,256]{2,1,0:T(8,128)S(1)}, u32[]{:S(2)}, u32[]{:S(2)}) async-start(f32[8,24,256]{2,1,0:T(8,128)} %get-tuple-element.23), calls=%async_computation.1 | async-start | bytes 393216 | tf_op jit(solution)/shard_map/all_to_all | solution.py:510
  24.0 0.0 collective-permute-start.2
  24.0 3.8 %collective-permute-start.3 = (f32[3,16,512]{2,1,0:T(8,128)S(1)}, f32[3,16,512]{2,1,0:T(8,128)S(1)}, u32[]{:S(2)}, u32[]{:S(2)}) collective-permute-start(f32[3,16,512]{2,1,0:T(8,128)S(1)} %get-tuple-element.29), channel_id=1, source_target_pairs={{0,3},{1,0},{2,1},{3,2},{4,7},{5,4},{6,5},{7,6},{8,11},{9,8},{10,9... | collective-permute-start | bytes 294920 | tf_op jit(solution)/shard_map/ppermute | solution.py:468
  27.8 0.4 %shard_map.54.n_ref = f32[3,2,16,512]{3,2,1,0:T(8,128)S(1)} custom-call(f32[8,40,256]{2,1,0:T(8,128)S(1)} %all-to-all-done.r_ref, f32[3,2,16,512]{3,2,1,0:T(8,128)S(1)} %get-tuple-element.25.b_ref, f32[2,16,512]{2,1,0:T(8,128)S(1)} %collective-permute-done.lo_ref, f32[2,16,512]{2,1,0:T(8,128)S(1)} %collective-permute-done.1.hi_ref, ...), custom_call_target="tpu_custom_call" | custom-call | flops 16777216 | bytes 1048576 | tf_op jit(solution)/shard_map/pallas_call | solution.py:512
  28.2 2.0 %all-to-all-done.1.r_ref = f32[8,24,256]{2,1,0:T(8,128)S(1)} async-done(((f32[8,24,256]{2,1,0:T(8,128)}), f32[8,24,256]{2,1,0:T(8,128)S(1)}, u32[]{:S(2)}, u32[]{:S(2)}) %all-to-all-start.1) | async-done | bytes 196640 | tf_op jit(solution)/shard_map/all_to_all | solution.py:510
  30.2 0.0 copy-done
  30.2 1.5 %shard_map.53 = f32[3,4,32,1024]{3,2,1,0:T(8,128)} custom-call(f32[8,24,256]{2,1,0:T(8,128)S(1)} %all-to-all-done.1.r_ref, bf16[64,64]{1,0:T(8,128)(2,1)S(1)} %get-tuple-element.24.g_ref, f32[3,4,32,1024]{3,2,1,0:T(8,128)S(1)} %copy-done), custom_call_target="tpu_custom_call" | custom-call | flops 16777216 | bytes 1048576 | tf_op jit(solution)/shard_map/pallas_call | solution.py:515
  31.6 0.0 collective-permute-done.2.lo_ref
  31.7 0.0 collective-permute-done.3.hi_ref
  31.7 0.7 %shard_map.55 = f32[3,2,16,512]{3,2,1,0:T(8,128)} custom-call(f32[3,2,16,512]{3,2,1,0:T(8,128)S(1)} %shard_map.54.n_ref, f32[3,16,512]{2,1,0:T(8,128)S(1)} %collective-permute-done.2.lo_ref, f32[3,16,512]{2,1,0:T(8,128)S(1)} %collective-permute-done.3.hi_ref), custom_call_target="tpu_custom_call" | custom-call | flops 16777216 | bytes 1048576 | tf_op jit(solution)/shard_map/pallas_call | solution.py:522
Async XLA Ops:
  3.4 26.7 %copy-start = (f32[3,4,32,1024]{3,2,1,0:T(8,128)S(1)}, f32[3,4,32,1024]{3,2,1,0:T(8,128)}, u32[]{:S(2)}) copy-start(f32[3,4,32,1024]{3,2,1,0:T(8,128)} %v_ref.1) | copy-start | bytes 4718596
  3.4 15.2 %all-to-all-start = ((f32[8,40,256]{2,1,0:T(8,128)}), f32[8,40,256]{2,1,0:T(8,128)S(1)}, u32[]{:S(2)}, u32[]{:S(2)}) async-start(f32[8,40,256]{2,1,0:T(8,128)} %get-tuple-element.16), calls=%async_computation | async-start | bytes 655360 | tf_op jit(solution)/shard_map/all_to_all | solution.py:492
  8.8 6.4 %collective-permute-start.1 = (f32[2,16,512]{2,1,0:T(8,128)}, f32[2,16,512]{2,1,0:T(8,128)S(1)}, u32[]{:S(2)}, u32[]{:S(2)}) collective-permute-start(f32[2,16,512]{2,1,0:T(8,128)} %get-tuple-element.22), channel_id=1, source_target_pairs={{0,3},{1,0},{2,1},{3,2},{4,7},{5,4},{6,5},{7,6},{8,11},{9,8},{10,9... | collective-permute-start | bytes 196616 | tf_op jit(solution)/shard_map/ppermute | solution.py:468
  12.4 6.3 %collective-permute-start = (f32[2,16,512]{2,1,0:T(8,128)}, f32[2,16,512]{2,1,0:T(8,128)S(1)}, u32[]{:S(2)}, u32[]{:S(2)}) collective-permute-start(f32[2,16,512]{2,1,0:T(8,128)} %get-tuple-element.17), channel_id=1, source_target_pairs={{0,1},{1,2},{2,3},{3,0},{4,5},{5,6},{6,7},{7,4},{8,9},{9,10},{10,1... | collective-permute-start | bytes 196616 | tf_op jit(solution)/shard_map/ppermute | solution.py:467
  12.4 0.9 %copy-start.1 = (f32[3,2,16,512]{3,2,1,0:T(8,128)S(1)}, f32[3,2,16,512]{3,2,1,0:T(8,128)}, u32[]{:S(2)}) copy-start(f32[3,2,16,512]{3,2,1,0:T(8,128)} %b_ref) | copy-start | bytes 589828
  13.3 0.7 %copy-start.2 = (s32[32]{0:T(128)S(1)}, s32[32]{0:T(128)}, u32[]{:S(2)}) copy-start(s32[32]{0:T(128)} %param.5) | copy-start | bytes 388
  19.8 10.4 %all-to-all-start.1 = ((f32[8,24,256]{2,1,0:T(8,128)}), f32[8,24,256]{2,1,0:T(8,128)S(1)}, u32[]{:S(2)}, u32[]{:S(2)}) async-start(f32[8,24,256]{2,1,0:T(8,128)} %get-tuple-element.23), calls=%async_computation.1 | async-start | bytes 393216 | tf_op jit(solution)/shard_map/all_to_all | solution.py:510
  24.0 7.7 %collective-permute-start.2 = (f32[3,16,512]{2,1,0:T(8,128)S(1)}, f32[3,16,512]{2,1,0:T(8,128)S(1)}, u32[]{:S(2)}, u32[]{:S(2)}) collective-permute-start(f32[3,16,512]{2,1,0:T(8,128)S(1)} %get-tuple-element.28), channel_id=1, source_target_pairs={{0,1},{1,2},{2,3},{3,0},{4,5},{5,6},{6,7},{7,4},{8,9},{9,10},{10,1... | collective-permute-start | bytes 294920 | tf_op jit(solution)/shard_map/ppermute | solution.py:467
  24.0 7.7 %collective-permute-start.3 = (f32[3,16,512]{2,1,0:T(8,128)S(1)}, f32[3,16,512]{2,1,0:T(8,128)S(1)}, u32[]{:S(2)}, u32[]{:S(2)}) collective-permute-start(f32[3,16,512]{2,1,0:T(8,128)S(1)} %get-tuple-element.29), channel_id=1, source_target_pairs={{0,3},{1,0},{2,1},{3,2},{4,7},{5,4},{6,5},{7,6},{8,11},{9,8},{10,9... | collective-permute-start | bytes 294920 | tf_op jit(solution)/shard_map/ppermute | solution.py:468

commit v10 on v9

--- a/solution.py
+++ b/solution.py
@@ -394,7 +394,7 @@
             next_ref[c, z] = b_ref[c, z] + 0.05 * total
 
 
-def widen_kernel(p, r_ref, g_ref, v_ref, vel_hbm, vel, sems):
+def finish_kernel(p, r_ref, g_ref, v_ref, n_ref, lo_ref, hi_ref, vel_hbm, mag_hbm, vel, mag, sems):
     zc = p.zc
     half_fine = p.edge * p.edge // 2
     half_area = p.area // 2
@@ -422,12 +422,6 @@
                     vel[c, 2 * z + d, :, fw] = v_ref[c, 2 * z + d, :, fw] + part
         copies.append(pltpu.make_async_copy(vel.at[c], vel_hbm.at[c], sems.at[c]))
         copies[-1].start()
-    for copy in copies:
-        copy.wait()
-
-
-def finish_kernel(p, n_ref, lo_ref, hi_ref, mag):
-    zc = p.zc
     for z in range(zc):
         dz = [jnp.zeros((p.ny, p.nx), F32)] * 2
         outer = dz[0]
@@ -440,6 +434,10 @@
         mag[0, z] = n_ref[0, z] + 0.05 * -dz[1]
         mag[1, z] = n_ref[1, z] + 0.05 * dz[0]
         mag[2, z] = n_ref[2, z] + 0.05 * outer
+    copies.append(pltpu.make_async_copy(mag, mag_hbm, sems.at[3]))
+    copies[-1].start()
+    for copy in copies:
+        copy.wait()
 
 
 def struct(*shape, dtype=F32):
@@ -512,17 +510,14 @@
     (partial,) = call(
         functools.partial(local_kernel, p), [VMEM] * 5, [(struct(*magnetic.shape), VMEM)]
     )(got, diffused, below, above, emf)
-    (updated,) = call(
-        functools.partial(widen_kernel, p),
-        [VMEM] * 3,
-        [(struct(*velocity.shape), HBM)],
-        [pltpu.VMEM(velocity.shape, F32), dma((3,))],
-    )(got_force, g3, velocity)
-    partial, _ = lax.optimization_barrier((partial, updated))
-    (finished,) = call(
-        functools.partial(finish_kernel, p), [VMEM] * 3, [(struct(*magnetic.shape), VMEM)]
-    )(partial, emf_below, emf_above)
-    return updated, finished
+    return tuple(
+        call(
+            functools.partial(finish_kernel, p),
+            [VMEM] * 6,
+            [(struct(*velocity.shape), HBM), (struct(*magnetic.shape), HBM)],
+            [pltpu.VMEM(velocity.shape, F32), pltpu.VMEM(magnetic.shape, F32), dma((4,))],
+        )(got_force, g3, velocity, partial, emf_below, emf_above)
+    )
 
 
 def solution(mesh):

time: 32.8 us -> 33.4 us (1.018)
  waiting for transfers between devices: 6.42 us -> 7.68 us
  Pallas kernels: 6.71 us -> 6.07 us
    ppermute x2, waiting for transfers between devices: 3.48 us -> 6.69 us  [planes(): below = lax.ppermute(up, 'gz', ring('gz', 1))]
    all_to_all x1, waiting for transfers between devices: 1.95 us -> 0.01 us  [body(): got_force = lax.all_to_all(sent, 'xy', 0, 0, tiled=True)]
    pallas_call x2 -> x1, Pallas kernels: 2.17 us -> 1.53 us  [body(): call(functools.partial(finish_kernel, p), [VMEM] * 6, [(struct(*velocity....]
  transfers between devices with their start and end apart: 6 -> 6, of which waited for: 3 -> 3; matrix products, arithmetic and copies ran while one was open for 0% -> 0% of each run, Pallas kernels for 6% -> 2%
where the time goes in v10:
time: 33.4 us; the launch traced here: 33 us
  starting transfers between devices  17 us (51%)
  waiting for transfers between devices  7.68 us (23%)
  Pallas kernels  6.07 us (18%)
  local copies, waits for them, and re-layouts  1.59 us (5%)
  between operations  0.68 us (2%)
    ppermute x2, starting transfers between devices, planes(): above = lax.ppermute(down, 'gz', ring('gz', -1))  7.42 us
    ppermute x2, waiting for transfers between devices, planes(): below = lax.ppermute(up, 'gz', ring('gz', 1))  6.69 us
    all_to_all x1, starting transfers between devices, body(): got = lax.all_to_all(sent, 'xy', 0, 0, tiled=True)  5.34 us
    all_to_all x1, starting transfers between devices, body(): got_force = lax.all_to_all(sent, 'xy', 0, 0, tiled=True)  4.2 us
    pallas_call x1, Pallas kernels, body(): call(functools.partial(restrict_kernel, p), [HBM] * 3, [(struct(p.n, p.r1...  2.8 us
    unnamed x6, local copies, waits for them, and re-layouts  1.59 us
    pallas_call x1, Pallas kernels, body(): call(functools.partial(finish_kernel, p), [VMEM] * 6, [(struct(*velocity....  1.53 us
    pallas_call x1, Pallas kernels, body(): call(functools.partial(field_kernel, p), [VMEM] * 5, [(struct(p.n, p.ru,...  1.1 us
  transfers between devices with their start and end apart: 6, of which 3 were waited for; matrix products, arithmetic and copies ran while one was open for 0% of the time, Pallas kernels for 2%

profile of v10, /device:TPU:0, one launch (start us, length us, event | category | flops | bytes accessed | tf_op | source)
XLA Modules:
  0.0 33.0 jit_solution(13633900024954969041)
XLA Ops:
  0.6 2.8 %shard_map.50 = (f32[8,40,256]{2,1,0:T(8,128)}, f32[2,16,512]{2,1,0:T(8,128)}, f32[2,16,512]{2,1,0:T(8,128)}) custom-call(f32[3,4,32,1024]{3,2,1,0:T(8,128)} %v_ref.1, s32[1,32]{1,0:T(1,128)} %bitcast.1, f32[3,2,16,512]{3,2,1,0:T(8,128)} %b_ref), custom_call_target="tpu_custom_call" | custom-call | flops 16777216 | bytes 1048576 | tf_op jit(solution)/shard_map/pallas_call | solution.py:475
  3.4 0.0 copy-start
  3.4 5.3 %all-to-all-start = ((f32[8,40,256]{2,1,0:T(8,128)}), f32[8,40,256]{2,1,0:T(8,128)S(1)}, u32[]{:S(2)}, u32[]{:S(2)}) async-start(f32[8,40,256]{2,1,0:T(8,128)} %get-tuple-element.15), calls=%async_computation | async-start | bytes 655360 | tf_op jit(solution)/shard_map/all_to_all | solution.py:490
  8.8 3.6 %collective-permute-start.1 = (f32[2,16,512]{2,1,0:T(8,128)}, f32[2,16,512]{2,1,0:T(8,128)S(1)}, u32[]{:S(2)}, u32[]{:S(2)}) collective-permute-start(f32[2,16,512]{2,1,0:T(8,128)} %get-tuple-element.21), channel_id=1, source_target_pairs={{0,3},{1,0},{2,1},{3,2},{4,7},{5,4},{6,5},{7,6},{8,11},{9,8},{10,9... | collective-permute-start | bytes 196616 | tf_op jit(solution)/shard_map/ppermute | solution.py:466
  12.4 0.0 collective-permute-start
  12.4 0.0 copy-start.1
  12.4 0.9 %copy-done.1 = f32[3,2,16,512]{3,2,1,0:T(8,128)S(1)} copy-done((f32[3,2,16,512]{3,2,1,0:T(8,128)S(1)}, f32[3,2,16,512]{3,2,1,0:T(8,128)}, u32[]{:S(2)}) %copy-start.1) | copy-done | bytes 196632
  13.3 0.0 copy-start.2
  13.3 0.7 %copy-done.2 = s32[32]{0:T(128)S(1)} copy-done((s32[32]{0:T(128)S(1)}, s32[32]{0:T(128)}, u32[]{:S(2)}) %copy-start.2) | copy-done | bytes 152
  14.0 0.2 shard_map.51
  14.2 1.0 %collective-permute-done.1.hi_ref = f32[2,16,512]{2,1,0:T(8,128)S(1)} collective-permute-done((f32[2,16,512]{2,1,0:T(8,128)}, f32[2,16,512]{2,1,0:T(8,128)S(1)}, u32[]{:S(2)}, u32[]{:S(2)}) %collective-permute-start.1) | collective-permute-done | bytes 65568 | tf_op jit(solution)/shard_map/ppermute | solution.py:466
  15.2 3.5 %collective-permute-done.lo_ref = f32[2,16,512]{2,1,0:T(8,128)S(1)} collective-permute-done((f32[2,16,512]{2,1,0:T(8,128)}, f32[2,16,512]{2,1,0:T(8,128)S(1)}, u32[]{:S(2)}, u32[]{:S(2)}) %collective-permute-start) | collective-permute-done | bytes 65568 | tf_op jit(solution)/shard_map/ppermute | solution.py:465
  18.7 0.0 all-to-all-done.r_ref
  18.7 1.1 %shard_map.52 = (f32[8,24,256]{2,1,0:T(8,128)}, f32[3,2,16,512]{3,2,1,0:T(8,128)S(1)}, f32[3,16,512]{2,1,0:T(8,128)S(1)}, f32[3,16,512]{2,1,0:T(8,128)S(1)}) custom-call(f32[8,40,256]{2,1,0:T(8,128)S(1)} %all-to-all-done.r_ref, f32[3,2,16,512]{3,2,1,0:T(8,128)S(1)} %get-tuple-element.19.b_ref, f32[3,2,16,512]{3,2,1,0:T(8,128)S(1)} %get-tuple-element.20.j_ref, ...), custom_call_target="tpu_custom_call" | custom-call | flops 16777216 | bytes 1048576 | tf_op jit(solution)/shard_map/pallas_call | solution.py:498
  19.8 4.2 %all-to-all-start.1 = ((f32[8,24,256]{2,1,0:T(8,128)}), f32[8,24,256]{2,1,0:T(8,128)S(1)}, u32[]{:S(2)}, u32[]{:S(2)}) async-start(f32[8,24,256]{2,1,0:T(8,128)} %get-tuple-element.22), calls=%async_computation.1 | async-start | bytes 393216 | tf_op jit(solution)/shard_map/all_to_all | solution.py:508
  24.0 0.0 collective-permute-start.2
  24.0 3.8 %collective-permute-start.3 = (f32[3,16,512]{2,1,0:T(8,128)S(1)}, f32[3,16,512]{2,1,0:T(8,128)S(1)}, u32[]{:S(2)}, u32[]{:S(2)}) collective-permute-start(f32[3,16,512]{2,1,0:T(8,128)S(1)} %get-tuple-element.27), channel_id=1, source_target_pairs={{0,3},{1,0},{2,1},{3,2},{4,7},{5,4},{6,5},{7,6},{8,11},{9,8},{10,9... | collective-permute-start | bytes 294920 | tf_op jit(solution)/shard_map/ppermute | solution.py:466
  27.8 0.4 %shard_map.53.n_ref = f32[3,2,16,512]{3,2,1,0:T(8,128)S(1)} custom-call(f32[8,40,256]{2,1,0:T(8,128)S(1)} %all-to-all-done.r_ref, f32[3,2,16,512]{3,2,1,0:T(8,128)S(1)} %get-tuple-element.24.b_ref, f32[2,16,512]{2,1,0:T(8,128)S(1)} %collective-permute-done.lo_ref, f32[2,16,512]{2,1,0:T(8,128)S(1)} %collective-permute-done.1.hi_ref, ...), custom_call_target="tpu_custom_call" | custom-call | flops 16777216 | bytes 1048576 | tf_op jit(solution)/shard_map/pallas_call | solution.py:510
  28.2 3.2 %collective-permute-done.2.lo_ref = f32[3,16,512]{2,1,0:T(8,128)S(1)} collective-permute-done((f32[3,16,512]{2,1,0:T(8,128)S(1)}, f32[3,16,512]{2,1,0:T(8,128)S(1)}, u32[]{:S(2)}, u32[]{:S(2)}) %collective-permute-start.2) | collective-permute-done | bytes 98336 | tf_op jit(solution)/shard_map/ppermute | solution.py:465
  31.4 0.0 collective-permute-done.3.hi_ref
  31.4 0.0 all-to-all-done.1.r_ref
  31.4 0.0 copy-done
  31.5 1.5 %shard_map.54 = (f32[3,4,32,1024]{3,2,1,0:T(8,128)}, f32[3,2,16,512]{3,2,1,0:T(8,128)}) custom-call(f32[8,24,256]{2,1,0:T(8,128)S(1)} %all-to-all-done.1.r_ref, bf16[64,64]{1,0:T(8,128)(2,1)S(1)} %get-tuple-element.23.g_ref, f32[3,4,32,1024]{3,2,1,0:T(8,128)S(1)} %copy-done, f32[3,2,16,512]{3,2,1,0:T(8,128)S(1)} %shard_map.53.n_ref, ...), custom_call_target="tpu_custom_call" | custom-call | flops 16777216 | bytes 1048576 | tf_op jit(solution)/shard_map/pallas_call | solution.py:514
Async XLA Ops:
  3.4 28.0 %copy-start = (f32[3,4,32,1024]{3,2,1,0:T(8,128)S(1)}, f32[3,4,32,1024]{3,2,1,0:T(8,128)}, u32[]{:S(2)}) copy-start(f32[3,4,32,1024]{3,2,1,0:T(8,128)} %v_ref.1) | copy-start | bytes 4718596
  3.4 15.2 %all-to-all-start = ((f32[8,40,256]{2,1,0:T(8,128)}), f32[8,40,256]{2,1,0:T(8,128)S(1)}, u32[]{:S(2)}, u32[]{:S(2)}) async-start(f32[8,40,256]{2,1,0:T(8,128)} %get-tuple-element.15), calls=%async_computation | async-start | bytes 655360 | tf_op jit(solution)/shard_map/all_to_all | solution.py:490
  8.8 6.4 %collective-permute-start.1 = (f32[2,16,512]{2,1,0:T(8,128)}, f32[2,16,512]{2,1,0:T(8,128)S(1)}, u32[]{:S(2)}, u32[]{:S(2)}) collective-permute-start(f32[2,16,512]{2,1,0:T(8,128)} %get-tuple-element.21), channel_id=1, source_target_pairs={{0,3},{1,0},{2,1},{3,2},{4,7},{5,4},{6,5},{7,6},{8,11},{9,8},{10,9... | collective-permute-start | bytes 196616 | tf_op jit(solution)/shard_map/ppermute | solution.py:466
  12.4 6.3 %collective-permute-start = (f32[2,16,512]{2,1,0:T(8,128)}, f32[2,16,512]{2,1,0:T(8,128)S(1)}, u32[]{:S(2)}, u32[]{:S(2)}) collective-permute-start(f32[2,16,512]{2,1,0:T(8,128)} %get-tuple-element.16), channel_id=1, source_target_pairs={{0,1},{1,2},{2,3},{3,0},{4,5},{5,6},{6,7},{7,4},{8,9},{9,10},{10,1... | collective-permute-start | bytes 196616 | tf_op jit(solution)/shard_map/ppermute | solution.py:465
  12.4 0.9 %copy-start.1 = (f32[3,2,16,512]{3,2,1,0:T(8,128)S(1)}, f32[3,2,16,512]{3,2,1,0:T(8,128)}, u32[]{:S(2)}) copy-start(f32[3,2,16,512]{3,2,1,0:T(8,128)} %b_ref) | copy-start | bytes 589828
  13.3 0.7 %copy-start.2 = (s32[32]{0:T(128)S(1)}, s32[32]{0:T(128)}, u32[]{:S(2)}) copy-start(s32[32]{0:T(128)} %param.5) | copy-start | bytes 388
  19.8 11.7 %all-to-all-start.1 = ((f32[8,24,256]{2,1,0:T(8,128)}), f32[8,24,256]{2,1,0:T(8,128)S(1)}, u32[]{:S(2)}, u32[]{:S(2)}) async-start(f32[8,24,256]{2,1,0:T(8,128)} %get-tuple-element.22), calls=%async_computation.1 | async-start | bytes 393216 | tf_op jit(solution)/shard_map/all_to_all | solution.py:508
  24.0 7.5 %collective-permute-start.2 = (f32[3,16,512]{2,1,0:T(8,128)S(1)}, f32[3,16,512]{2,1,0:T(8,128)S(1)}, u32[]{:S(2)}, u32[]{:S(2)}) collective-permute-start(f32[3,16,512]{2,1,0:T(8,128)S(1)} %get-tuple-element.26), channel_id=1, source_target_pairs={{0,1},{1,2},{2,3},{3,0},{4,5},{5,6},{6,7},{7,4},{8,9},{9,10},{10,1... | collective-permute-start | bytes 294920 | tf_op jit(solution)/shard_map/ppermute | solution.py:465
  24.0 7.5 %collective-permute-start.3 = (f32[3,16,512]{2,1,0:T(8,128)S(1)}, f32[3,16,512]{2,1,0:T(8,128)S(1)}, u32[]{:S(2)}, u32[]{:S(2)}) collective-permute-start(f32[3,16,512]{2,1,0:T(8,128)S(1)} %get-tuple-element.27), channel_id=1, source_target_pairs={{0,3},{1,0},{2,1},{3,2},{4,7},{5,4},{6,5},{7,6},{8,11},{9,8},{10,9... | collective-permute-start | bytes 294920 | tf_op jit(solution)/shard_map/ppermute | solution.py:466

commit v11 on v10

--- a/solution.py
+++ b/solution.py
@@ -272,7 +272,7 @@
     return north, jnp.where(y == 0, row_of(p, ref, prv, at), 0.0)
 
 
-def field_kernel(p, r_ref, b_ref, j_ref, lo_ref, hi_ref, out, e_ref, up_ref, down_ref):
+def field_kernel(p, r_ref, b_ref, j_ref, lo_ref, hi_ref, out_hbm, e_ref, up_ref, down_ref, out, sems):
     n, k, zc = p.n, p.k, p.zc
     me = lax.axis_index("xy")
     nxt, prv = lax.rem(me + 1, n), lax.rem(me + n - 1, n)
@@ -306,9 +306,12 @@
         j1 = j_ref[1, z] + dz[0] * 0.5
         j2 = j_ref[2, z] - dy[0] * 0.5
         force.append([j1 * bz[2] - j2 * bz[1], j2 * bz[0] - j0 * bz[2], j0 * bz[1] - j1 * bz[0]])
+    sends = []
     for c in range(3):
         f_blk = jnp.concatenate([grid_to_blocks(p, force[z][c]) for z in range(zc)], axis=0)
         out[:, c * p.rc : (c + 1) * p.rc, :] = select(g, f_blk).reshape(n, p.rc, p.area)
+    sends.append(pltpu.make_async_copy(out, out_hbm, sems.at[0]))
+    sends[-1].start()
     p_l, z_l, _ = lane_route(p)
     shape = (n, p.rows)
     col_l = jnp.sum(
@@ -331,6 +334,8 @@
             up_ref[0], up_ref[1], up_ref[2] = ez[0], ez[1], bz[2]
         if z == 0:
             down_ref[0], down_ref[1], down_ref[2] = ez[0], ez[1], bz[2]
+    for send in sends:
+        send.wait()
 
 
 def outer_velocity(p, r_ref):
@@ -499,11 +504,12 @@
         functools.partial(field_kernel, p),
         [VMEM] * 5,
         [
-            (struct(p.n, p.ru, p.area), VMEM),
+            (struct(p.n, p.ru, p.area), HBM),
             (struct(*magnetic.shape), VMEM),
             (struct(3, *plane), VMEM),
             (struct(3, *plane), VMEM),
         ],
+        [pltpu.VMEM((p.n, p.ru, p.area), F32), dma((1,))],
     )(got, field, current, below, above)
     got_force = lax.all_to_all(sent, "xy", 0, 0, tiled=True)
     emf_below, emf_above = planes(up, down)

time: 33.4 us -> 33.4 us (level)
  no operation moved by 1% of the time
where the time goes in v11:
time: 33.4 us; the launch traced here: 33 us
  starting transfers between devices  17 us (51%)
  waiting for transfers between devices  7.68 us (23%)
  Pallas kernels  6.08 us (18%)
  local copies, waits for them, and re-layouts  1.59 us (5%)
  between operations  0.69 us (2%)
    ppermute x2, starting transfers between devices, planes(): above = lax.ppermute(down, 'gz', ring('gz', -1))  7.42 us
    ppermute x2, waiting for transfers between devices, planes(): below = lax.ppermute(up, 'gz', ring('gz', 1))  6.69 us
    all_to_all x1, starting transfers between devices, body(): got = lax.all_to_all(sent, 'xy', 0, 0, tiled=True)  5.34 us
    all_to_all x1, starting transfers between devices, body(): got_force = lax.all_to_all(sent, 'xy', 0, 0, tiled=True)  4.21 us
    pallas_call x1, Pallas kernels, body(): call(functools.partial(restrict_kernel, p), [HBM] * 3, [(struct(p.n, p.r1...  2.8 us
    unnamed x6, local copies, waits for them, and re-layouts  1.59 us
    pallas_call x1, Pallas kernels, body(): call(functools.partial(finish_kernel, p), [VMEM] * 6, [(struct(*velocity....  1.53 us
    pallas_call x1, Pallas kernels, body(): call(functools.partial(field_kernel, p), [VMEM] * 5, [(struct(p.n, p.ru,...  1.11 us
  transfers between devices with their start and end apart: 6, of which 3 were waited for; matrix products, arithmetic and copies ran while one was open for 0% of the time, Pallas kernels for 2%

profile of v11, /device:TPU:0, one launch (start us, length us, event | category | flops | bytes accessed | tf_op | source)
XLA Modules:
  0.0 33.0 jit_solution(10680306751535527900)
XLA Ops:
  0.6 2.8 %shard_map.50 = (f32[8,40,256]{2,1,0:T(8,128)}, f32[2,16,512]{2,1,0:T(8,128)}, f32[2,16,512]{2,1,0:T(8,128)}) custom-call(f32[3,4,32,1024]{3,2,1,0:T(8,128)} %v_ref.1, s32[1,32]{1,0:T(1,128)} %bitcast.1, f32[3,2,16,512]{3,2,1,0:T(8,128)} %b_ref), custom_call_target="tpu_custom_call" | custom-call | flops 16777216 | bytes 1048576 | tf_op jit(solution)/shard_map/pallas_call | solution.py:480
  3.4 0.0 copy-start
  3.4 5.3 %all-to-all-start = ((f32[8,40,256]{2,1,0:T(8,128)}), f32[8,40,256]{2,1,0:T(8,128)S(1)}, u32[]{:S(2)}, u32[]{:S(2)}) async-start(f32[8,40,256]{2,1,0:T(8,128)} %get-tuple-element.15), calls=%async_computation | async-start | bytes 655360 | tf_op jit(solution)/shard_map/all_to_all | solution.py:495
  8.8 3.6 %collective-permute-start.1 = (f32[2,16,512]{2,1,0:T(8,128)}, f32[2,16,512]{2,1,0:T(8,128)S(1)}, u32[]{:S(2)}, u32[]{:S(2)}) collective-permute-start(f32[2,16,512]{2,1,0:T(8,128)} %get-tuple-element.21), channel_id=1, source_target_pairs={{0,3},{1,0},{2,1},{3,2},{4,7},{5,4},{6,5},{7,6},{8,11},{9,8},{10,9... | collective-permute-start | bytes 196616 | tf_op jit(solution)/shard_map/ppermute | solution.py:471
  12.4 0.0 collective-permute-start
  12.4 0.0 copy-start.1
  12.4 0.9 %copy-done.1 = f32[3,2,16,512]{3,2,1,0:T(8,128)S(1)} copy-done((f32[3,2,16,512]{3,2,1,0:T(8,128)S(1)}, f32[3,2,16,512]{3,2,1,0:T(8,128)}, u32[]{:S(2)}) %copy-start.1) | copy-done | bytes 196632
  13.3 0.0 copy-start.2
  13.3 0.7 %copy-done.2 = s32[32]{0:T(128)S(1)} copy-done((s32[32]{0:T(128)S(1)}, s32[32]{0:T(128)}, u32[]{:S(2)}) %copy-start.2) | copy-done | bytes 152
  14.0 0.2 shard_map.51
  14.2 1.0 %collective-permute-done.1.hi_ref = f32[2,16,512]{2,1,0:T(8,128)S(1)} collective-permute-done((f32[2,16,512]{2,1,0:T(8,128)}, f32[2,16,512]{2,1,0:T(8,128)S(1)}, u32[]{:S(2)}, u32[]{:S(2)}) %collective-permute-start.1) | collective-permute-done | bytes 65568 | tf_op jit(solution)/shard_map/ppermute | solution.py:471
  15.2 3.5 %collective-permute-done.lo_ref = f32[2,16,512]{2,1,0:T(8,128)S(1)} collective-permute-done((f32[2,16,512]{2,1,0:T(8,128)}, f32[2,16,512]{2,1,0:T(8,128)S(1)}, u32[]{:S(2)}, u32[]{:S(2)}) %collective-permute-start) | collective-permute-done | bytes 65568 | tf_op jit(solution)/shard_map/ppermute | solution.py:470
  18.7 0.0 all-to-all-done.r_ref
  18.7 1.1 %shard_map.52 = (f32[8,24,256]{2,1,0:T(8,128)}, f32[3,2,16,512]{3,2,1,0:T(8,128)S(1)}, f32[3,16,512]{2,1,0:T(8,128)S(1)}, f32[3,16,512]{2,1,0:T(8,128)S(1)}) custom-call(f32[8,40,256]{2,1,0:T(8,128)S(1)} %all-to-all-done.r_ref, f32[3,2,16,512]{3,2,1,0:T(8,128)S(1)} %get-tuple-element.19.b_ref, f32[3,2,16,512]{3,2,1,0:T(8,128)S(1)} %get-tuple-element.20.j_ref, ...), custom_call_target="tpu_custom_call" | custom-call | flops 16777216 | bytes 1048576 | tf_op jit(solution)/shard_map/pallas_call | solution.py:503
  19.8 4.2 %all-to-all-start.1 = ((f32[8,24,256]{2,1,0:T(8,128)}), f32[8,24,256]{2,1,0:T(8,128)S(1)}, u32[]{:S(2)}, u32[]{:S(2)}) async-start(f32[8,24,256]{2,1,0:T(8,128)} %get-tuple-element.22), calls=%async_computation.1 | async-start | bytes 393216 | tf_op jit(solution)/shard_map/all_to_all | solution.py:514
  24.0 0.0 collective-permute-start.2
  24.0 3.8 %collective-permute-start.3 = (f32[3,16,512]{2,1,0:T(8,128)S(1)}, f32[3,16,512]{2,1,0:T(8,128)S(1)}, u32[]{:S(2)}, u32[]{:S(2)}) collective-permute-start(f32[3,16,512]{2,1,0:T(8,128)S(1)} %get-tuple-element.27), channel_id=1, source_target_pairs={{0,3},{1,0},{2,1},{3,2},{4,7},{5,4},{6,5},{7,6},{8,11},{9,8},{10,9... | collective-permute-start | bytes 294920 | tf_op jit(solution)/shard_map/ppermute | solution.py:471
  27.8 0.4 %shard_map.53.n_ref = f32[3,2,16,512]{3,2,1,0:T(8,128)S(1)} custom-call(f32[8,40,256]{2,1,0:T(8,128)S(1)} %all-to-all-done.r_ref, f32[3,2,16,512]{3,2,1,0:T(8,128)S(1)} %get-tuple-element.24.b_ref, f32[2,16,512]{2,1,0:T(8,128)S(1)} %collective-permute-done.lo_ref, f32[2,16,512]{2,1,0:T(8,128)S(1)} %collective-permute-done.1.hi_ref, ...), custom_call_target="tpu_custom_call" | custom-call | flops 16777216 | bytes 1048576 | tf_op jit(solution)/shard_map/pallas_call | solution.py:516
  28.3 3.2 %collective-permute-done.2.lo_ref = f32[3,16,512]{2,1,0:T(8,128)S(1)} collective-permute-done((f32[3,16,512]{2,1,0:T(8,128)S(1)}, f32[3,16,512]{2,1,0:T(8,128)S(1)}, u32[]{:S(2)}, u32[]{:S(2)}) %collective-permute-start.2) | collective-permute-done | bytes 98336 | tf_op jit(solution)/shard_map/ppermute | solution.py:470
  31.5 0.0 collective-permute-done.3.hi_ref
  31.5 0.0 all-to-all-done.1.r_ref
  31.5 0.0 copy-done
  31.5 1.5 %shard_map.54 = (f32[3,4,32,1024]{3,2,1,0:T(8,128)}, f32[3,2,16,512]{3,2,1,0:T(8,128)}) custom-call(f32[8,24,256]{2,1,0:T(8,128)S(1)} %all-to-all-done.1.r_ref, bf16[64,64]{1,0:T(8,128)(2,1)S(1)} %get-tuple-element.23.g_ref, f32[3,4,32,1024]{3,2,1,0:T(8,128)S(1)} %copy-done, f32[3,2,16,512]{3,2,1,0:T(8,128)S(1)} %shard_map.53.n_ref, ...), custom_call_target="tpu_custom_call" | custom-call | flops 16777216 | bytes 1048576 | tf_op jit(solution)/shard_map/pallas_call | solution.py:520
Async XLA Ops:
  3.4 28.0 %copy-start = (f32[3,4,32,1024]{3,2,1,0:T(8,128)S(1)}, f32[3,4,32,1024]{3,2,1,0:T(8,128)}, u32[]{:S(2)}) copy-start(f32[3,4,32,1024]{3,2,1,0:T(8,128)} %v_ref.1) | copy-start | bytes 4718596
  3.4 15.2 %all-to-all-start = ((f32[8,40,256]{2,1,0:T(8,128)}), f32[8,40,256]{2,1,0:T(8,128)S(1)}, u32[]{:S(2)}, u32[]{:S(2)}) async-start(f32[8,40,256]{2,1,0:T(8,128)} %get-tuple-element.15), calls=%async_computation | async-start | bytes 655360 | tf_op jit(solution)/shard_map/all_to_all | solution.py:495
  8.8 6.4 %collective-permute-start.1 = (f32[2,16,512]{2,1,0:T(8,128)}, f32[2,16,512]{2,1,0:T(8,128)S(1)}, u32[]{:S(2)}, u32[]{:S(2)}) collective-permute-start(f32[2,16,512]{2,1,0:T(8,128)} %get-tuple-element.21), channel_id=1, source_target_pairs={{0,3},{1,0},{2,1},{3,2},{4,7},{5,4},{6,5},{7,6},{8,11},{9,8},{10,9... | collective-permute-start | bytes 196616 | tf_op jit(solution)/shard_map/ppermute | solution.py:471
  12.4 6.3 %collective-permute-start = (f32[2,16,512]{2,1,0:T(8,128)}, f32[2,16,512]{2,1,0:T(8,128)S(1)}, u32[]{:S(2)}, u32[]{:S(2)}) collective-permute-start(f32[2,16,512]{2,1,0:T(8,128)} %get-tuple-element.16), channel_id=1, source_target_pairs={{0,1},{1,2},{2,3},{3,0},{4,5},{5,6},{6,7},{7,4},{8,9},{9,10},{10,1... | collective-permute-start | bytes 196616 | tf_op jit(solution)/shard_map/ppermute | solution.py:470
  12.4 0.9 %copy-start.1 = (f32[3,2,16,512]{3,2,1,0:T(8,128)S(1)}, f32[3,2,16,512]{3,2,1,0:T(8,128)}, u32[]{:S(2)}) copy-start(f32[3,2,16,512]{3,2,1,0:T(8,128)} %b_ref) | copy-start | bytes 589828
  13.3 0.7 %copy-start.2 = (s32[32]{0:T(128)S(1)}, s32[32]{0:T(128)}, u32[]{:S(2)}) copy-start(s32[32]{0:T(128)} %param.5) | copy-start | bytes 388
  19.8 11.7 %all-to-all-start.1 = ((f32[8,24,256]{2,1,0:T(8,128)}), f32[8,24,256]{2,1,0:T(8,128)S(1)}, u32[]{:S(2)}, u32[]{:S(2)}) async-start(f32[8,24,256]{2,1,0:T(8,128)} %get-tuple-element.22), calls=%async_computation.1 | async-start | bytes 393216 | tf_op jit(solution)/shard_map/all_to_all | solution.py:514
  24.0 7.5 %collective-permute-start.2 = (f32[3,16,512]{2,1,0:T(8,128)S(1)}, f32[3,16,512]{2,1,0:T(8,128)S(1)}, u32[]{:S(2)}, u32[]{:S(2)}) collective-permute-start(f32[3,16,512]{2,1,0:T(8,128)S(1)} %get-tuple-element.26), channel_id=1, source_target_pairs={{0,1},{1,2},{2,3},{3,0},{4,5},{5,6},{6,7},{7,4},{8,9},{9,10},{10,1... | collective-permute-start | bytes 294920 | tf_op jit(solution)/shard_map/ppermute | solution.py:470
  24.0 7.5 %collective-permute-start.3 = (f32[3,16,512]{2,1,0:T(8,128)S(1)}, f32[3,16,512]{2,1,0:T(8,128)S(1)}, u32[]{:S(2)}, u32[]{:S(2)}) collective-permute-start(f32[3,16,512]{2,1,0:T(8,128)S(1)} %get-tuple-element.27), channel_id=1, source_target_pairs={{0,3},{1,0},{2,1},{3,2},{4,7},{5,4},{6,5},{7,6},{8,11},{9,8},{10,9... | collective-permute-start | bytes 294920 | tf_op jit(solution)/shard_map/ppermute | solution.py:471
